TPU v7x, 32 devices: a whole 2x2x4 slice. The times are simulated.
32 devices in a mesh: dp: 4 (over y, core), row: 2 (over x), col: 4 (over z).
Axes of the slice: x: 2, y: 2, z: 4, core: 2. Of those that a mesh axis runs over, the one named last changes fastest.
Arguments:
- tokens: bfloat16 [12288, 768], P(('dp', 'col'), 'row'), may hold values from -6 to 6
- cotangent: bfloat16 [12288, 768], P(('dp', 'col'), 'row'), may hold values from -6 to 6
- timestep: int32 [4], P('dp'), may hold values from 0 to 999
- piece_starts: int32 [4, 4], P('dp'), may hold values from 0 to 2816, as said below
- w_mod: bfloat16 [128, 6, 768], P(None, None, 'row'), may hold values from -0.5 to 0.5
- b_mod: float32 [6, 768], P(None, 'row'), may hold values from -3 to 3
- gain_attn: float32 [768], P('row'), may hold values from 0.5 to 1.5
- w_qkv: bfloat16 [2304, 768], P('col', 'row'), may hold values from -0.21875 to 0.21875
- w_out: bfloat16 [768, 768], P('col', 'row'), may hold values from -0.875 to 0.875
- gain_mlp: float32 [768], P('row'), may hold values from 0.5 to 1.5
- w_up: bfloat16 [768, 3072], P('row', 'col'), may hold values from -0.21875 to 0.21875
- b_up: bfloat16 [3072], P('col'), may hold values from -3 to 3
- w_down: bfloat16 [3072, 768], P('col', 'row'), may hold values from -0.109375 to 0.109375
- b_down: float32 [768], P('row'), may hold values from -3 to 3
Outputs:
- block_out: bfloat16 [12288, 768], P(('dp', 'col'), 'row')
- d_tokens: float32 [12288, 768], P(('dp', 'col'), 'row')
- d_mod_w: float32 [128, 6, 768], P(None, None, 'row')
- d_mod_b: float32 [6, 768], P(None, 'row')
- d_gain_attn: float32 [768], P('row')
- d_qkv: float32 [2304, 768], P('col', 'row')
- d_out_proj: float32 [768, 768], P('col', 'row')
- d_gain_mlp: float32 [768], P('row')
- d_up: float32 [768, 3072], P('row', 'col')
- d_up_bias: float32 [3072], P('col')
- d_down: float32 [3072, 768], P('col', 'row')
- d_down_bias: float32 [768], P('row')
Inputs may be any that keep to these rules, and one draw needn't show every extreme that they name: `piece_starts`: in every sequence the 4 pieces of 256 tokens rise, do not intersect and lie inside the sequence; the first opens the sequence and the last closes it.
All inputs are finite; a program needn't handle non-finite values.
Results may differ from a plain program's by a relative error of at most 0.014.
The roundings to bfloat16 on the way count: a program that leaves them out, or rounds other values in their place, can miss the bound.
Values may be sent and summed in bfloat16 or wider, within the bound.
No kernel may reach another device: no remote copies, remote signals or barrier semaphores. Data moves between devices by JAX's collectives and lax.ppermute only.
A program may use at most 192 MiB of HBM per device.

v0:
```python
import math

import jax
import jax.numpy as jnp
from jax import lax
from jax.sharding import PartitionSpec as P

D = 768
HEAD = 64
COND = 128
PIECE = 256
PIECES = 4


precise = lax.Precision.HIGHEST
epsilon = 1e-05


def embed_time(time_step):
    half_size = COND // 2
    frequency = jnp.exp(-math.log(10000.0) * jnp.arange(half_size, dtype=jnp.float32) / half_size)
    angles = time_step * frequency
    return jax.nn.silu(jnp.concatenate([jnp.cos(angles), jnp.sin(angles)]))


def rotate(vectors, places):
    half_size = HEAD // 2
    frequency = jnp.exp(-math.log(10000.0) * jnp.arange(half_size, dtype=jnp.float32) / half_size)
    angles = places.astype(jnp.float32)[:, None] * frequency[None, :]
    cosine = jnp.cos(angles)[:, None, :]
    sine_part = jnp.sin(angles)[:, None, :]
    first_half = vectors[..., :half_size]
    second_half = vectors[..., half_size:]
    return jnp.concatenate(
        [
            first_half * cosine - second_half * sine_part,
            second_half * cosine + first_half * sine_part,
        ],
        -1,
    )


def piece_ids(places, starts):
    inside = (places[:, None] >= starts[None, :]) & (places[:, None] < starts[None, :] + PIECE)
    labels = jnp.arange(1, PIECES + 1, dtype=jnp.int32)[None, :]
    return jnp.sum(jnp.where(inside, labels, 0), axis=1) - 1


def visible(query_places, seq_len, starts):
    key_places = jnp.arange(seq_len, dtype=jnp.int32)
    query_piece = piece_ids(query_places, starts)
    key_piece = piece_ids(key_places, starts)
    return (key_places[None, :] <= query_places[:, None]) | (
        query_piece[:, None] == key_piece[None, :]
    ) & (query_piece[:, None] >= 0)


def into_heads(activation, weight, contract):
    gathered = lax.all_gather(activation, "col", axis=0, tiled=True)
    share_rows = gathered.shape[0] // lax.axis_size("row")

    def partial_product(start_row, row_count):
        return lax.dot_general(
            gathered, weight, (((1,), (contract,)), ((), ())), preferred_element_type=jnp.float32
        )

    return (
        lax.psum_scatter(
            partial_product(jnp.int32(0), share_rows * lax.axis_size("row")),
            "row",
            scatter_dimension=0,
            tiled=True,
        ),
        gathered,
    )


def into_stream(activation, weight, contract):
    gathered = lax.all_gather(activation, "row", axis=0, tiled=True)
    share_rows = gathered.shape[0] // lax.axis_size("col")

    def partial_product(start_row, row_count):
        return lax.dot_general(
            gathered, weight, (((1,), (contract,)), ((), ())), preferred_element_type=jnp.float32
        )

    return (
        lax.psum_scatter(
            partial_product(jnp.int32(0), share_rows * lax.axis_size("col")),
            "col",
            scatter_dimension=0,
            tiled=True,
        ),
        gathered,
    )


def weight_grad(first_operand, second_operand):
    return lax.dot_general(
        first_operand, second_operand, (((0,), (0,)), ((), ())), preferred_element_type=jnp.float32
    )


def row_totals(first_sum, second_sum):
    return lax.psum((first_sum, second_sum), "row")


def norm_forward(values, gain_vec, shift_vec, scale_vec, totals):
    row_total, row_square = totals(jnp.sum(values, -1), jnp.sum(values * values, -1))
    row_mean = row_total / D
    inv_std = lax.rsqrt(row_square / D - row_mean * row_mean + epsilon)
    normed = (values - row_mean[:, None]) * inv_std[:, None]
    return (
        normed,
        inv_std,
        (normed * gain_vec * (1.0 + scale_vec) + shift_vec).astype(jnp.bfloat16),
    )


def norm_backward(upstream, normed, inv_std, gain_vec, scale_vec, totals):
    d_shift = jnp.sum(upstream, 0)
    d_scale = jnp.sum(upstream * normed * gain_vec, 0)
    d_gain = jnp.sum(upstream * normed * (1.0 + scale_vec), 0)
    d_normed = upstream * gain_vec * (1.0 + scale_vec)
    mean_grad, mean_proj = totals(jnp.sum(d_normed, -1), jnp.sum(d_normed * normed, -1))
    d_values = inv_std[:, None] * (
        d_normed - mean_grad[:, None] / D - normed * mean_proj[:, None] / D
    )
    return (d_values, d_gain, d_shift, d_scale)


def attend(query_head, key_head, value_head, allowed):
    scores = lax.dot_general(
        query_head, key_head, (((1,), (1,)), ((), ())), preferred_element_type=jnp.float32
    ) * HEAD ** (-0.5)
    scores = jnp.where(allowed, scores, -1e30)
    row_max = jnp.max(scores, -1, keepdims=True)
    weights_raw = jnp.exp(scores - row_max)
    row_sum = jnp.sum(weights_raw, -1, keepdims=True)
    probabilities = (weights_raw / row_sum).astype(jnp.bfloat16)
    mixed_head = jnp.dot(probabilities, value_head, preferred_element_type=jnp.float32)
    return (mixed_head, (row_max + jnp.log(row_sum))[:, 0])


def attend_back(query_head, key_head, value_head, d_mixed_head, log_sum, allowed):
    scores = lax.dot_general(
        query_head, key_head, (((1,), (1,)), ((), ())), preferred_element_type=jnp.float32
    ) * HEAD ** (-0.5)
    probabilities = jnp.where(allowed, jnp.exp(scores - log_sum[:, None]), 0.0)
    d_prob = lax.dot_general(
        d_mixed_head, value_head, (((1,), (1,)), ((), ())), preferred_element_type=jnp.float32
    )
    d_scores = (
        probabilities * (d_prob - jnp.sum(probabilities * d_prob, -1, keepdims=True))
    ).astype(jnp.bfloat16)
    d_query = jnp.dot(d_scores, key_head, preferred_element_type=jnp.float32) * HEAD ** (-0.5)
    d_key = weight_grad(d_scores, query_head) * HEAD ** (-0.5)
    d_value = weight_grad(probabilities.astype(jnp.bfloat16), d_mixed_head)
    return (d_query, d_key, d_value)


def rotate_pair(projected, places):
    return jax.vjp(
        lambda first_in, second_in: (rotate(first_in, places), rotate(second_in, places)),
        projected[:, :, 0],
        projected[:, :, 1],
    )


def attention_forward(queries, key_value_all, allowed):
    heads_query = queries.transpose(1, 0, 2)
    heads_key = key_value_all[:, :, 0].transpose(1, 0, 2)
    heads_value = key_value_all[:, :, 1].transpose(1, 0, 2)
    mixed, log_sum = lax.map(
        lambda operands: attend(operands[0], operands[1], operands[2], allowed),
        (heads_query, heads_key, heads_value),
    )
    mixed = (
        mixed.transpose(1, 0, 2)
        .reshape(queries.shape[0], queries.shape[1] * HEAD)
        .astype(jnp.bfloat16)
    )
    return (mixed, log_sum, (heads_query, heads_key, heads_value))


def attention_backward(saved, d_mixed, log_sum, allowed):
    heads_query, heads_key, heads_value = saved
    head_count = heads_query.shape[0]
    query_rows = heads_query.shape[1]
    seq_len = heads_key.shape[1]
    d_mixed_heads = (
        d_mixed.astype(jnp.bfloat16).reshape(query_rows, head_count, HEAD).transpose(1, 0, 2)
    )
    d_query, d_key, d_value = lax.map(
        lambda operands: attend_back(
            operands[0], operands[1], operands[2], operands[3], operands[4], allowed
        ),
        (heads_query, heads_key, heads_value, d_mixed_heads, log_sum),
    )
    d_key_value = jnp.stack([d_key.transpose(1, 0, 2), d_value.transpose(1, 0, 2)], 2).reshape(
        seq_len, head_count * 2 * HEAD
    )
    return (d_query.transpose(1, 0, 2), d_key_value)


def small_stack(
    d_shift_attn,
    d_scale_attn,
    d_gate_attn,
    d_shift_mlp,
    d_scale_mlp,
    d_gate_mlp,
    d_gain_attn,
    d_gain_mlp,
    d_down_bias,
):
    return jnp.stack(
        [
            d_shift_attn,
            d_scale_attn,
            d_gate_attn,
            d_shift_mlp,
            d_scale_mlp,
            d_gate_mlp,
            d_gain_attn,
            d_gain_mlp,
            d_down_bias,
        ],
        0,
    )


def blocked_layer(
    tokens,
    cotangent,
    modulation,
    starts,
    gain_attn,
    w_qkv,
    w_out,
    gain_mlp,
    w_up,
    b_up,
    w_down,
    b_down,
):
    residual = tokens.astype(jnp.float32)
    shift_attn, scale_attn, gate_attn = (modulation[0], modulation[1], modulation[2])
    shift_mlp, scale_mlp, gate_mlp = (modulation[3], modulation[4], modulation[5])
    normed_one, inv_std_one, normed_in = norm_forward(
        residual, gain_attn, shift_attn, scale_attn, row_totals
    )
    projected, normed_in_all = into_heads(normed_in, w_qkv, 1)
    query_rows = projected.shape[0]
    heads_local = projected.shape[1] // (3 * HEAD)
    projected = projected.reshape(query_rows, heads_local, 3, HEAD)
    seq_len = query_rows * lax.axis_size("row")
    query_places = lax.axis_index("row") * query_rows + jnp.arange(query_rows, dtype=jnp.int32)
    rotated, rotate_back = rotate_pair(projected, query_places)
    queries = rotated[0].astype(jnp.bfloat16)
    key_value = jnp.stack(
        [rotated[1].astype(jnp.bfloat16), projected[:, :, 2].astype(jnp.bfloat16)], 2
    ).reshape(query_rows, heads_local * 2 * HEAD)
    key_value_all = lax.all_gather(key_value, "row", axis=0, tiled=True).reshape(
        seq_len, heads_local, 2, HEAD
    )
    allowed = visible(query_places, seq_len, starts)
    mixed, log_sum, saved = attention_forward(queries, key_value_all, allowed)
    attended, mixed_all = into_stream(mixed, w_out, 0)
    middle = residual + gate_attn * attended
    normed_two, inv_std_two, normed_mid = norm_forward(
        middle, gain_mlp, shift_mlp, scale_mlp, row_totals
    )
    hidden, normed_mid_all = into_heads(normed_mid, w_up, 0)
    hidden = hidden + b_up.astype(jnp.float32)
    active_full, gelu_back = jax.vjp(lambda inner: jax.nn.gelu(inner, approximate=True), hidden)
    active = active_full.astype(jnp.bfloat16)
    branch, active_all = into_stream(active, w_down, 0)
    branch = branch + b_down
    block_out = (middle + gate_mlp * branch).astype(jnp.bfloat16)
    upstream = cotangent.astype(jnp.float32)
    d_gate_mlp = jnp.sum(upstream * branch, 0)
    d_branch = (upstream * gate_mlp).astype(jnp.bfloat16)
    d_down_bias = jnp.sum(d_branch.astype(jnp.float32), 0)
    d_active, d_branch_all = into_heads(d_branch, w_down, 1)
    d_down = weight_grad(active_all, d_branch_all)
    d_hidden = gelu_back(d_active)[0].astype(jnp.bfloat16)
    d_up_bias = jnp.sum(d_hidden.astype(jnp.float32), 0)
    d_normed_mid, d_hidden_all = into_stream(d_hidden, w_up, 1)
    d_up = weight_grad(normed_mid_all, d_hidden_all)
    d_middle, d_gain_mlp, d_shift_mlp, d_scale_mlp = norm_backward(
        d_normed_mid, normed_two, inv_std_two, gain_mlp, scale_mlp, row_totals
    )
    d_middle = d_middle + upstream
    d_gate_attn = jnp.sum(d_middle * attended, 0)
    d_attended = (d_middle * gate_attn).astype(jnp.bfloat16)
    d_mixed, d_attended_all = into_heads(d_attended, w_out, 1)
    d_out_proj = weight_grad(mixed_all, d_attended_all)
    d_query, d_key_value = attention_backward(saved, d_mixed, log_sum, allowed)
    d_key_value = (
        lax.psum_scatter(d_key_value.astype(jnp.bfloat16), "row", scatter_dimension=0, tiled=True)
        .astype(jnp.float32)
        .reshape(query_rows, heads_local, 2, HEAD)
    )
    d_query_raw, d_key_raw = rotate_back((d_query, d_key_value[:, :, 0]))
    d_projected = (
        jnp.stack([d_query_raw, d_key_raw, d_key_value[:, :, 1]], 2)
        .reshape(query_rows, heads_local * 3 * HEAD)
        .astype(jnp.bfloat16)
    )
    d_normed_in, d_projected_all = into_stream(d_projected, w_qkv, 0)
    d_qkv = weight_grad(d_projected_all, normed_in_all)
    d_input, d_gain_attn, d_shift_attn, d_scale_attn = norm_backward(
        d_normed_in, normed_one, inv_std_one, gain_attn, scale_attn, row_totals
    )
    d_tokens = d_input + d_middle
    small_rows = small_stack(
        d_shift_attn,
        d_scale_attn,
        d_gate_attn,
        d_shift_mlp,
        d_scale_mlp,
        d_gate_mlp,
        d_gain_attn,
        d_gain_mlp,
        d_down_bias,
    )
    row_here = lax.axis_index("row")
    col_here = lax.axis_index("col")
    row_slots = jnp.where(
        (jnp.arange(lax.axis_size("row"), dtype=jnp.int32) == row_here)[:, None, None],
        small_rows[None],
        0.0,
    )
    col_slots = jnp.where(
        (jnp.arange(lax.axis_size("col"), dtype=jnp.int32) == col_here)[:, None],
        d_up_bias[None],
        0.0,
    )
    row_slots, col_slots = lax.psum((row_slots, col_slots), ("row", "col"))
    small_rows = lax.dynamic_index_in_dim(row_slots, row_here, 0, keepdims=False)
    d_up_bias = lax.dynamic_index_in_dim(col_slots, col_here, 0, keepdims=False)
    return (block_out, d_tokens, d_qkv, d_out_proj, d_up, d_down, small_rows, d_up_bias)


def shards(
    tokens,
    cotangent,
    timestep,
    piece_starts,
    w_mod,
    b_mod,
    gain_attn,
    w_qkv,
    w_out,
    gain_mlp,
    w_up,
    b_up,
    w_down,
    b_down,
):
    condition = embed_time(timestep[0].astype(jnp.float32))
    modulation = (
        jnp.einsum("k,kjd->jd", condition, w_mod.astype(jnp.float32), precision=precise) + b_mod
    )
    starts = piece_starts[0]
    results = blocked_layer(
        tokens,
        cotangent,
        modulation,
        starts,
        gain_attn,
        w_qkv,
        w_out,
        gain_mlp,
        w_up,
        b_up,
        w_down,
        b_down,
    )
    block_out, d_tokens, d_qkv, d_out_proj, d_up, d_down, small_rows, d_up_bias = results
    d_mod_w = condition[:, None, None] * small_rows[:6][None, :, :]
    d_qkv, d_out_proj, d_up, d_down, d_mod_w, small_rows, d_up_bias = lax.psum(
        (d_qkv, d_out_proj, d_up, d_down, d_mod_w, small_rows, d_up_bias), "dp"
    )
    return (
        block_out,
        d_tokens,
        d_mod_w,
        small_rows[:6],
        small_rows[6],
        d_qkv,
        d_out_proj,
        small_rows[7],
        d_up,
        d_up_bias,
        d_down,
        small_rows[8],
    )


def solution(mesh):
    return jax.shard_map(
        shards,
        mesh=mesh,
        in_specs=(
            P(("dp", "col"), "row"),
            P(("dp", "col"), "row"),
            P("dp"),
            P("dp", None),
            P(None, None, "row"),
            P(None, "row"),
            P("row"),
            P("col", "row"),
            P("col", "row"),
            P("row"),
            P("row", "col"),
            P("col"),
            P("col", "row"),
            P("row"),
        ),
        out_specs=(
            P(("dp", "col"), "row"),
            P(("dp", "col"), "row"),
            P(None, None, "row"),
            P(None, "row"),
            P("row"),
            P("col", "row"),
            P("col", "row"),
            P("row"),
            P("row", "col"),
            P("col"),
            P("col", "row"),
            P("row"),
        ),
        check_vma=False,
    )
```

profile of v0, /device:TPU:9, one launch (start us, length us, event | category | flops | bytes accessed | tf_op | source)
XLA Modules:
  0.0 1631.6 jit_solution(5533274232627833205)
XLA Ops:
  11.6 3.8 all-reduce.10
  17.3 50.5 %all-gather.10.cloned.1.call-done = bf16[3072,384]{1,0:T(8,128)(2,1)} async-done(((bf16[768,384]{1,0:T(8,128)(2,1)}), bf16[3072,384]{1,0:T(8,128)(2,1)}) %all-gather.10.cloned.1.call-update) | async-done | bytes 2359312 | tf_op jit(solution)/shard_map/all_gather | solution.py:59
  67.8 6.6 fusion.93
  75.9 84.9 %reduce-scatter.10.cloned.1.call-done = f32[1536,576]{0,1:T(8,128)} async-done(((f32[3072,576]{0,1:T(8,128)}), f32[1536,576]{0,1:T(8,128)}) %reduce-scatter.10.cloned.1.call-update) | async-done | bytes 3538960 | tf_op jit(solution)/shard_map/reduce_scatter | solution.py:68
  170.2 31.4 %all-gather.12.cloned.1.call-done = bf16[3072,384]{0,1:T(8,128)(2,1)} async-done(((bf16[1536,384]{0,1:T(8,128)(2,1)}), bf16[3072,384]{0,1:T(8,128)(2,1)}) %all-gather.12.cloned.1.call-update) | async-done | bytes 2359312 | tf_op jit(solution)/shard_map/all_gather | solution.py:264
  207.7 3.7 copy.47
  211.4 93.5 %while.30 = (s32[]{:T(128)}, bf16[3,1536,64]{1,2,0:T(8,128)(2,1)S(1)}, f32[3,1536]{1,0:T(4,128)}, bf16[3,1536,64]{2,1,0:T(8,128)(2,1)}, bf16[3,3072,64]{2,1,0:T(...) while((s32[]{:T(128)}, ...), condition=%wide.region_10.11_spmd.clone.clone, body=%wide.region_7.10_spmd.clone.sunk.clone | while | flops 1264581120 | bytes 59093104 | solution.py:174
  211.4 12.4 fusion.165
  223.8 9.0 fusion.166
  232.7 8.4 fusion.167
  242.6 12.3 fusion.165
  254.9 9.0 fusion.166
  263.9 8.4 fusion.167
  273.8 12.3 fusion.165
  286.1 9.0 fusion.166
  295.1 8.4 fusion.167
  305.8 22.9 %all-gather.14.cloned.1.call-done = bf16[3072,192]{0,1:T(8,128)(2,1)} async-done(((bf16[1536,192]{0,1:T(8,128)(2,1)}), bf16[3072,192]{0,1:T(8,128)(2,1)}) %all-gather.14.cloned.1.call-update) | async-done | bytes 1179664 | tf_op jit(solution)/shard_map/all_gather | solution.py:79
  328.7 4.4 fusion.94
  335.8 82.9 %reduce-scatter.12.cloned.1.call-done = f32[768,384]{1,0:T(8,128)} async-done(((f32[3072,384]{1,0:T(8,128)}), f32[768,384]{1,0:T(8,128)}) %reduce-scatter.12.cloned.1.call-update) | async-done | bytes 1179664 | tf_op jit(solution)/shard_map/reduce_scatter | solution.py:88
  420.3 3.8 all-reduce.9
  425.6 43.8 %all-gather.20.cloned.1.call-done = bf16[3072,384]{1,0:T(8,128)(2,1)} async-done(((bf16[768,384]{1,0:T(8,128)(2,1)}), bf16[3072,384]{1,0:T(8,128)(2,1)}) %all-gather.20.cloned.1.call-update) | async-done | bytes 2359312 | tf_op jit(solution)/shard_map/all_gather | solution.py:59
  469.4 7.9 fusion.97
  477.4 42.9 %all-gather.16.cloned.1.call-done = bf16[3072,384]{1,0:T(8,128)(2,1)} async-done(((bf16[768,384]{1,0:T(8,128)(2,1)}), bf16[3072,384]{1,0:T(8,128)(2,1)}) %all-gather.16.cloned.1.call-update) | async-done | bytes 2359312 | tf_op jit(solution)/shard_map/all_gather | solution.py:59
  520.3 7.9 fusion.95
  528.9 104.9 %reduce-scatter.18.cloned.1.call-done = f32[1536,768]{1,0:T(8,128)} async-done(((f32[3072,768]{1,0:T(8,128)}), f32[1536,768]{1,0:T(8,128)}) %reduce-scatter.18.cloned.1.call-update) | async-done | bytes 4718608 | tf_op jit(solution)/shard_map/reduce_scatter | solution.py:68
  633.8 113.0 %reduce-scatter.14.cloned.1.call-done = f32[1536,768]{1,0:T(8,128)} async-done(((f32[3072,768]{1,0:T(8,128)}), f32[1536,768]{1,0:T(8,128)}) %reduce-scatter.14.cloned.1.call-update) | async-done | bytes 4718608 | tf_op jit(solution)/shard_map/reduce_scatter | solution.py:68
  746.7 8.4 convert_reduce_fusion
  755.9 62.0 %all-gather.22.cloned.1.call-done = bf16[3072,768]{1,0:T(8,128)(2,1)} async-done(((bf16[1536,768]{1,0:T(8,128)(2,1)}), bf16[3072,768]{1,0:T(8,128)(2,1)}) %all-gather.22.cloned.1.call-update) | async-done | bytes 4718608 | tf_op jit(solution)/shard_map/all_gather | solution.py:79
  817.9 7.1 fusion.98
  825.1 57.0 %all-gather.18.cloned.1.call-done = bf16[3072,768]{1,0:T(8,128)(2,1)} async-done(((bf16[1536,768]{1,0:T(8,128)(2,1)}), bf16[3072,768]{1,0:T(8,128)(2,1)}) %all-gather.18.cloned.1.call-update) | async-done | bytes 4718608 | tf_op jit(solution)/shard_map/all_gather | solution.py:79
  882.1 7.1 fusion.96
  889.5 80.2 %reduce-scatter.20.cloned.1.call-done = f32[768,384]{1,0:T(8,128)} async-done(((f32[3072,384]{1,0:T(8,128)}), f32[768,384]{1,0:T(8,128)}) %reduce-scatter.20.cloned.1.call-update) | async-done | bytes 1179664 | tf_op jit(solution)/shard_map/reduce_scatter | solution.py:88
  972.3 3.8 all-reduce.8
  976.1 81.7 %reduce-scatter.16.cloned.1.call-done = f32[768,384]{1,0:T(8,128)} async-done(((f32[3072,384]{1,0:T(8,128)}), f32[768,384]{1,0:T(8,128)}) %reduce-scatter.16.cloned.1.call-update) | async-done | bytes 1179664 | tf_op jit(solution)/shard_map/reduce_scatter | solution.py:88
  1057.9 3.5 fusion.58
  1063.3 48.8 %all-gather.24.cloned.1.call-done = bf16[3072,384]{1,0:T(8,128)(2,1)} async-done(((bf16[768,384]{1,0:T(8,128)(2,1)}), bf16[3072,384]{1,0:T(8,128)(2,1)}) %all-gather.24.cloned.1.call-update) | async-done | bytes 2359312 | tf_op jit(solution)/shard_map/all_gather | solution.py:59
  1112.1 4.1 fusion.99
  1116.3 35.4 %reduce-scatter.22.cloned.1.call-done = f32[1536,192]{0,1:T(8,128)} async-done(((f32[3072,192]{0,1:T(8,128)}), f32[1536,192]{0,1:T(8,128)}) %reduce-scatter.22.cloned.1.call-update) | async-done | bytes 1179664 | tf_op jit(solution)/shard_map/reduce_scatter | solution.py:68
  1154.3 147.2 %while.31 = (s32[]{:T(128)}, f32[3,1536,64]{1,2,0:T(8,128)}, bf16[3,3072,64]{1,2,0:T(8,128)(2,1)}, bf16[3,3072,64]{1,2,0:T(8,128)(2,1)}, bf16[3,1536,64]{2,1,0:T...) while((s32[]{:T(128)}, f32[3,1536,64]{1,2,0:T(8,128)}, ...), condition=%wide.region_27.28_spmd.clone.clone, body=%wide.region_25.27_spmd.clone.sunk.clone | while | flops 3081533952 | bytes 189987504 | solution.py:194
  1155.0 9.2 fusion.176
  1164.2 13.4 multiply_reduce_fusion.10
  1177.6 13.0 multiply_convert_fusion.5
  1193.2 6.4 fusion.178
  1199.6 3.7 fusion.177
  1204.1 9.2 fusion.176
  1213.2 13.4 multiply_reduce_fusion.10
  1226.6 13.0 multiply_convert_fusion.5
  1242.3 6.4 fusion.178
  1248.6 3.7 fusion.177
  1253.2 9.2 fusion.176
  1262.3 13.4 multiply_reduce_fusion.10
  1275.7 13.0 multiply_convert_fusion.5
  1291.3 6.4 fusion.178
  1297.7 3.7 fusion.177
  1305.0 34.6 %reduce-scatter.24.cloned.1.call-done = bf16[1536,384]{0,1:T(8,128)(2,1)} async-done(((bf16[3072,384]{0,1:T(8,128)(2,1)}), bf16[1536,384]{0,1:T(8,128)(2,1)}) %reduce-scatter.24.cloned.1.call-update) | async-done | bytes 1179664 | tf_op jit(solution)/shard_map/reduce_scatter | solution.py:301
  1343.8 49.5 %all-gather.26.cloned.1.call-done = bf16[3072,576]{0,1:T(8,128)(2,1)} async-done(((bf16[1536,576]{0,1:T(8,128)(2,1)}), bf16[3072,576]{0,1:T(8,128)(2,1)}) %all-gather.26.cloned.1.call-update) | async-done | bytes 3538960 | tf_op jit(solution)/shard_map/all_gather | solution.py:79
  1393.2 6.6 fusion.100
  1401.5 5.5 fusion.103
  1407.1 6.3 fusion.104
  1418.1 67.3 %reduce-scatter.26.cloned.1.call-done = f32[768,384]{1,0:T(8,128)} async-done(((f32[3072,384]{1,0:T(8,128)}), f32[768,384]{1,0:T(8,128)}) %reduce-scatter.26.cloned.1.call-update) | async-done | bytes 1179664 | tf_op jit(solution)/shard_map/reduce_scatter | solution.py:88
  1487.7 26.1 %all-reduce.4 = (f32[2,9,384]{2,1,0:T(8,128)S(1)}, f32[4,768]{1,0:T(4,128)S(1)}) all-reduce(f32[2,9,384]{2,1,0:T(8,128)S(1)} %broadcast_select_fusion, f32[4,768]{1,0:T(4,128)S(1)} %broadcast_select_fusion.1), channel_id=1, replica_groups=mesh['dp'=4,'row'=2,'col'=4] {'row','col'}, use_global_device_ids=true, to_apply=%region_43.44 | all-reduce | flops 9984 | bytes 79872 | tf_op jit(solution)/shard_map/psum | solution.py:340
  1515.1 18.5 %all-reduce.5 = (f32[9,384]{1,0:T(8,128)S(1)}, f32[768]{0:T(1024)}) all-reduce(f32[9,384]{1,0:T(8,128)S(1)} %dynamic-slice_bitcast_fusion, f32[768]{0:T(1024)S(1)} %dynamic-slice_reduce_fusion.1), channel_id=1, replica_groups=mesh['dp'=4,'row'=2,'col'=4] {'dp'}, use_global_device_ids=true, to_apply=%region_45.46 | all-reduce | flops 4224 | bytes 33792 | tf_op jit(solution)/shard_map/psum | solution.py:383
  1534.2 4.2 all-reduce.7
  1540.5 77.1 %all-reduce.13.cloned.1.call-done = (f32[128,6,384]{2,0,1:T(8,128)}, f32[576,384]{1,0:T(8,128)}, f32[192,384]{1,0:T(8,128)}, f32[384,768]{1,0:T(8,128)}, f32[768,384]{1,0:T(8,128)}) async-done(((f32[128,6,384]{2,0,1:T(8,128)}, f32[576,384]{1,0:T(8,128)}, f32[192,384]{1,0:T(8,128)}, f32[384,768]{1,0:T(8,128)}, f32[768,384]{1,0:T(8,128)}), (f32[128,6,384]{2,0,1:T(8,128)}, f32[576,384]{1,0:T(8,128)}, ...) | async-done | bytes 4718608 | tf_op jit(solution)/shard_map/psum | solution.py:383
  (266 shorter events, 79.3 us)
Async XLA Ops:
  7.2 513.1 %copy-start = (bf16[384,768]{1,0:T(8,128)(2,1)S(1)}, bf16[384,768]{1,0:T(8,128)(2,1)}, u32[]{:S(2)}) copy-start(bf16[384,768]{1,0:T(8,128)(2,1)} %param.28) | copy-start | bytes 1769476
  7.2 8.8 copy-start.6
  7.2 3.8 copy-start.48
  7.2 8.8 copy-start.40
  7.2 60.5 %all-gather.10.cloned.1.call-start = ((), (), s32[]{:S(2)}) async-start(), calls=%async_computation.9 | async-start | bytes 2949120 | tf_op jit(solution)/shard_map/all_gather | solution.py:59
  9.5 58.3 %copy-start.30 = (bf16[576,384]{1,0:T(8,128)(2,1)S(1)}, bf16[576,384]{1,0:T(8,128)(2,1)}, u32[]{:S(2)}) copy-start(bf16[576,384]{1,0:T(8,128)(2,1)} %param.25) | copy-start | bytes 1327108
  11.6 62.8 %copy-start.37 = (f32[384]{0:T(512)}, f32[384]{0:T(512)S(1)}, u32[]{:S(2)}) copy-start(f32[384]{0:T(512)S(1)} %get-tuple-element.257) | copy-start | bytes 4612
  17.2 143.5 %reduce-scatter.10.cloned.1.call-start = ((), (), s32[]{:S(2)}) async-start(), calls=%async_computation.10 | async-start | bytes 10616832 | tf_op jit(solution)/shard_map/reduce_scatter | solution.py:68
  74.4 127.2 %all-gather.12.cloned.1.call-start = ((), (), s32[]{:S(2)}) async-start(), calls=%async_computation.11 | async-start | bytes 3538944 | tf_op jit(solution)/shard_map/all_gather | solution.py:264
  75.8 88.0 %copy-start.20 = (f32[1536,32]{0,1:T(8,128)}, f32[1536,32]{0,1:T(8,128)S(1)}, u32[]{:S(2)}) copy-start(f32[1536,32]{0,1:T(8,128)S(1)} %get-tuple-element.356) | copy-start | bytes 589828
  75.8 88.0 %copy-start.22 = (f32[1536,32]{0,1:T(8,128)}, f32[1536,32]{0,1:T(8,128)S(1)}, u32[]{:S(2)}) copy-start(f32[1536,32]{0,1:T(8,128)S(1)} %get-tuple-element.357) | copy-start | bytes 589828
  165.4 163.3 %all-gather.14.cloned.1.call-start = ((), (), s32[]{:S(2)}) async-start(), calls=%async_computation.12 | async-start | bytes 1769472 | tf_op jit(solution)/shard_map/all_gather | solution.py:79
  304.9 28.2 %copy-start.4 = (bf16[3,3072,64]{2,1,0:T(8,128)(2,1)}, bf16[3,3072,64]{2,1,0:T(8,128)(2,1)S(1)}, u32[]{:S(2)}) copy-start(bf16[3,3072,64]{2,1,0:T(8,128)(2,1)S(1)} %get-tuple-element.688) | copy-start | bytes 3538948
  305.8 112.9 %reduce-scatter.12.cloned.1.call-start = ((), (), s32[]{:S(2)}) async-start(), calls=%async_computation.13 | async-start | bytes 5898240 | tf_op jit(solution)/shard_map/reduce_scatter | solution.py:88
  333.1 85.5 %copy-start.7 = (bf16[768,384]{1,0:T(8,128)(2,1)S(1)}, bf16[768,384]{1,0:T(8,128)(2,1)}, u32[]{:S(2)}) copy-start(bf16[768,384]{1,0:T(8,128)(2,1)} %param.18) | copy-start | bytes 1769476
  333.1 85.5 %copy-start.42 = (f32[384]{0:T(512)S(1)}, f32[384]{0:T(512)}, u32[]{:S(2)}) copy-start(f32[384]{0:T(512)} %get-tuple-element.258) | copy-start | bytes 4612
  333.2 136.2 %all-gather.20.cloned.1.call-start = ((), (), s32[]{:S(2)}) async-start(), calls=%async_computation.18 | async-start | bytes 2949120 | tf_op jit(solution)/shard_map/all_gather | solution.py:59
  335.8 184.5 %all-gather.16.cloned.1.call-start = ((), (), s32[]{:S(2)}) async-start(), calls=%async_computation.14 | async-start | bytes 2949120 | tf_op jit(solution)/shard_map/all_gather | solution.py:59
  418.7 5.5 copy-start.39
  418.7 5.5 copy-start.45
  418.7 5.5 copy-start.54
  424.2 45.2 %copy-start.28 = (bf16[768,384]{1,0:T(8,128)(2,1)S(1)}, bf16[768,384]{1,0:T(8,128)(2,1)}, u32[]{:S(2)}) copy-start(bf16[768,384]{1,0:T(8,128)(2,1)} %param.30) | copy-start | bytes 1769476
  425.4 208.4 %reduce-scatter.18.cloned.1.call-start = ((), (), s32[]{:S(2)}) async-start(), calls=%async_computation.19 | async-start | bytes 14155776 | tf_op jit(solution)/shard_map/reduce_scatter | solution.py:68
  477.3 269.4 %reduce-scatter.14.cloned.1.call-start = ((), (), s32[]{:S(2)}) async-start(), calls=%async_computation.15 | async-start | bytes 14155776 | tf_op jit(solution)/shard_map/reduce_scatter | solution.py:68
  528.2 289.7 %all-gather.22.cloned.1.call-start = ((), (), s32[]{:S(2)}) async-start(), calls=%async_computation.20 | async-start | bytes 7077888 | tf_op jit(solution)/shard_map/all_gather | solution.py:79
  755.1 127.0 %all-gather.18.cloned.1.call-start = ((), (), s32[]{:S(2)}) async-start(), calls=%async_computation.16 | async-start | bytes 7077888 | tf_op jit(solution)/shard_map/all_gather | solution.py:79
  755.9 213.8 %reduce-scatter.20.cloned.1.call-start = ((), (), s32[]{:S(2)}) async-start(), calls=%async_computation.21 | async-start | bytes 5898240 | tf_op jit(solution)/shard_map/reduce_scatter | solution.py:88
  825.0 232.8 %reduce-scatter.16.cloned.1.call-start = ((), (), s32[]{:S(2)}) async-start(), calls=%async_computation.17 | async-start | bytes 5898240 | tf_op jit(solution)/shard_map/reduce_scatter | solution.py:88
  889.2 80.5 %copy-start.46 = (f32[384]{0:T(512)S(1)}, f32[384]{0:T(512)}, u32[]{:S(2)}) copy-start(f32[384]{0:T(512)} %param.27) | copy-start | bytes 4612
  889.3 168.6 %copy-start.15 = (f32[768,384]{1,0:T(8,128)S(1)}, f32[768,384]{1,0:T(8,128)}, u32[]{:S(2)}) copy-start(f32[768,384]{1,0:T(8,128)} %reduce-scatter.12.cloned.1.call-done) | copy-start | bytes 3538948
  889.3 168.6 %copy-start.44 = (f32[384]{0:T(512)S(1)}, f32[384]{0:T(512)}, u32[]{:S(2)}) copy-start(f32[384]{0:T(512)} %get-tuple-element.253) | copy-start | bytes 4612
  889.3 168.6 %copy-start.61 = (f32[384]{0:T(512)S(1)}, f32[384]{0:T(512)}, u32[]{:S(2)}) copy-start(f32[384]{0:T(512)} %param.31) | copy-start | bytes 4612
  889.3 222.8 %all-gather.24.cloned.1.call-start = ((), (), s32[]{:S(2)}) async-start(), calls=%async_computation.22 | async-start | bytes 2949120 | tf_op jit(solution)/shard_map/all_gather | solution.py:59
  1062.4 49.7 %copy-start.29 = (bf16[192,384]{1,0:T(8,128)(2,1)S(1)}, bf16[192,384]{1,0:T(8,128)(2,1)}, u32[]{:S(2)}) copy-start(bf16[192,384]{1,0:T(8,128)(2,1)} %param.26) | copy-start | bytes 442372
  1063.3 88.4 %reduce-scatter.22.cloned.1.call-start = ((), (), s32[]{:S(2)}) async-start(), calls=%async_computation.23 | async-start | bytes 3538944 | tf_op jit(solution)/shard_map/reduce_scatter | solution.py:68
  1116.2 223.5 %reduce-scatter.24.cloned.1.call-start = ((), (), s32[]{:S(2)}) async-start(), calls=%async_computation.24 | async-start | bytes 3538944 | tf_op jit(solution)/shard_map/reduce_scatter | solution.py:301
  1155.0 9.2 copy-start.5
  1193.2 6.4 copy-start.2
  1204.1 9.2 copy-start.5
  1242.3 6.4 copy-start.2
  1253.1 9.2 copy-start.5
  1291.3 6.4 copy-start.2
  1304.7 88.5 %all-gather.26.cloned.1.call-start = ((), (), s32[]{:S(2)}) async-start(), calls=%async_computation.25 | async-start | bytes 5308416 | tf_op jit(solution)/shard_map/all_gather | solution.py:79
  1343.7 49.5 %copy-start.31 = (bf16[576,384]{1,0:T(8,128)(2,1)S(1)}, bf16[576,384]{1,0:T(8,128)(2,1)}, u32[]{:S(2)}) copy-start(bf16[576,384]{1,0:T(8,128)(2,1)} %param.25) | copy-start | bytes 1327108
  1343.7 141.7 %reduce-scatter.26.cloned.1.call-start = ((), (), s32[]{:S(2)}) async-start(), calls=%async_computation.26 | async-start | bytes 5898240 | tf_op jit(solution)/shard_map/reduce_scatter | solution.py:88
  1399.8 217.8 %all-reduce.13.cloned.1.call-start = ((), (), s32[]{:S(2)}) async-start(), calls=%async_computation.27 | async-start | bytes 9437184 | tf_op jit(solution)/shard_map/psum | solution.py:383
  1401.5 5.5 copy-start.9
  1407.0 6.4 copy-start.53
  1407.0 6.4 copy-start.52
  1407.0 6.4 copy-start.51
  1407.0 6.4 copy-start.56
  1407.1 6.4 copy-start.55
  1407.1 6.5 copy-start.13
  1407.1 6.5 copy-start.16
  1407.1 8.0 copy-start.62
  1415.2 70.2 %copy-start.8 = (bf16[768,384]{1,0:T(8,128)(2,1)S(1)}, bf16[768,384]{1,0:T(8,128)(2,1)}, u32[]{:S(2)}) copy-start(bf16[768,384]{1,0:T(8,128)(2,1)} %param.18) | copy-start | bytes 1769476
  1415.2 70.2 %copy-start.34 = (f32[768]{0:T(1024)S(1)}, f32[768]{0:T(1024)}, u32[]{:S(2)}) copy-start(f32[768]{0:T(1024)} %copy-done.33) | copy-start | bytes 9220
  1415.2 70.2 %copy-start.36 = (f32[768]{0:T(1024)S(1)}, f32[768]{0:T(1024)}, u32[]{:S(2)}) copy-start(f32[768]{0:T(1024)} %copy-done.35) | copy-start | bytes 9220
  1415.2 70.2 %copy-start.38 = (f32[384]{0:T(512)S(1)}, f32[384]{0:T(512)}, u32[]{:S(2)}) copy-start(f32[384]{0:T(512)} %copy-done.37) | copy-start | bytes 4612
  1415.2 70.2 %copy-start.41 = (f32[384]{0:T(512)S(1)}, f32[384]{0:T(512)}, u32[]{:S(2)}) copy-start(f32[384]{0:T(512)} %param.24) | copy-start | bytes 4612
  1418.1 95.6 %copy-start.60 = (f32[128]{0:T(128)S(1)}, f32[128]{0:T(128)}, u32[]{:S(2)}) copy-start(f32[128]{0:T(128)} %copy-done.59) | copy-start | bytes 1540
  1515.0 24.0 %copy-start.11 = (f32[768,384]{1,0:T(8,128)S(1)}, f32[768,384]{1,0:T(8,128)}, u32[]{:S(2)}) copy-start(f32[768,384]{1,0:T(8,128)} %copy-done.10) | copy-start | bytes 3538948
  1515.0 24.0 %copy-start.14 = (f32[768,384]{1,0:T(8,128)S(1)}, f32[768,384]{1,0:T(8,128)}, u32[]{:S(2)}) copy-start(f32[768,384]{1,0:T(8,128)} %reduce-scatter.26.cloned.1.call-done) | copy-start | bytes 3538948
  1621.9 2.7 copy-start.1
  (22 other events, 27.2 us)
Sparse Core Ops, SparseCore 0:
  17.3 50.3 all-gather.9
  74.5 86.1 reduce-scatter.9
  165.6 36.0 all-gather.11
  305.9 22.7 all-gather.13
  333.3 85.3 reduce-scatter.11
  420.7 48.6 all-gather.19
  471.5 48.7 all-gather.15
  522.6 111.1 reduce-scatter.17
  636.1 110.6 reduce-scatter.13
  755.2 62.6 all-gather.21
  819.5 62.6 all-gather.17
  884.3 85.3 reduce-scatter.19
  972.0 85.7 reduce-scatter.15
  1063.4 48.6 all-gather.23
  1116.3 35.2 reduce-scatter.21
  1304.9 34.7 reduce-scatter.23
  1343.8 49.3 all-gather.25
  1400.0 85.4 reduce-scatter.25
  1515.1 102.4 all-reduce.12
where the time goes:
time: 1640 us; the launch traced here: 1630 us
  waiting for transfers between devices  1170 us (71%)
  matrix products  238 us (15%)
  other arithmetic  106 us (6%)
  blocking collectives  60.3 us (4%)
  local copies, waits for them, and re-layouts  38 us (2%)
    reduce_scatter x4, waiting for transfers between devices, into_heads(): lax.psum_scatter(partial_product(jnp.int32(0), share_rows * lax.axis_size...  338 us
    reduce_scatter x4, waiting for transfers between devices, into_stream(): lax.psum_scatter(partial_product(jnp.int32(0), share_rows * lax.axis_size...  312 us
    all_gather x4, waiting for transfers between devices, into_stream(): gathered = lax.all_gather(activation, 'row', axis=0, tiled=True)  191 us
    all_gather x4, waiting for transfers between devices, into_heads(): gathered = lax.all_gather(activation, 'col', axis=0, tiled=True)  186 us
    psum x1, waiting for transfers between devices, shards(): lax.psum((d_qkv, d_out_proj, d_up, d_down, d_mod_w, small_rows, d_up_bias...  77.1 us
    dot_general x8, matrix products, partial_product(): lax.dot_general(gathered, weight, (((1,), (contract,)), ((), ())), prefer...  51.7 us
    dot_general x10, matrix products, weight_grad(): lax.dot_general(first_operand, second_operand, (((0,), (0,)), ((), ())),...  43.1 us
    dot_general x3, matrix products, attend_back(): lax.dot_general(query_head, key_head, (((1,), (1,)), ((), ())), preferred...  40.2 us
  transfers between devices with their start and end apart: 19, of which 19 were waited for; matrix products, arithmetic and copies ran while one was open for 4% of the time, Pallas kernels for 0%

commit v1 on v0

v1 whole, which is shorter than its diff:
```python
import functools
import math

import jax
import jax.numpy as jnp
from jax import lax
from jax.experimental import pallas as pl
from jax.experimental.pallas import tpu as pltpu
from jax.sharding import PartitionSpec as P

D = 768
HEAD = 64
HALF = HEAD // 2
COND = 128
PIECE = 256
KEYS = 256
LANES = 128
SCORE = HEAD ** (-0.5) * math.log2(math.e)
MASKED = -1e30

precise = lax.Precision.HIGHEST
epsilon = 1e-05
f32 = jnp.float32
bf16 = jnp.bfloat16


def row_swap(value):
    return lax.ppermute(value, "row", [(0, 1), (1, 0)])


def dp_swap(value, bit):
    return lax.ppermute(value, "dp", [(i, i ^ (1 << bit)) for i in range(lax.axis_size("dp"))])


def col_swap(value, bit):
    return lax.ppermute(value, "col", [(i, i ^ (1 << bit)) for i in range(lax.axis_size("col"))])


def col_from(value, hop):
    size = lax.axis_size("col")
    return lax.ppermute(value, "col", [(i, (i + hop) % size) for i in range(size)]) if hop else value


def col_to(value, hop):
    size = lax.axis_size("col")
    return lax.ppermute(value, "col", [(i, (i - hop) % size) for i in range(size)]) if hop else value


def bits(axis):
    return lax.axis_size(axis).bit_length() - 1


def core_bit():
    return lax.axis_index("dp") % 2


def in_order(bit, mine, theirs):
    first = bit == 0
    return jnp.where(first, mine, theirs), jnp.where(first, theirs, mine)


def half_at(value, index, axis):
    size = value.shape[axis] // 2
    return lax.dynamic_slice_in_dim(value, index * size, size, axis)


def gather_pieces(mine, join_axis):
    cols = lax.axis_size("col")
    own = jnp.stack([col_from(mine, k) for k in range(cols)])
    other = row_swap(own)
    joined = jnp.concatenate([own, other], join_axis)
    return joined, dp_swap(joined, 0)


def scatter_pieces(mine, theirs, join_axis):
    cols = lax.axis_size("col")
    total = (mine.astype(f32) + dp_swap(theirs, 0).astype(f32)).astype(bf16)
    own, other = jnp.split(total, 2, join_axis)
    total = (own.astype(f32) + row_swap(other).astype(f32)).astype(bf16)
    total = sum(col_to(total[k], k).astype(f32) for k in range(cols))
    for bit in range(1, bits("dp")):
        total = total + dp_swap(total, bit)
    return in_order(core_bit(), total, dp_swap(total, 0))


def place_stripes(scalars, own_refs, other_refs, keys, values_t, keys_t=None, values=None):
    row, col = scalars[0], scalars[1]
    count = len(own_refs)
    width = own_refs[0].shape[1]
    parts = width // LANES
    for hop in range(count):
        place = lax.rem(col + hop, count)
        for stripe, ref, offset in (
            (2 * place + row, own_refs[hop], HEAD),
            (2 * place + 1 - row, other_refs[hop], 0),
        ):
            start = pl.multiple_of(stripe * width, LANES)
            key_t = ref[offset : offset + HEAD, :]
            value_t = ref[offset + HEAD : offset + 2 * HEAD, :]
            keys[pl.ds(start, width), :] = key_t.astype(f32).T.astype(bf16)
            if values is not None:
                values[pl.ds(start, width), :] = value_t.astype(f32).T.astype(bf16)
            for part in range(parts):
                lanes = slice(part * LANES, (part + 1) * LANES)
                if values_t is not None:
                    values_t[stripe * parts + part] = value_t[:, lanes]
                if keys_t is not None:
                    keys_t[stripe * parts + part] = key_t[:, lanes]


def lane_block(ref, block):
    parts = KEYS // LANES
    return jnp.concatenate([ref[block * parts + part] for part in range(parts)], 1)


def forward_kernel(count, scalars, *refs):
    own_refs, other_refs = refs[:count], refs[count : 2 * count]
    limit_ref, out_ref, wide_ref, log_ref, keys, values_t = refs[2 * count :]
    width = own_refs[0].shape[1]
    place_stripes(scalars, own_refs, other_refs, keys, values_t)
    row, col = scalars[0], scalars[1]
    for hop in range(count):
        query_t = own_refs[hop][0:HEAD, :]
        limit = limit_ref[hop]
        first = (2 * lax.rem(col + hop, count) + row) * width

        def step(masked, block, carry):
            top, total, mixed = carry
            start = pl.multiple_of(block * KEYS, KEYS)
            scores = jnp.dot(keys[pl.ds(start, KEYS), :], query_t, preferred_element_type=f32) * SCORE
            if masked:
                place = start + lax.broadcasted_iota(jnp.int32, scores.shape, 0)
                scores = jnp.where(place <= limit, scores, MASKED)
            new_top = jnp.maximum(top, jnp.max(scores, 0, keepdims=True))
            fade = jnp.exp2(top - new_top)
            weight = jnp.exp2(scores - new_top)
            total = total * fade + jnp.sum(weight, 0, keepdims=True)
            mixed = mixed * fade + jnp.dot(
                lane_block(values_t, block), weight.astype(bf16), preferred_element_type=f32
            )
            return new_top, total, mixed

        carry = (
            jnp.full((1, width), MASKED, f32),
            jnp.zeros((1, width), f32),
            jnp.zeros((HEAD, width), f32),
        )
        whole = first // KEYS
        carry = lax.fori_loop(0, whole, functools.partial(step, False), carry)
        top, total, mixed = lax.fori_loop(whole, scalars[2 + hop], functools.partial(step, True), carry)
        mixed = mixed / total
        out_ref[hop] = mixed.astype(bf16)
        wide_ref[hop] = mixed
        log_ref[hop] = top + jnp.log2(total)


def backward_kernel(count, scalars, *refs):
    own_refs, other_refs, grad_refs = refs[:count], refs[count : 2 * count], refs[2 * count : 3 * count]
    (wide_ref, log_ref, limit_ref, turn_ref, d_query_ref, d_own_ref, d_other_ref) = refs[3 * count : 3 * count + 7]
    keys, values, keys_t, d_keys, d_values = refs[3 * count + 7 :]
    width = own_refs[0].shape[1]
    place_stripes(scalars, own_refs, other_refs, keys, None, keys_t, values)
    row, col = scalars[0], scalars[1]
    d_keys[...] = jnp.zeros_like(d_keys)
    d_values[...] = jnp.zeros_like(d_values)

    def turn_back(vectors, stripe):
        cosine, sine = turn_ref[stripe, 0:HALF, :], turn_ref[stripe, HALF:HEAD, :]
        upper, lower = vectors[0:HALF], vectors[HALF:HEAD]
        return jnp.concatenate([upper * cosine + lower * sine, lower * cosine - upper * sine], 0)

    for hop in range(count):
        query_t = own_refs[hop][0:HEAD, :]
        grad_t = grad_refs[hop][...]
        query = query_t.astype(f32).T.astype(bf16)
        grad = grad_t.astype(f32).T.astype(bf16)
        drift = jnp.sum(grad_t.astype(f32) * wide_ref[hop], 0, keepdims=True)
        log_sum = log_ref[hop]
        limit = limit_ref[hop]
        stripe = 2 * lax.rem(col + hop, count) + row
        first = stripe * width

        def step(masked, block, d_query):
            start = pl.multiple_of(block * KEYS, KEYS)
            rows = pl.ds(start, KEYS)
            scores = jnp.dot(keys[rows, :], query_t, preferred_element_type=f32) * SCORE
            weight = jnp.exp2(scores - log_sum)
            if masked:
                place = start + lax.broadcasted_iota(jnp.int32, scores.shape, 0)
                weight = jnp.where(place <= limit, weight, 0.0)
            d_weight = jnp.dot(values[rows, :], grad_t, preferred_element_type=f32)
            d_scores = (weight * (d_weight - drift)).astype(bf16)
            d_values[rows, :] += jnp.dot(weight.astype(bf16), grad, preferred_element_type=f32)
            d_keys[rows, :] += jnp.dot(d_scores, query, preferred_element_type=f32)
            return d_query + jnp.dot(lane_block(keys_t, block), d_scores, preferred_element_type=f32)

        d_query = jnp.zeros((HEAD, width), f32)
        whole = first // KEYS
        d_query = lax.fori_loop(0, whole, functools.partial(step, False), d_query)
        d_query = lax.fori_loop(whole, scalars[2 + hop], functools.partial(step, True), d_query)
        d_query_ref[hop] = turn_back(d_query * HEAD ** (-0.5), stripe).astype(bf16)

    for hop in range(count):
        place = lax.rem(col + hop, count)
        for stripe, ref in ((2 * place + row, d_own_ref), (2 * place + 1 - row, d_other_ref)):
            start = pl.multiple_of(stripe * width, LANES)
            d_key = d_keys[pl.ds(start, width), :].T * HEAD ** (-0.5)
            ref[hop, 0:HEAD, :] = turn_back(d_key, stripe).astype(ref.dtype)
            ref[hop, HEAD : 2 * HEAD, :] = d_values[pl.ds(start, width), :].T.astype(ref.dtype)


def vmem(count):
    return [pl.BlockSpec(memory_space=pltpu.VMEM)] * count


def attention_forward(scalars, own, other, limit):
    count = len(own)
    width = own[0].shape[1]
    seq_len = 2 * count * width
    return pl.pallas_call(
        functools.partial(forward_kernel, count),
        in_specs=[pl.BlockSpec(memory_space=pltpu.SMEM)] + vmem(2 * count + 1),
        out_specs=vmem(3),
        out_shape=[
            jax.ShapeDtypeStruct((count, HEAD, width), bf16),
            jax.ShapeDtypeStruct((count, HEAD, width), f32),
            jax.ShapeDtypeStruct((count, 1, width), f32),
        ],
        scratch_shapes=[
            pltpu.VMEM((seq_len, HEAD), bf16),
            pltpu.VMEM((seq_len // LANES, HEAD, LANES), bf16),
        ],
        cost_estimate=pl.CostEstimate(flops=8_000_000_000, bytes_accessed=3_000_000, transcendentals=3_000_000),
        name="attend",
    )(scalars, *own, *other, limit)


def attention_backward(scalars, own, other, grads, wide, log_sum, limit, turns):
    count = len(own)
    width = own[0].shape[1]
    seq_len = 2 * count * width
    return pl.pallas_call(
        functools.partial(backward_kernel, count),
        in_specs=[pl.BlockSpec(memory_space=pltpu.SMEM)] + vmem(3 * count + 4),
        out_specs=vmem(3),
        out_shape=[
            jax.ShapeDtypeStruct((count, HEAD, width), bf16),
            jax.ShapeDtypeStruct((count, 2 * HEAD, width), f32),
            jax.ShapeDtypeStruct((count, 2 * HEAD, width), bf16),
        ],
        scratch_shapes=[
            pltpu.VMEM((seq_len, HEAD), bf16),
            pltpu.VMEM((seq_len, HEAD), bf16),
            pltpu.VMEM((seq_len // LANES, HEAD, LANES), bf16),
            pltpu.VMEM((seq_len, HEAD), f32),
            pltpu.VMEM((seq_len, HEAD), f32),
        ],
        cost_estimate=pl.CostEstimate(flops=16_000_000_000, bytes_accessed=4_000_000, transcendentals=3_000_000),
        name="attend_back",
    )(scalars, *own, *other, *grads, wide, log_sum, limit, turns)


def contract(first, second, first_axis, second_axis):
    return lax.dot_general(
        first, second, (((first_axis,), (second_axis,)), ((), ())), preferred_element_type=f32
    )


def feed_kernel(h_ref, df_ref, up_ref, bias_ref, down_ref, f_ref, dh_ref, d_up_ref, d_down_ref, d_bias_ref):
    step = pl.program_id(0)

    @pl.when(step == 0)
    def _():
        f_ref[...] = jnp.zeros_like(f_ref)
        dh_ref[...] = jnp.zeros_like(dh_ref)

    h = h_ref[...]
    df = df_ref[...]
    up = up_ref[0]
    down = down_ref[0]
    hidden = contract(h, up, 1, 0) + bias_ref[0]
    squared = hidden * hidden
    bent = jnp.tanh(0.79788456 * hidden * (1.0 + 0.044715 * squared))
    active = (0.5 * hidden * (1.0 + bent)).astype(bf16)
    slope = 0.5 * (1.0 + bent) + 0.5 * hidden * (1.0 - bent * bent) * (
        0.79788456 * (1.0 + 3.0 * 0.044715 * squared)
    )
    f_ref[...] += contract(active, down, 1, 0)
    d_hidden_wide = slope * contract(df, down, 1, 1)
    d_hidden = d_hidden_wide.astype(bf16)
    d_bias_ref[0] = jnp.sum(d_hidden.astype(f32), 0, keepdims=True)
    dh_ref[...] += contract(d_hidden, up, 1, 1)
    d_down_ref[0] = contract(active, df, 0, 0).astype(bf16)
    d_up_ref[0] = contract(h, d_hidden, 0, 0).astype(bf16)


def feed_forward(h, df, up, bias, down):
    blocks, width, hidden = up.shape
    rows = h.shape[0]
    whole = pl.BlockSpec((rows, width), lambda b: (0, 0))
    return pl.pallas_call(
        feed_kernel,
        grid=(blocks,),
        in_specs=[
            whole,
            whole,
            pl.BlockSpec((1, width, hidden), lambda b: (b, 0, 0)),
            pl.BlockSpec((1, 1, hidden), lambda b: (b, 0, 0)),
            pl.BlockSpec((1, hidden, width), lambda b: (b, 0, 0)),
        ],
        out_specs=[
            whole,
            whole,
            pl.BlockSpec((1, width, hidden), lambda b: (b, 0, 0)),
            pl.BlockSpec((1, hidden, width), lambda b: (b, 0, 0)),
            pl.BlockSpec((1, 1, hidden), lambda b: (b, 0, 0)),
        ],
        out_shape=[
            jax.ShapeDtypeStruct((rows, width), f32),
            jax.ShapeDtypeStruct((rows, width), f32),
            jax.ShapeDtypeStruct(up.shape, bf16),
            jax.ShapeDtypeStruct(down.shape, bf16),
            jax.ShapeDtypeStruct((blocks, 1, hidden), f32),
        ],
        cost_estimate=pl.CostEstimate(
            flops=12 * rows * width * hidden * blocks, bytes_accessed=24_000_000, transcendentals=1_000_000
        ),
        name="feed",
    )(h, df, up, bias, down)


def embed_time(time_step):
    half_size = COND // 2
    frequency = jnp.exp(-math.log(10000.0) * jnp.arange(half_size, dtype=f32) / half_size)
    angles = time_step * frequency
    return jax.nn.silu(jnp.concatenate([jnp.cos(angles), jnp.sin(angles)]))


def norm_forward(values, gain, shift, scale):
    mean = jnp.mean(values, -1, keepdims=True)
    centered = values - mean
    inv_std = lax.rsqrt(jnp.mean(centered * centered, -1, keepdims=True) + epsilon)
    normed = centered * inv_std
    return normed, inv_std, (normed * gain * (1.0 + scale) + shift).astype(bf16)


def norm_backward(upstream, normed, inv_std, gain, scale):
    scaled = upstream * (gain * (1.0 + scale))
    mean_grad = jnp.mean(scaled, -1, keepdims=True)
    mean_proj = jnp.mean(scaled * normed, -1, keepdims=True)
    return (
        inv_std * (scaled - mean_grad - normed * mean_proj),
        jnp.sum(upstream, 0),
        jnp.sum(upstream * normed, 0),
    )


def rotate(first, second, cosine, sine):
    return first * cosine - second * sine, second * cosine + first * sine


def shards(
    tokens, cotangent, timestep, piece_starts, w_mod, b_mod, gain_attn, w_qkv, w_out, gain_mlp, w_up, b_up, w_down, b_down
):
    cols = lax.axis_size("col")
    row, col, core = lax.axis_index("row"), lax.axis_index("col"), core_bit()
    block_rows, part = tokens.shape
    width = block_rows // 2
    slots = w_qkv.shape[0] // (3 * HEAD)

    def half_rows(block):
        other = row_swap(half_at(block, 1 - row, 0))
        return jnp.concatenate([half_at(block, row, 0), other], 1).astype(f32)

    residual = half_rows(tokens)
    condition = embed_time(timestep[0].astype(f32))
    modulation = jnp.einsum("k,kjd->jd", condition, w_mod.astype(f32), precision=precise) + b_mod
    small = jnp.concatenate([modulation, gain_attn[None], gain_mlp[None], b_down[None]], 0)
    small = jnp.concatenate([small, row_swap(small)], 1)
    shift_attn, scale_attn, gate_attn, shift_mlp, scale_mlp, gate_mlp, gain_a, gain_m, bias_down = (
        small[i : i + 1] for i in range(9)
    )

    normed_one, inv_one, h_one = norm_forward(residual, gain_a, shift_attn, scale_attn)

    lane = jnp.arange(width, dtype=jnp.int32)
    frequency = jnp.exp(-math.log(10000.0) * jnp.arange(HALF, dtype=f32) / HALF)
    places = jnp.arange(2 * cols, dtype=jnp.int32)[:, None] * width + lane[None]
    angles = places.astype(f32)[:, None, :] * frequency[None, :, None]
    turns = jnp.concatenate([jnp.cos(angles), jnp.sin(angles)], 1)
    here = lax.dynamic_index_in_dim(turns, 2 * col + row, 0, keepdims=False)
    cosine, sine = here[:HALF], here[HALF:]
    own_stripes = 2 * ((col + jnp.arange(cols, dtype=jnp.int32)) % cols) + row
    own_places = own_stripes[:, None] * width + lane[None]
    starts = piece_starts[0]
    inside = (own_places[..., None] >= starts) & (own_places[..., None] < starts + PIECE)
    limit = jnp.max(jnp.where(inside, starts + PIECE - 1, own_places[..., None]), -1)
    scalars = jnp.concatenate([row[None], col[None], jnp.max(limit, 1) // KEYS + 1]).astype(jnp.int32)
    limit = limit[:, None, :]

    w_qkv_parts = w_qkv.reshape(slots, 3, 2, HALF, part)
    w_slots, own_heads, other_heads, forward = [], [], [], []
    for slot in range(slots):
        mine = lax.dynamic_index_in_dim(w_qkv_parts[slot], core, 1, keepdims=False).reshape(3 * HALF, part)
        mine, theirs = gather_pieces(mine, 2)
        lower, upper = in_order(
            core, mine.reshape(cols, 3, HALF, 2 * part), theirs.reshape(cols, 3, HALF, 2 * part)
        )
        weight = jnp.stack([lower, upper], 2).reshape(cols * 3 * HEAD, 2 * part)
        w_slots.append(weight)
        projected = contract(weight, h_one, 1, 1).reshape(cols, 3, 2, HALF, width)
        first, second = projected[:, :2, 0], projected[:, :2, 1]
        first, second = rotate(first, second, cosine, sine)
        turned = jnp.stack([first, second], 2)
        pieces = jnp.concatenate([turned, projected[:, 2:]], 1).reshape(cols, 3 * HEAD, width).astype(bf16)
        own = [col_to(pieces[k], k) for k in range(cols)]
        other = [row_swap(piece[HEAD:]) for piece in own]
        own_heads.append(own)
        other_heads.append(other)
        forward.append(attention_forward(scalars, own, other, limit))

    mixed = jnp.stack(
        [jnp.stack([col_from(forward[slot][0][k], k) for k in range(cols)]) for slot in range(slots)], 1
    ).reshape(cols * slots * HEAD, width)

    mine, theirs = gather_pieces(half_at(w_out, core, 0), 2)
    w_out_all = jnp.stack(in_order(core, mine, theirs), 1).reshape(cols * slots * HEAD, 2 * part)
    up = jnp.concatenate(gather_pieces(half_at(w_up, core, 1), 1), 0)
    down = jnp.concatenate(gather_pieces(half_at(w_down, core, 0), 2), 0)
    bias = jnp.stack([col_from(b_up[None], k) for k in range(cols)])
    bias = jnp.concatenate([half_at(bias, core, 2), half_at(bias, 1 - core, 2)], 0).astype(f32)

    attended = contract(mixed, w_out_all, 0, 0)
    middle = residual + gate_attn * attended
    normed_two, inv_two, h_two = norm_forward(middle, gain_m, shift_mlp, scale_mlp)
    upstream = half_rows(cotangent)
    d_branch = (upstream * gate_mlp).astype(bf16)
    branch, d_h_two, d_up, d_down, d_bias = feed_forward(h_two, d_branch, up, bias, down)
    branch = branch + bias_down
    block_out = (middle + gate_mlp * branch).astype(bf16)

    d_middle, sum_two, proj_two = norm_backward(d_h_two, normed_two, inv_two, gain_m, scale_mlp)
    d_middle = d_middle + upstream
    d_attended = (d_middle * gate_attn).astype(bf16)
    d_mixed = contract(w_out_all, d_attended, 1, 1).astype(bf16).reshape(cols, slots, HEAD, width)
    d_out = contract(mixed, d_attended, 1, 0).astype(bf16).reshape(cols, 2, slots * HEAD // 2, 2 * part)

    def halves(value, axis):
        return (
            lax.dynamic_index_in_dim(value, core, axis, keepdims=False),
            lax.dynamic_index_in_dim(value, 1 - core, axis, keepdims=False),
        )

    d_h_one = 0.0
    d_qkv = []
    for slot in range(slots):
        grads = [col_to(d_mixed[k, slot], k) for k in range(cols)]
        d_query, d_own, d_other = attention_backward(
            scalars, own_heads[slot], other_heads[slot], grads, forward[slot][1], forward[slot][2], limit, turns
        )
        d_keys = (d_own + row_swap(d_other).astype(f32)).astype(bf16)
        pieces = jnp.concatenate([d_query, d_keys], 1)
        back = jnp.stack([col_from(pieces[k], k) for k in range(cols)]).reshape(cols * 3 * HEAD, width)
        d_h_one = d_h_one + contract(back, w_slots[slot], 0, 0)
        grad = contract(back, h_one, 1, 0).astype(bf16).reshape(cols, 3, 2, HALF, 2 * part)
        mine, theirs = halves(grad, 2)
        lower, upper = scatter_pieces(
            mine.reshape(cols, 3 * HALF, 2 * part), theirs.reshape(cols, 3 * HALF, 2 * part), 2
        )
        d_qkv.append(
            jnp.stack([lower.reshape(3, HALF, part), upper.reshape(3, HALF, part)], 1).reshape(3 * HEAD, part)
        )
    d_qkv = jnp.concatenate(d_qkv, 0)

    d_input, sum_one, proj_one = norm_backward(d_h_one, normed_one, inv_one, gain_a, scale_attn)
    d_tokens = d_input + d_middle

    d_up = jnp.concatenate(scatter_pieces(d_up[:cols], d_up[cols:], 1), 1)
    d_down = jnp.concatenate(scatter_pieces(d_down[:cols], d_down[cols:], 2), 0)
    d_out_proj = jnp.concatenate(scatter_pieces(*halves(d_out, 1), 2), 0)

    def whole_rows(value):
        own, other = value[:, :part], row_swap(value[:, part:])
        return jnp.concatenate(in_order(row, own, other), 0)

    sums = jnp.stack(
        [
            sum_one,
            proj_one,
            jnp.sum(d_middle * attended, 0),
            sum_two,
            proj_two,
            jnp.sum(upstream * branch, 0),
            jnp.sum(d_branch.astype(f32), 0),
        ]
    )
    sums = sums[:, :part] + row_swap(sums[:, part:])
    for bit in range(bits("col")):
        sums = sums + col_swap(sums, bit)
    per_seq = jnp.stack(
        [
            sums[0],
            sums[1] * gain_attn,
            sums[2],
            sums[3],
            sums[4] * gain_mlp,
            sums[5],
            sums[1] * (1.0 + modulation[1]),
            sums[4] * (1.0 + modulation[4]),
            sums[6],
        ]
    )[None]
    conditions = condition[None]
    index = lax.axis_index("dp")
    for bit in range(bits("dp")):
        place = (index >> bit) % 2
        per_seq = jnp.concatenate(in_order(place, per_seq, dp_swap(per_seq, bit)), 0)
        conditions = jnp.concatenate(in_order(place, conditions, dp_swap(conditions, bit)), 0)
    d_mod_w = sum(conditions[s][:, None, None] * per_seq[s, :6][None] for s in range(per_seq.shape[0]))
    totals = jnp.sum(per_seq, 0)

    d_bias = d_bias.reshape(2, cols, d_bias.shape[-1])
    d_bias = jnp.stack(in_order(core, d_bias[0], d_bias[1]), 1)
    d_bias = d_bias + row_swap(d_bias)
    d_bias = sum(col_to(d_bias[k], k) for k in range(cols))
    for bit in range(bits("dp")):
        d_bias = d_bias + dp_swap(d_bias, bit)

    return (
        whole_rows(block_out),
        whole_rows(d_tokens),
        d_mod_w,
        totals[:6],
        totals[6],
        d_qkv,
        d_out_proj,
        totals[7],
        d_up,
        d_bias.reshape(-1),
        d_down,
        totals[8],
    )


def solution(mesh):
    blocks = P(("dp", "col"), "row")
    return jax.shard_map(
        shards,
        mesh=mesh,
        in_specs=(
            blocks,
            blocks,
            P("dp"),
            P("dp", None),
            P(None, None, "row"),
            P(None, "row"),
            P("row"),
            P("col", "row"),
            P("col", "row"),
            P("row"),
            P("row", "col"),
            P("col"),
            P("col", "row"),
            P("row"),
        ),
        out_specs=(
            blocks,
            blocks,
            P(None, None, "row"),
            P(None, "row"),
            P("row"),
            P("col", "row"),
            P("col", "row"),
            P("row"),
            P("row", "col"),
            P("col"),
            P("col", "row"),
            P("row"),
        ),
        check_vma=False,
    )
```

time: 1640 us -> 615 us (0.38)
  waiting for transfers between devices: 1170 us -> 182 us
  matrix products: 238 us -> 13.8 us
  starting transfers between devices: 1.89 us -> 211 us
  Pallas kernels: 0 us -> 108 us
  blocking collectives: 60.3 us -> 0 us
  other arithmetic: 106 us -> 57.1 us
    reduce_scatter x9 -> x0, waiting for transfers between devices: 685 us -> none  [the longest x4 338 us: into_heads(): lax.psum_scatter(partial_product(jnp.int32(0), share_rows * lax.axis_size...]
    all_gather x9 -> x0, waiting for transfers between devices: 409 us -> none  [the longest x4 191 us: into_stream(): gathered = lax.all_gather(activation, 'row', axis=0, tiled=True)]
    dot_general x34 -> x13, matrix products: 238 us -> 13.8 us  [the longest x12 13.4 us: contract(): lax.dot_general(first, second, (((first_axis,), (second_axis,)), ((), ())...]
    ppermute x0 -> x144, starting transfers between devices: none -> 211 us  [the longest x30 67.5 us: dp_swap(): lax.ppermute(value, 'dp', [(i, i ^ 1 << bit) for i in range(lax.axis_size...]
    ppermute x0 -> x144, waiting for transfers between devices: none -> 182 us  [the longest x34 67.4 us: row_swap(): return lax.ppermute(value, 'row', [(0, 1), (1, 0)])]
    pallas_call x0 -> x7, Pallas kernels: none -> 108 us  [the longest x3 46.4 us: attention_backward(): pl.pallas_call(functools.partial(backward_kernel, count), in_specs=[pl.Bl...]
    psum x1 -> x0, waiting for transfers between devices: 77.1 us -> none  [shards(): lax.psum((d_qkv, d_out_proj, d_up, d_down, d_mod_w, small_rows, d_up_bias...]
    psum x6 -> x0, blocking collectives: 60.3 us -> none  [the longest x1 26.1 us: blocked_layer(): row_slots, col_slots = lax.psum((row_slots, col_slots), ('row', 'col'))]
  transfers between devices with their start and end apart: 19 -> 144, of which waited for: 19 -> 45; matrix products, arithmetic and copies ran while one was open for 4% -> 15% of each run, Pallas kernels for 0% -> 14%
where the time goes in v1:
time: 615 us; the launch traced here: 605 us
  starting transfers between devices  211 us (34%)
  waiting for transfers between devices  182 us (30%)
  Pallas kernels  108 us (18%)
  other arithmetic  57.1 us (9%)
  local copies, waits for them, and re-layouts  29.2 us (5%)
  matrix products  13.8 us (2%)
    ppermute x30, starting transfers between devices, dp_swap(): lax.ppermute(value, 'dp', [(i, i ^ 1 << bit) for i in range(lax.axis_size...  67.5 us
    ppermute x34, waiting for transfers between devices, row_swap(): return lax.ppermute(value, 'row', [(0, 1), (1, 0)])  67.4 us
    ppermute x39, waiting for transfers between devices, col_from(): lax.ppermute(value, 'col', [(i, (i + hop) % size) for i in range(size)])  57.5 us
    ppermute x39, starting transfers between devices, col_to(): lax.ppermute(value, 'col', [(i, (i - hop) % size) for i in range(size)])  56.8 us
    pallas_call x3, Pallas kernels, attention_backward(): pl.pallas_call(functools.partial(backward_kernel, count), in_specs=[pl.Bl...  46.4 us
    ppermute x39, starting transfers between devices, col_from(): lax.ppermute(value, 'col', [(i, (i + hop) % size) for i in range(size)])  46 us
    pallas_call x3, Pallas kernels, attention_forward(): pl.pallas_call(functools.partial(forward_kernel, count), in_specs=[pl.Blo...  41 us
    ppermute x34, starting transfers between devices, row_swap(): return lax.ppermute(value, 'row', [(0, 1), (1, 0)])  38.8 us
  transfers between devices with their start and end apart: 144, of which 45 were waited for; matrix products, arithmetic and copies ran while one was open for 15% of the time, Pallas kernels for 14%

profile of v1, /device:TPU:9, one launch (start us, length us, event | category | flops | bytes accessed | tf_op | source)
XLA Modules:
  0.0 605.4 jit_solution(1081153485217098124)
XLA Ops:
  5.3 3.2 collective-permute-start.59
  32.3 2.6 collective-permute-start.33
  38.5 2.7 collective-permute-start.48
  42.4 3.2 collective-permute-start.53
  45.6 2.6 collective-permute-start.54
  54.4 20.4 %collective-permute-done.54 = bf16[384,384]{1,0:T(8,128)(2,1)S(1)} collective-permute-done((bf16[384,384]{1,0:T(8,128)(2,1)}, bf16[384,384]{1,0:T(8,128)(2,1)S(1)}, u32[]{:S(2)}, u32[]{:S(2)}) %collective-permute-start.54) | collective-permute-done | bytes 294944 | tf_op jit(solution)/shard_map/ppermute | solution.py:41
  75.1 11.4 %collective-permute-done.55 = bf16[384,384]{1,0:T(8,128)(2,1)S(1)} collective-permute-done((bf16[384,384]{1,0:T(8,128)(2,1)}, bf16[384,384]{1,0:T(8,128)(2,1)S(1)}, u32[]{:S(2)}, u32[]{:S(2)}) %collective-permute-start.55) | collective-permute-done | bytes 294944 | tf_op jit(solution)/shard_map/ppermute | solution.py:41
  87.4 8.2 %collective-permute-start.6 = (bf16[4,96,768]{2,1,0:T(8,128)(2,1)S(1)}, bf16[4,96,768]{2,1,0:T(8,128)(2,1)S(1)}, u32[]{:S(2)}, u32[]{:S(2)}) collective-permute-start(bf16[4,96,768]{2,1,0:T(8,128)(2,1)S(1)} %pad_maximum_fusion.16), channel_id=1, source_target_pairs={{0,8},{8,0},{16,24},{24,16},{1,9},{9,1},{17,25},{25,17},{2,10},{10... | collective-permute-start | bytes 1769480 | tf_op jit(solution)/shard_map/ppermute | solution.py:32
  101.1 2.8 collective-permute-start.21
  104.1 2.3 collective-permute-start.51
  112.1 2.7 collective-permute-start.8
  124.7 3.5 collective-permute-start.37
  128.2 5.4 collective-permute-done.9.refs_3_
  138.2 4.3 collective-permute-done.23.refs_2_
  142.5 2.4 collective-permute-start.10
  157.5 13.7 %attend.3 = (bf16[4,64,384]{2,1,0:T(8,128)(2,1)}, f32[4,64,384]{2,1,0:T(8,128)}, f32[4,1,384]{2,1,0:T(1,128)}) custom-call(s32[6]{0:T(128)} %pad_add_fusion.scalars, bf16[192,384]{1,0:T(8,128)(2,1)} %bitcast.476, bf16[192,384]{1,0:T(8,128)(2,1)} %copy-done.61, bf16[192,384]{1,0:T(8,128)(2,1)} %copy-done.63, bf16[192,384]{1,0:T(8,128)(2,1)} %copy-done.64, ...), custom_call_target="tpu_custom_call" | custom-call | flops 8000000000 | bytes 3000000 | tf_op jit(solution)/shard_map/attend/pallas_call | solution.py:220
  171.2 11.5 %collective-permute-done.25.refs_4_ = bf16[128,384]{1,0:T(8,128)(2,1)} collective-permute-done((bf16[128,384]{1,0:T(8,128)(2,1)}, bf16[128,384]{1,0:T(8,128)(2,1)}, u32[]{:S(2)}, u32[]{:S(2)}) %collective-permute-start.25) | collective-permute-done | bytes 98336 | tf_op jit(solution)/shard_map/ppermute | solution.py:28
  190.3 13.7 %attend.4 = (bf16[4,64,384]{2,1,0:T(8,128)(2,1)}, f32[4,64,384]{2,1,0:T(8,128)}, f32[4,1,384]{2,1,0:T(1,128)}) custom-call(s32[6]{0:T(128)} %pad_add_fusion.scalars, bf16[192,384]{1,0:T(8,128)(2,1)} %bitcast.474, bf16[192,384]{1,0:T(8,128)(2,1)} %copy-done.58, bf16[192,384]{1,0:T(8,128)(2,1)} %copy-done.65, bf16[192,384]{1,0:T(8,128)(2,1)} %copy-done.66, ...), custom_call_target="tpu_custom_call" | custom-call | flops 8000000000 | bytes 3000000 | tf_op jit(solution)/shard_map/attend/pallas_call | solution.py:220
  204.0 2.4 collective-permute-start.64
  208.4 2.4 collective-permute-start.15
  210.9 13.7 %attend.5 = (bf16[4,64,384]{2,1,0:T(8,128)(2,1)}, f32[4,64,384]{2,1,0:T(8,128)}, f32[4,1,384]{2,1,0:T(1,128)}) custom-call(s32[6]{0:T(128)} %pad_add_fusion.scalars, bf16[192,384]{1,0:T(8,128)(2,1)} %bitcast.472, bf16[192,384]{1,0:T(8,128)(2,1)} %copy-done.59, bf16[192,384]{1,0:T(8,128)(2,1)} %copy-done.60, bf16[192,384]{1,0:T(8,128)(2,1)} %copy-done.62, ...), custom_call_target="tpu_custom_call" | custom-call | flops 8000000000 | bytes 3000000 | tf_op jit(solution)/shard_map/attend/pallas_call | solution.py:220
  224.6 3.3 pad_maximum_fusion.2
  227.9 4.8 collective-permute-start.57
  235.1 2.5 collective-permute-start.29
  237.6 2.4 collective-permute-start.30
  253.9 4.0 pad_maximum_fusion.up_ref
  258.0 3.8 pad_maximum_fusion.1.down_ref
  261.7 20.7 %feed.1 = (f32[384,768]{1,0:T(8,128)}, f32[384,768]{1,0:T(8,128)}, bf16[8,768,384]{2,1,0:T(8,128)(2,1)}, bf16[8,384,768]{2,1,0:T(8,128)(2,1)}, f32[8,1,384]{2,1,0:T(1,128)}) custom-call(bf16[384,768]{1,0:T(8,128)(2,1)} %add_convert_fusion.5.h_ref, bf16[384,768]{1,0:T(8,128)(2,1)} %get-tuple-element.89.df_ref, bf16[8,768,384]{2,1,0:T(8,128)(2,1)} %pad_maximum_fusion.up_ref, ...), custom_call_target="tpu_custom_call" | custom-call | flops 10871635968 | bytes 24000000 | tf_op jit(solution)/shard_map/feed/pallas_call | solution.py:301
  286.8 2.4 fusion.16
  295.5 3.9 collective-permute-start.137
  315.6 15.5 %attend_back.3 = (bf16[4,64,384]{2,1,0:T(8,128)(2,1)}, f32[4,128,384]{2,1,0:T(8,128)}, bf16[4,128,384]{2,1,0:T(8,128)(2,1)}) custom-call(s32[6]{0:T(128)} %pad_add_fusion.scalars, bf16[192,384]{1,0:T(8,128)(2,1)} %bitcast.477, bf16[192,384]{1,0:T(8,128)(2,1)} %copy-done.61, bf16[192,384]{1,0:T(8,128)(2,1)} %copy-done.63, bf16[192,384]{1,0:T(8,128)(2,1)} %copy-done.64, ...), custom_call_target="tpu_custom_call" | custom-call | flops 16000000000 | bytes 4000000 | tf_op jit(solution)/shard_map/attend_back/pallas_call | solution.py:242
  334.6 15.4 %attend_back.4 = (bf16[4,64,384]{2,1,0:T(8,128)(2,1)}, f32[4,128,384]{2,1,0:T(8,128)}, bf16[4,128,384]{2,1,0:T(8,128)(2,1)}) custom-call(s32[6]{0:T(128)} %pad_add_fusion.scalars, bf16[192,384]{1,0:T(8,128)(2,1)} %bitcast.475, bf16[192,384]{1,0:T(8,128)(2,1)} %copy-done.58, bf16[192,384]{1,0:T(8,128)(2,1)} %copy-done.65, bf16[192,384]{1,0:T(8,128)(2,1)} %copy-done.66, ...), custom_call_target="tpu_custom_call" | custom-call | flops 16000000000 | bytes 4000000 | tf_op jit(solution)/shard_map/attend_back/pallas_call | solution.py:242
  350.0 3.4 collective-permute-start.66
  354.9 15.4 %attend_back.5 = (bf16[4,64,384]{2,1,0:T(8,128)(2,1)}, f32[4,128,384]{2,1,0:T(8,128)}, bf16[4,128,384]{2,1,0:T(8,128)(2,1)}) custom-call(s32[6]{0:T(128)} %pad_add_fusion.scalars, bf16[192,384]{1,0:T(8,128)(2,1)} %bitcast.473, bf16[192,384]{1,0:T(8,128)(2,1)} %copy-done.59, bf16[192,384]{1,0:T(8,128)(2,1)} %copy-done.60, bf16[192,384]{1,0:T(8,128)(2,1)} %copy-done.62, ...), custom_call_target="tpu_custom_call" | custom-call | flops 16000000000 | bytes 4000000 | tf_op jit(solution)/shard_map/attend_back/pallas_call | solution.py:242
  381.0 3.9 collective-permute-done.84
  387.6 3.0 collective-permute-start.72
  390.5 6.9 %collective-permute-done.80 = bf16[192,384]{1,0:T(8,128)(2,1)S(1)} collective-permute-done((bf16[192,384]{1,0:T(8,128)(2,1)S(1)}, bf16[192,384]{1,0:T(8,128)(2,1)S(1)}, u32[]{:S(2)}, u32[]{:S(2)}) %collective-permute-start.80) | collective-permute-done | bytes 147488 | tf_op jit(solution)/shard_map/ppermute | solution.py:41
  403.2 8.2 %collective-permute-done.73 = bf16[192,384]{1,0:T(8,128)(2,1)S(1)} collective-permute-done((bf16[192,384]{1,0:T(8,128)(2,1)S(1)}, bf16[192,384]{1,0:T(8,128)(2,1)S(1)}, u32[]{:S(2)}, u32[]{:S(2)}) %collective-permute-start.73) | collective-permute-done | bytes 147488 | tf_op jit(solution)/shard_map/ppermute | solution.py:41
  414.4 3.6 collective-permute-start.96
  429.9 4.6 collective-permute-start.94
  436.0 2.4 collective-permute-done.95
  443.0 5.6 collective-permute-start.103
  459.1 10.9 %collective-permute-done.88 = f32[384,384]{1,0:T(8,128)S(1)} collective-permute-done((f32[384,384]{1,0:T(8,128)S(1)}, f32[384,384]{1,0:T(8,128)S(1)}, u32[]{:S(2)}, u32[]{:S(2)}) %collective-permute-start.88) | collective-permute-done | bytes 589856 | tf_op jit(solution)/shard_map/ppermute | solution.py:28
  471.9 4.4 collective-permute-done.97
  477.8 4.8 collective-permute-done.104
  482.6 2.7 collective-permute-start.98
  485.5 3.5 collective-permute-done.111
  491.9 2.4 collective-permute-start.106
  494.2 3.1 collective-permute-done.99
  502.4 3.5 collective-permute-start.113
  508.1 2.8 collective-permute-start.123
  513.3 2.5 collective-permute-done.101
  515.8 2.4 collective-permute-start.102
  519.0 3.1 collective-permute-done.115
  522.1 5.0 collective-permute-done.138
  527.5 3.4 collective-permute-start.139
  533.3 19.1 %collective-permute-done.125 = bf16[4,384,384]{2,1,0:T(8,128)(2,1)S(1)} collective-permute-done((bf16[4,384,384]{2,1,0:T(8,128)(2,1)S(1)}, bf16[4,384,384]{2,1,0:T(8,128)(2,1)S(1)}, u32[]{:S(2)}, u32[]{:S(2)}) %collective-permute-start.125) | collective-permute-done | bytes 1179680 | tf_op jit(solution)/shard_map/ppermute | solution.py:28
  552.8 3.4 collective-permute-start.126
  558.6 3.7 collective-permute-start.109
  562.6 13.3 %collective-permute-done.127 = bf16[384,384]{1,0:T(8,128)(2,1)S(1)} collective-permute-done((bf16[384,384]{1,0:T(8,128)(2,1)S(1)}, bf16[384,384]{1,0:T(8,128)(2,1)S(1)}, u32[]{:S(2)}, u32[]{:S(2)}) %collective-permute-start.127) | collective-permute-done | bytes 294944 | tf_op jit(solution)/shard_map/ppermute | solution.py:46
  575.9 6.3 %collective-permute-done.128 = bf16[384,384]{1,0:T(8,128)(2,1)S(1)} collective-permute-done((bf16[384,384]{1,0:T(8,128)(2,1)S(1)}, bf16[384,384]{1,0:T(8,128)(2,1)S(1)}, u32[]{:S(2)}, u32[]{:S(2)}) %collective-permute-start.128) | collective-permute-done | bytes 294944 | tf_op jit(solution)/shard_map/ppermute | solution.py:46
  582.6 9.3 %collective-permute-start.143 = (f32[384,384]{1,0:T(8,128)S(1)}, f32[384,384]{1,0:T(8,128)S(1)}, u32[]{:S(2)}, u32[]{:S(2)}) collective-permute-start(f32[384,384]{1,0:T(8,128)S(1)} %add.509), channel_id=1, source_target_pairs={{0,8},{8,0},{16,24},{24,16},{1,9},{9,1},{17,25},{25,17},{2,10},{10... | collective-permute-start | bytes 1769480 | tf_op jit(solution)/shard_map/ppermute | solution.py:32
  592.0 5.8 collective-permute-done.129
  597.8 3.6 collective-permute-start.130
  (735 shorter events, 210.9 us)
Async XLA Ops:
  1.9 28.9 %collective-permute-start.17 = (bf16[96,384]{1,0:T(8,128)(2,1)S(1)}, bf16[96,384]{1,0:T(8,128)(2,1)S(1)}, u32[]{:S(2)}, u32[]{:S(2)}) collective-permute-start(bf16[96,384]{1,0:T(8,128)(2,1)S(1)} %bitcast.398), channel_id=1, source_target_pairs={{0,1},{1,2},{2,3},{3,0},{4,5},{5,6},{6,7},{7,4},{8,9},{9,10},{10,1... | collective-permute-start | bytes 221192 | tf_op jit(solution)/shard_map/ppermute | solution.py:41
  3.3 29.0 %collective-permute-start.18 = (bf16[96,384]{1,0:T(8,128)(2,1)S(1)}, bf16[96,384]{1,0:T(8,128)(2,1)S(1)}, u32[]{:S(2)}, u32[]{:S(2)}) collective-permute-start(bf16[96,384]{1,0:T(8,128)(2,1)S(1)} %bitcast.399), channel_id=1, source_target_pairs={{0,2},{1,3},{2,0},{3,1},{4,6},{5,7},{6,4},{7,5},{8,10},{9,11},{10,... | collective-permute-start | bytes 221192 | tf_op jit(solution)/shard_map/ppermute | solution.py:41
  5.1 19.2 %collective-permute-start.58 = (bf16[1,768]{1,0:T(2,128)(2,1)S(1)}, bf16[1,768]{1,0:T(2,128)(2,1)S(1)}, u32[]{:S(2)}, u32[]{:S(2)}) collective-permute-start(bf16[1,768]{1,0:T(2,128)(2,1)S(1)} %broadcast_in_dim.33), channel_id=1, source_target_pairs={{0,1},{1,2},{2,3},{3,0},{4,5},{5,6},{6,7},{7,4},{8,9},{9,10},{10,1... | collective-permute-start | bytes 4616 | tf_op jit(solution)/shard_map/ppermute | solution.py:41
  5.3 19.9 %collective-permute-start.59 = (bf16[1,768]{1,0:T(2,128)(2,1)S(1)}, bf16[1,768]{1,0:T(2,128)(2,1)S(1)}, u32[]{:S(2)}, u32[]{:S(2)}) collective-permute-start(bf16[1,768]{1,0:T(2,128)(2,1)S(1)} %broadcast_in_dim.33), channel_id=1, source_target_pairs={{0,2},{1,3},{2,0},{3,1},{4,6},{5,7},{6,4},{7,5},{8,10},{9,11},{10,... | collective-permute-start | bytes 4616 | tf_op jit(solution)/shard_map/ppermute | solution.py:41
  45.6 29.3 %collective-permute-start.54 = (bf16[384,384]{1,0:T(8,128)(2,1)}, bf16[384,384]{1,0:T(8,128)(2,1)S(1)}, u32[]{:S(2)}, u32[]{:S(2)}) collective-permute-start(bf16[384,384]{1,0:T(8,128)(2,1)} %constant_dynamic-slice_fusion.9), channel_id=1, source_target_pairs={{0,2},{1,3},{2,0},{3,1},{4,6},{5,7},{6,4},{7,5},{8,10},{9,11},{10,... | collective-permute-start | bytes 884744 | tf_op jit(solution)/shard_map/ppermute | solution.py:41
  48.2 38.3 %collective-permute-start.55 = (bf16[384,384]{1,0:T(8,128)(2,1)}, bf16[384,384]{1,0:T(8,128)(2,1)S(1)}, u32[]{:S(2)}, u32[]{:S(2)}) collective-permute-start(bf16[384,384]{1,0:T(8,128)(2,1)} %constant_dynamic-slice_fusion.9), channel_id=1, source_target_pairs={{0,3},{1,0},{2,1},{3,2},{4,7},{5,4},{6,5},{7,6},{8,11},{9,8},{10,9... | collective-permute-start | bytes 884744 | tf_op jit(solution)/shard_map/ppermute | solution.py:41
  48.3 39.1 %collective-permute-start.61 = (bf16[384,384]{1,0:T(8,128)(2,1)S(1)}, bf16[384,384]{1,0:T(8,128)(2,1)S(1)}, u32[]{:S(2)}, u32[]{:S(2)}) collective-permute-start(bf16[384,384]{1,0:T(8,128)(2,1)S(1)} %copy-done.47), channel_id=1, source_target_pairs={{0,1},{1,2},{2,3},{3,0},{4,5},{5,6},{6,7},{7,4},{8,9},{9,10},{10,1... | collective-permute-start | bytes 884744 | tf_op jit(solution)/shard_map/ppermute | solution.py:41
  50.0 24.9 %collective-permute-start.5 = (bf16[4,96,384]{2,1,0:T(8,128)(2,1)S(1)}, bf16[4,96,384]{2,1,0:T(8,128)(2,1)S(1)}, u32[]{:S(2)}, u32[]{:S(2)}) collective-permute-start(bf16[4,96,384]{2,1,0:T(8,128)(2,1)S(1)} %pad_maximum_fusion.29), channel_id=1, source_target_pairs={{0,4},{4,0},{1,5},{5,1},{2,6},{6,2},{3,7},{7,3},{8,12},{12,8},{9,1... | collective-permute-start | bytes 884744 | tf_op jit(solution)/shard_map/ppermute | solution.py:28
  54.4 42.5 %collective-permute-start.62 = (bf16[384,384]{1,0:T(8,128)(2,1)S(1)}, bf16[384,384]{1,0:T(8,128)(2,1)S(1)}, u32[]{:S(2)}, u32[]{:S(2)}) collective-permute-start(bf16[384,384]{1,0:T(8,128)(2,1)S(1)} %copy-done.47), channel_id=1, source_target_pairs={{0,2},{1,3},{2,0},{3,1},{4,6},{5,7},{6,4},{7,5},{8,10},{9,11},{10,... | collective-permute-start | bytes 884744 | tf_op jit(solution)/shard_map/ppermute | solution.py:41
  74.9 24.3 %collective-permute-start.63 = (bf16[384,384]{1,0:T(8,128)(2,1)S(1)}, bf16[384,384]{1,0:T(8,128)(2,1)S(1)}, u32[]{:S(2)}, u32[]{:S(2)}) collective-permute-start(bf16[384,384]{1,0:T(8,128)(2,1)S(1)} %copy-done.47), channel_id=1, source_target_pairs={{0,3},{1,0},{2,1},{3,2},{4,7},{5,4},{6,5},{7,6},{8,11},{9,8},{10,9... | collective-permute-start | bytes 884744 | tf_op jit(solution)/shard_map/ppermute | solution.py:41
  74.9 26.1 %collective-permute-start.20 = (bf16[4,96,384]{2,1,0:T(8,128)(2,1)S(1)}, bf16[4,96,384]{2,1,0:T(8,128)(2,1)S(1)}, u32[]{:S(2)}, u32[]{:S(2)}) collective-permute-start(bf16[4,96,384]{2,1,0:T(8,128)(2,1)S(1)} %pad_maximum_fusion.30), channel_id=1, source_target_pairs={{0,4},{4,0},{1,5},{5,1},{2,6},{6,2},{3,7},{7,3},{8,12},{12,8},{9,1... | collective-permute-start | bytes 884744 | tf_op jit(solution)/shard_map/ppermute | solution.py:28
  86.5 17.4 %collective-permute-start.35 = (bf16[4,96,384]{2,1,0:T(8,128)(2,1)S(1)}, bf16[4,96,384]{2,1,0:T(8,128)(2,1)S(1)}, u32[]{:S(2)}, u32[]{:S(2)}) collective-permute-start(bf16[4,96,384]{2,1,0:T(8,128)(2,1)S(1)} %pad_maximum_fusion.31), channel_id=1, source_target_pairs={{0,4},{4,0},{1,5},{5,1},{2,6},{6,2},{3,7},{7,3},{8,12},{12,8},{9,1... | collective-permute-start | bytes 884744 | tf_op jit(solution)/shard_map/ppermute | solution.py:28
  87.4 19.1 %collective-permute-start.6 = (bf16[4,96,768]{2,1,0:T(8,128)(2,1)S(1)}, bf16[4,96,768]{2,1,0:T(8,128)(2,1)S(1)}, u32[]{:S(2)}, u32[]{:S(2)}) collective-permute-start(bf16[4,96,768]{2,1,0:T(8,128)(2,1)S(1)} %pad_maximum_fusion.16), channel_id=1, source_target_pairs={{0,8},{8,0},{16,24},{24,16},{1,9},{9,1},{17,25},{25,17},{2,10},{10... | collective-permute-start | bytes 1769480 | tf_op jit(solution)/shard_map/ppermute | solution.py:32
  114.8 18.8 %collective-permute-start.9 = (bf16[192,384]{1,0:T(8,128)(2,1)S(1)}, bf16[192,384]{1,0:T(8,128)(2,1)S(1)}, u32[]{:S(2)}, u32[]{:S(2)}) collective-permute-start(bf16[192,384]{1,0:T(8,128)(2,1)S(1)} %bitcast.483), channel_id=1, source_target_pairs={{0,1},{1,2},{2,3},{3,0},{4,5},{5,6},{6,7},{7,4},{8,9},{9,10},{10,1... | collective-permute-start | bytes 442376 | tf_op jit(solution)/shard_map/ppermute | solution.py:46
  118.0 18.6 %collective-permute-start.22 = (bf16[192,384]{1,0:T(8,128)(2,1)S(1)}, bf16[192,384]{1,0:T(8,128)(2,1)S(1)}, u32[]{:S(2)}, u32[]{:S(2)}) collective-permute-start(bf16[192,384]{1,0:T(8,128)(2,1)S(1)} %bitcast.485), channel_id=1, source_target_pairs={{0,3},{1,0},{2,1},{3,2},{4,7},{5,4},{6,5},{7,6},{8,11},{9,8},{10,9... | collective-permute-start | bytes 442376 | tf_op jit(solution)/shard_map/ppermute | solution.py:46
  121.4 21.1 %collective-permute-start.23 = (bf16[192,384]{1,0:T(8,128)(2,1)S(1)}, bf16[192,384]{1,0:T(8,128)(2,1)S(1)}, u32[]{:S(2)}, u32[]{:S(2)}) collective-permute-start(bf16[192,384]{1,0:T(8,128)(2,1)S(1)} %bitcast.482), channel_id=1, source_target_pairs={{0,2},{1,3},{2,0},{3,1},{4,6},{5,7},{6,4},{7,5},{8,10},{9,11},{10,... | collective-permute-start | bytes 442376 | tf_op jit(solution)/shard_map/ppermute | solution.py:46
  122.6 23.7 %collective-permute-start.24 = (bf16[192,384]{1,0:T(8,128)(2,1)S(1)}, bf16[192,384]{1,0:T(8,128)(2,1)S(1)}, u32[]{:S(2)}, u32[]{:S(2)}) collective-permute-start(bf16[192,384]{1,0:T(8,128)(2,1)S(1)} %bitcast.480), channel_id=1, source_target_pairs={{0,1},{1,2},{2,3},{3,0},{4,5},{5,6},{6,7},{7,4},{8,9},{9,10},{10,1... | collective-permute-start | bytes 442376 | tf_op jit(solution)/shard_map/ppermute | solution.py:46
  124.7 24.5 %collective-permute-start.37 = (bf16[192,384]{1,0:T(8,128)(2,1)S(1)}, bf16[192,384]{1,0:T(8,128)(2,1)S(1)}, u32[]{:S(2)}, u32[]{:S(2)}) collective-permute-start(bf16[192,384]{1,0:T(8,128)(2,1)S(1)} %bitcast.481), channel_id=1, source_target_pairs={{0,3},{1,0},{2,1},{3,2},{4,7},{5,4},{6,5},{7,6},{8,11},{9,8},{10,9... | collective-permute-start | bytes 442376 | tf_op jit(solution)/shard_map/ppermute | solution.py:46
  133.6 17.0 %collective-permute-start.38 = (bf16[192,384]{1,0:T(8,128)(2,1)S(1)}, bf16[192,384]{1,0:T(8,128)(2,1)S(1)}, u32[]{:S(2)}, u32[]{:S(2)}) collective-permute-start(bf16[192,384]{1,0:T(8,128)(2,1)S(1)} %bitcast.479), channel_id=1, source_target_pairs={{0,2},{1,3},{2,0},{3,1},{4,6},{5,7},{6,4},{7,5},{8,10},{9,11},{10,... | collective-permute-start | bytes 442376 | tf_op jit(solution)/shard_map/ppermute | solution.py:46
  136.5 16.3 %collective-permute-start.39 = (bf16[192,384]{1,0:T(8,128)(2,1)S(1)}, bf16[192,384]{1,0:T(8,128)(2,1)S(1)}, u32[]{:S(2)}, u32[]{:S(2)}) collective-permute-start(bf16[192,384]{1,0:T(8,128)(2,1)S(1)} %bitcast.478), channel_id=1, source_target_pairs={{0,1},{1,2},{2,3},{3,0},{4,5},{5,6},{6,7},{7,4},{8,9},{9,10},{10,1... | collective-permute-start | bytes 442376 | tf_op jit(solution)/shard_map/ppermute | solution.py:46
  152.8 71.8 %collective-permute-start.56 = (bf16[4,384,384]{2,1,0:T(8,128)(2,1)}, bf16[4,384,384]{2,1,0:T(8,128)(2,1)}, u32[]{:S(2)}, u32[]{:S(2)}) collective-permute-start(bf16[4,384,384]{2,1,0:T(8,128)(2,1)} %pad_maximum_fusion.8), channel_id=1, source_target_pairs={{0,4},{4,0},{1,5},{5,1},{2,6},{6,2},{3,7},{7,3},{8,12},{12,8},{9,1... | collective-permute-start | bytes 3538952 | tf_op jit(solution)/shard_map/ppermute | solution.py:28
  154.5 28.2 %collective-permute-start.25 = (bf16[128,384]{1,0:T(8,128)(2,1)}, bf16[128,384]{1,0:T(8,128)(2,1)}, u32[]{:S(2)}, u32[]{:S(2)}) collective-permute-start(bf16[128,384]{1,0:T(8,128)(2,1)} %slice_bitcast_fusion.9), channel_id=1, source_target_pairs={{0,4},{4,0},{1,5},{5,1},{2,6},{6,2},{3,7},{7,3},{8,12},{12,8},{9,1... | collective-permute-start | bytes 294920 | tf_op jit(solution)/shard_map/ppermute | solution.py:28
  154.6 30.2 %collective-permute-start.26 = (bf16[128,384]{1,0:T(8,128)(2,1)}, bf16[128,384]{1,0:T(8,128)(2,1)}, u32[]{:S(2)}, u32[]{:S(2)}) collective-permute-start(bf16[128,384]{1,0:T(8,128)(2,1)} %slice.634), channel_id=1, source_target_pairs={{0,4},{4,0},{1,5},{5,1},{2,6},{6,2},{3,7},{7,3},{8,12},{12,8},{9,1... | collective-permute-start | bytes 294920 | tf_op jit(solution)/shard_map/ppermute | solution.py:28
  156.0 30.9 %collective-permute-start.27 = (bf16[128,384]{1,0:T(8,128)(2,1)}, bf16[128,384]{1,0:T(8,128)(2,1)S(1)}, u32[]{:S(2)}, u32[]{:S(2)}) collective-permute-start(bf16[128,384]{1,0:T(8,128)(2,1)} %slice.635), channel_id=1, source_target_pairs={{0,4},{4,0},{1,5},{5,1},{2,6},{6,2},{3,7},{7,3},{8,12},{12,8},{9,1... | collective-permute-start | bytes 294920 | tf_op jit(solution)/shard_map/ppermute | solution.py:28
  156.1 32.8 %collective-permute-start.28 = (bf16[128,384]{1,0:T(8,128)(2,1)S(1)}, bf16[128,384]{1,0:T(8,128)(2,1)S(1)}, u32[]{:S(2)}, u32[]{:S(2)}) collective-permute-start(bf16[128,384]{1,0:T(8,128)(2,1)S(1)} %slice.636), channel_id=1, source_target_pairs={{0,4},{4,0},{1,5},{5,1},{2,6},{6,2},{3,7},{7,3},{8,12},{12,8},{9,1... | collective-permute-start | bytes 294920 | tf_op jit(solution)/shard_map/ppermute | solution.py:28
  182.7 21.3 %collective-permute-start.40 = (bf16[128,384]{1,0:T(8,128)(2,1)S(1)}, bf16[128,384]{1,0:T(8,128)(2,1)}, u32[]{:S(2)}, u32[]{:S(2)}) collective-permute-start(bf16[128,384]{1,0:T(8,128)(2,1)S(1)} %copy-done.55), channel_id=1, source_target_pairs={{0,4},{4,0},{1,5},{5,1},{2,6},{6,2},{3,7},{7,3},{8,12},{12,8},{9,1... | collective-permute-start | bytes 294920 | tf_op jit(solution)/shard_map/ppermute | solution.py:28
  184.8 21.6 %collective-permute-start.41 = (bf16[128,384]{1,0:T(8,128)(2,1)S(1)}, bf16[128,384]{1,0:T(8,128)(2,1)}, u32[]{:S(2)}, u32[]{:S(2)}) collective-permute-start(bf16[128,384]{1,0:T(8,128)(2,1)S(1)} %slice.645), channel_id=1, source_target_pairs={{0,4},{4,0},{1,5},{5,1},{2,6},{6,2},{3,7},{7,3},{8,12},{12,8},{9,1... | collective-permute-start | bytes 294920 | tf_op jit(solution)/shard_map/ppermute | solution.py:28
  186.9 21.5 %collective-permute-start.42 = (bf16[128,384]{1,0:T(8,128)(2,1)S(1)}, bf16[128,384]{1,0:T(8,128)(2,1)}, u32[]{:S(2)}, u32[]{:S(2)}) collective-permute-start(bf16[128,384]{1,0:T(8,128)(2,1)S(1)} %slice.646), channel_id=1, source_target_pairs={{0,4},{4,0},{1,5},{5,1},{2,6},{6,2},{3,7},{7,3},{8,12},{12,8},{9,1... | collective-permute-start | bytes 294920 | tf_op jit(solution)/shard_map/ppermute | solution.py:28
  188.9 21.9 %collective-permute-start.43 = (bf16[128,384]{1,0:T(8,128)(2,1)S(1)}, bf16[128,384]{1,0:T(8,128)(2,1)}, u32[]{:S(2)}, u32[]{:S(2)}) collective-permute-start(bf16[128,384]{1,0:T(8,128)(2,1)S(1)} %slice.647), channel_id=1, source_target_pairs={{0,4},{4,0},{1,5},{5,1},{2,6},{6,2},{3,7},{7,3},{8,12},{12,8},{9,1... | collective-permute-start | bytes 294920 | tf_op jit(solution)/shard_map/ppermute | solution.py:28
  204.0 28.8 %collective-permute-start.64 = (bf16[4,384,384]{2,1,0:T(8,128)(2,1)}, bf16[4,384,384]{2,1,0:T(8,128)(2,1)}, u32[]{:S(2)}, u32[]{:S(2)}) collective-permute-start(bf16[4,384,384]{2,1,0:T(8,128)(2,1)} %pad_maximum_fusion.9), channel_id=1, source_target_pairs={{0,4},{4,0},{1,5},{5,1},{2,6},{6,2},{3,7},{7,3},{8,12},{12,8},{9,1... | collective-permute-start | bytes 3538952 | tf_op jit(solution)/shard_map/ppermute | solution.py:28
  206.4 28.7 %collective-permute-start.14 = (bf16[64,384]{1,0:T(8,128)(2,1)S(1)}, bf16[64,384]{1,0:T(8,128)(2,1)S(1)}, u32[]{:S(2)}, u32[]{:S(2)}) collective-permute-start(bf16[64,384]{1,0:T(8,128)(2,1)S(1)} %get-tuple-element.198), channel_id=1, source_target_pairs={{0,1},{1,2},{2,3},{3,0},{4,5},{5,6},{6,7},{7,4},{8,9},{9,10},{10,1... | collective-permute-start | bytes 147464 | tf_op jit(solution)/shard_map/ppermute | solution.py:41
  208.4 29.2 %collective-permute-start.15 = (bf16[64,384]{1,0:T(8,128)(2,1)S(1)}, bf16[64,384]{1,0:T(8,128)(2,1)}, u32[]{:S(2)}, u32[]{:S(2)}) collective-permute-start(bf16[64,384]{1,0:T(8,128)(2,1)S(1)} %get-tuple-element.197), channel_id=1, source_target_pairs={{0,2},{1,3},{2,0},{3,1},{4,6},{5,7},{6,4},{7,5},{8,10},{9,11},{10,... | collective-permute-start | bytes 147464 | tf_op jit(solution)/shard_map/ppermute | solution.py:41
  210.9 29.2 %collective-permute-start.16 = (bf16[64,384]{1,0:T(8,128)(2,1)S(1)}, bf16[64,384]{1,0:T(8,128)(2,1)S(1)}, u32[]{:S(2)}, u32[]{:S(2)}) collective-permute-start(bf16[64,384]{1,0:T(8,128)(2,1)S(1)} %get-tuple-element.196), channel_id=1, source_target_pairs={{0,3},{1,0},{2,1},{3,2},{4,7},{5,4},{6,5},{7,6},{8,11},{9,8},{10,9... | collective-permute-start | bytes 147464 | tf_op jit(solution)/shard_map/ppermute | solution.py:41
  227.9 26.0 %collective-permute-start.57 = (bf16[4,768,384]{2,1,0:T(8,128)(2,1)S(1)}, bf16[4,768,384]{2,1,0:T(8,128)(2,1)S(1)}, u32[]{:S(2)}, u32[]{:S(2)}) collective-permute-start(bf16[4,768,384]{2,1,0:T(8,128)(2,1)S(1)} %pad_maximum_fusion.2), channel_id=1, source_target_pairs={{0,8},{8,0},{16,24},{24,16},{1,9},{9,1},{17,25},{25,17},{2,10},{10... | collective-permute-start | bytes 7077896 | tf_op jit(solution)/shard_map/ppermute | solution.py:32
  234.2 23.7 %collective-permute-start.65 = (bf16[4,384,768]{2,1,0:T(8,128)(2,1)S(1)}, bf16[4,384,768]{2,1,0:T(8,128)(2,1)S(1)}, u32[]{:S(2)}, u32[]{:S(2)}) collective-permute-start(bf16[4,384,768]{2,1,0:T(8,128)(2,1)S(1)} %pad_maximum_fusion.3), channel_id=1, source_target_pairs={{0,8},{8,0},{16,24},{24,16},{1,9},{9,1},{17,25},{25,17},{2,10},{10... | collective-permute-start | bytes 7077896 | tf_op jit(solution)/shard_map/ppermute | solution.py:32
  295.5 201.9 %collective-permute-start.137 = (bf16[4,384,768]{2,1,0:T(8,128)(2,1)}, bf16[4,384,768]{2,1,0:T(8,128)(2,1)}, u32[]{:S(2)}, u32[]{:S(2)}) collective-permute-start(bf16[4,384,768]{2,1,0:T(8,128)(2,1)} %slice.607), channel_id=1, source_target_pairs={{0,8},{8,0},{16,24},{24,16},{1,9},{9,1},{17,25},{25,17},{2,10},{10... | collective-permute-start | bytes 7077896 | tf_op jit(solution)/shard_map/ppermute | solution.py:32
  310.0 88.4 %collective-permute-start.117 = (bf16[4,96,768]{2,1,0:T(8,128)(2,1)S(1)}, bf16[4,96,768]{2,1,0:T(8,128)(2,1)}, u32[]{:S(2)}, u32[]{:S(2)}) collective-permute-start(bf16[4,96,768]{2,1,0:T(8,128)(2,1)S(1)} %dynamic-slice_bitcast_fusion), channel_id=1, source_target_pairs={{0,8},{8,0},{16,24},{24,16},{1,9},{9,1},{17,25},{25,17},{2,10},{10... | collective-permute-start | bytes 1769480 | tf_op jit(solution)/shard_map/ppermute | solution.py:32
  311.6 19.5 %collective-permute-start.74 = (bf16[64,384]{1,0:T(8,128)(2,1)S(1)}, bf16[64,384]{1,0:T(8,128)(2,1)S(1)}, u32[]{:S(2)}, u32[]{:S(2)}) collective-permute-start(bf16[64,384]{1,0:T(8,128)(2,1)S(1)} %get-tuple-element.142), channel_id=1, source_target_pairs={{0,3},{1,0},{2,1},{3,2},{4,7},{5,4},{6,5},{7,6},{8,11},{9,8},{10,9... | collective-permute-start | bytes 147464 | tf_op jit(solution)/shard_map/ppermute | solution.py:46
  311.7 19.6 %collective-permute-start.75 = (bf16[64,384]{1,0:T(8,128)(2,1)S(1)}, bf16[64,384]{1,0:T(8,128)(2,1)S(1)}, u32[]{:S(2)}, u32[]{:S(2)}) collective-permute-start(bf16[64,384]{1,0:T(8,128)(2,1)S(1)} %get-tuple-element.141), channel_id=1, source_target_pairs={{0,2},{1,3},{2,0},{3,1},{4,6},{5,7},{6,4},{7,5},{8,10},{9,11},{10,... | collective-permute-start | bytes 147464 | tf_op jit(solution)/shard_map/ppermute | solution.py:46
  313.3 19.1 %collective-permute-start.76 = (bf16[64,384]{1,0:T(8,128)(2,1)S(1)}, bf16[64,384]{1,0:T(8,128)(2,1)S(1)}, u32[]{:S(2)}, u32[]{:S(2)}) collective-permute-start(bf16[64,384]{1,0:T(8,128)(2,1)S(1)} %get-tuple-element.140), channel_id=1, source_target_pairs={{0,1},{1,2},{2,3},{3,0},{4,5},{5,6},{6,7},{7,4},{8,9},{9,10},{10,1... | collective-permute-start | bytes 147464 | tf_op jit(solution)/shard_map/ppermute | solution.py:46
  331.2 18.8 %collective-permute-start.81 = (bf16[64,384]{1,0:T(8,128)(2,1)S(1)}, bf16[64,384]{1,0:T(8,128)(2,1)S(1)}, u32[]{:S(2)}, u32[]{:S(2)}) collective-permute-start(bf16[64,384]{1,0:T(8,128)(2,1)S(1)} %get-tuple-element.138), channel_id=1, source_target_pairs={{0,3},{1,0},{2,1},{3,2},{4,7},{5,4},{6,5},{7,6},{8,11},{9,8},{10,9... | collective-permute-start | bytes 147464 | tf_op jit(solution)/shard_map/ppermute | solution.py:46
  331.3 22.2 %collective-permute-start.82 = (bf16[64,384]{1,0:T(8,128)(2,1)S(1)}, bf16[64,384]{1,0:T(8,128)(2,1)S(1)}, u32[]{:S(2)}, u32[]{:S(2)}) collective-permute-start(bf16[64,384]{1,0:T(8,128)(2,1)S(1)} %get-tuple-element.137), channel_id=1, source_target_pairs={{0,2},{1,3},{2,0},{3,1},{4,6},{5,7},{6,4},{7,5},{8,10},{9,11},{10,... | collective-permute-start | bytes 147464 | tf_op jit(solution)/shard_map/ppermute | solution.py:46
  332.5 21.1 %collective-permute-start.83 = (bf16[64,384]{1,0:T(8,128)(2,1)S(1)}, bf16[64,384]{1,0:T(8,128)(2,1)S(1)}, u32[]{:S(2)}, u32[]{:S(2)}) collective-permute-start(bf16[64,384]{1,0:T(8,128)(2,1)S(1)} %get-tuple-element.136), channel_id=1, source_target_pairs={{0,1},{1,2},{2,3},{3,0},{4,5},{5,6},{6,7},{7,4},{8,9},{9,10},{10,1... | collective-permute-start | bytes 147464 | tf_op jit(solution)/shard_map/ppermute | solution.py:46
  350.0 20.3 %collective-permute-start.66 = (bf16[384,384]{1,0:T(8,128)(2,1)}, bf16[384,384]{1,0:T(8,128)(2,1)}, u32[]{:S(2)}, u32[]{:S(2)}) collective-permute-start(bf16[384,384]{1,0:T(8,128)(2,1)} %slice.649), channel_id=1, source_target_pairs={{0,4},{4,0},{1,5},{5,1},{2,6},{6,2},{3,7},{7,3},{8,12},{12,8},{9,1... | collective-permute-start | bytes 884744 | tf_op jit(solution)/shard_map/ppermute | solution.py:28
  353.4 25.3 %collective-permute-start.70 = (bf16[4,128,384]{2,1,0:T(8,128)(2,1)}, bf16[4,128,384]{2,1,0:T(8,128)(2,1)}, u32[]{:S(2)}, u32[]{:S(2)}) collective-permute-start(bf16[4,128,384]{2,1,0:T(8,128)(2,1)} %get-tuple-element.44), channel_id=1, source_target_pairs={{0,4},{4,0},{1,5},{5,1},{2,6},{6,2},{3,7},{7,3},{8,12},{12,8},{9,1... | collective-permute-start | bytes 1179656 | tf_op jit(solution)/shard_map/ppermute | solution.py:28
  353.5 23.0 %collective-permute-start.77 = (bf16[4,128,384]{2,1,0:T(8,128)(2,1)}, bf16[4,128,384]{2,1,0:T(8,128)(2,1)}, u32[]{:S(2)}, u32[]{:S(2)}) collective-permute-start(bf16[4,128,384]{2,1,0:T(8,128)(2,1)} %get-tuple-element.49), channel_id=1, source_target_pairs={{0,4},{4,0},{1,5},{5,1},{2,6},{6,2},{3,7},{7,3},{8,12},{12,8},{9,1... | collective-permute-start | bytes 1179656 | tf_op jit(solution)/shard_map/ppermute | solution.py:28
  411.3 27.1 %collective-permute-start.118 = (bf16[4,96,384]{2,1,0:T(8,128)(2,1)}, bf16[4,96,384]{2,1,0:T(8,128)(2,1)}, u32[]{:S(2)}, u32[]{:S(2)}) collective-permute-start(bf16[4,96,384]{2,1,0:T(8,128)(2,1)} %split.55), channel_id=1, source_target_pairs={{0,4},{4,0},{1,5},{5,1},{2,6},{6,2},{3,7},{7,3},{8,12},{12,8},{9,1... | collective-permute-start | bytes 884744 | tf_op jit(solution)/shard_map/ppermute | solution.py:28
  414.4 40.6 %collective-permute-start.96 = (bf16[4,96,768]{2,1,0:T(8,128)(2,1)}, bf16[4,96,768]{2,1,0:T(8,128)(2,1)}, u32[]{:S(2)}, u32[]{:S(2)}) collective-permute-start(bf16[4,96,768]{2,1,0:T(8,128)(2,1)} %bitcast.144), channel_id=1, source_target_pairs={{0,8},{8,0},{16,24},{24,16},{1,9},{9,1},{17,25},{25,17},{2,10},{10... | collective-permute-start | bytes 1769480 | tf_op jit(solution)/shard_map/ppermute | solution.py:32
  453.6 47.9 %collective-permute-start.124 = (bf16[4,768,384]{2,1,0:T(8,128)(2,1)S(1)}, bf16[4,768,384]{2,1,0:T(8,128)(2,1)S(1)}, u32[]{:S(2)}, u32[]{:S(2)}) collective-permute-start(bf16[4,768,384]{2,1,0:T(8,128)(2,1)S(1)} %copy-done.28), channel_id=1, source_target_pairs={{0,8},{8,0},{16,24},{24,16},{1,9},{9,1},{17,25},{25,17},{2,10},{10... | collective-permute-start | bytes 7077896 | tf_op jit(solution)/shard_map/ppermute | solution.py:32
  457.1 19.2 %collective-permute-start.97 = (bf16[4,96,384]{2,1,0:T(8,128)(2,1)S(1)}, bf16[4,96,384]{2,1,0:T(8,128)(2,1)S(1)}, u32[]{:S(2)}, u32[]{:S(2)}) collective-permute-start(bf16[4,96,384]{2,1,0:T(8,128)(2,1)S(1)} %split.49), channel_id=1, source_target_pairs={{0,4},{4,0},{1,5},{5,1},{2,6},{6,2},{3,7},{7,3},{8,12},{12,8},{9,1... | collective-permute-start | bytes 884744 | tf_op jit(solution)/shard_map/ppermute | solution.py:28
  458.1 24.5 %collective-permute-start.104 = (bf16[4,96,384]{2,1,0:T(8,128)(2,1)S(1)}, bf16[4,96,384]{2,1,0:T(8,128)(2,1)S(1)}, u32[]{:S(2)}, u32[]{:S(2)}) collective-permute-start(bf16[4,96,384]{2,1,0:T(8,128)(2,1)S(1)} %split.51), channel_id=1, source_target_pairs={{0,4},{4,0},{1,5},{5,1},{2,6},{6,2},{3,7},{7,3},{8,12},{12,8},{9,1... | collective-permute-start | bytes 884744 | tf_op jit(solution)/shard_map/ppermute | solution.py:28
  470.0 19.0 %collective-permute-start.111 = (bf16[4,96,384]{2,1,0:T(8,128)(2,1)S(1)}, bf16[4,96,384]{2,1,0:T(8,128)(2,1)S(1)}, u32[]{:S(2)}, u32[]{:S(2)}) collective-permute-start(bf16[4,96,384]{2,1,0:T(8,128)(2,1)S(1)} %split.53), channel_id=1, source_target_pairs={{0,4},{4,0},{1,5},{5,1},{2,6},{6,2},{3,7},{7,3},{8,12},{12,8},{9,1... | collective-permute-start | bytes 884744 | tf_op jit(solution)/shard_map/ppermute | solution.py:28
  501.5 25.6 %collective-permute-start.138 = (bf16[4,384,384]{2,1,0:T(8,128)(2,1)S(1)}, bf16[4,384,384]{2,1,0:T(8,128)(2,1)S(1)}, u32[]{:S(2)}, u32[]{:S(2)}) collective-permute-start(bf16[4,384,384]{2,1,0:T(8,128)(2,1)S(1)} %split.59), channel_id=1, source_target_pairs={{0,4},{4,0},{1,5},{5,1},{2,6},{6,2},{3,7},{7,3},{8,12},{12,8},{9,1... | collective-permute-start | bytes 3538952 | tf_op jit(solution)/shard_map/ppermute | solution.py:28
  506.7 45.6 %collective-permute-start.125 = (bf16[4,384,384]{2,1,0:T(8,128)(2,1)S(1)}, bf16[4,384,384]{2,1,0:T(8,128)(2,1)S(1)}, u32[]{:S(2)}, u32[]{:S(2)}) collective-permute-start(bf16[4,384,384]{2,1,0:T(8,128)(2,1)S(1)} %split.57), channel_id=1, source_target_pairs={{0,4},{4,0},{1,5},{5,1},{2,6},{6,2},{3,7},{7,3},{8,12},{12,8},{9,1... | collective-permute-start | bytes 3538952 | tf_op jit(solution)/shard_map/ppermute | solution.py:28
  515.8 40.4 %collective-permute-start.102 = (f32[96,384]{1,0:T(8,128)S(1)}, f32[96,384]{1,0:T(8,128)S(1)}, u32[]{:S(2)}, u32[]{:S(2)}) collective-permute-start(f32[96,384]{1,0:T(8,128)S(1)} %add.473), channel_id=1, source_target_pairs={{0,8},{8,0},{16,24},{24,16},{1,9},{9,1},{17,25},{25,17},{2,10},{10... | collective-permute-start | bytes 442376 | tf_op jit(solution)/shard_map/ppermute | solution.py:32
  527.5 29.2 %collective-permute-start.139 = (bf16[384,384]{1,0:T(8,128)(2,1)S(1)}, bf16[384,384]{1,0:T(8,128)(2,1)S(1)}, u32[]{:S(2)}, u32[]{:S(2)}) collective-permute-start(bf16[384,384]{1,0:T(8,128)(2,1)S(1)} %get-tuple-element.108), channel_id=1, source_target_pairs={{0,3},{1,0},{2,1},{3,2},{4,7},{5,4},{6,5},{7,6},{8,11},{9,8},{10,9... | collective-permute-start | bytes 884744 | tf_op jit(solution)/shard_map/ppermute | solution.py:46
  530.9 27.7 %collective-permute-start.140 = (bf16[384,384]{1,0:T(8,128)(2,1)S(1)}, bf16[384,384]{1,0:T(8,128)(2,1)S(1)}, u32[]{:S(2)}, u32[]{:S(2)}) collective-permute-start(bf16[384,384]{1,0:T(8,128)(2,1)S(1)} %get-tuple-element.110), channel_id=1, source_target_pairs={{0,2},{1,3},{2,0},{3,1},{4,6},{5,7},{6,4},{7,5},{8,10},{9,11},{10,... | collective-permute-start | bytes 884744 | tf_op jit(solution)/shard_map/ppermute | solution.py:46
  531.4 30.9 %collective-permute-start.141 = (bf16[384,384]{1,0:T(8,128)(2,1)S(1)}, bf16[384,384]{1,0:T(8,128)(2,1)S(1)}, u32[]{:S(2)}, u32[]{:S(2)}) collective-permute-start(bf16[384,384]{1,0:T(8,128)(2,1)S(1)} %get-tuple-element.109), channel_id=1, source_target_pairs={{0,1},{1,2},{2,3},{3,0},{4,5},{5,6},{6,7},{7,4},{8,9},{9,10},{10,1... | collective-permute-start | bytes 884744 | tf_op jit(solution)/shard_map/ppermute | solution.py:46
  556.2 19.7 %collective-permute-start.127 = (bf16[384,384]{1,0:T(8,128)(2,1)S(1)}, bf16[384,384]{1,0:T(8,128)(2,1)S(1)}, u32[]{:S(2)}, u32[]{:S(2)}) collective-permute-start(bf16[384,384]{1,0:T(8,128)(2,1)S(1)} %get-tuple-element.115), channel_id=1, source_target_pairs={{0,2},{1,3},{2,0},{3,1},{4,6},{5,7},{6,4},{7,5},{8,10},{9,11},{10,... | collective-permute-start | bytes 884744 | tf_op jit(solution)/shard_map/ppermute | solution.py:46
  556.7 25.5 %collective-permute-start.128 = (bf16[384,384]{1,0:T(8,128)(2,1)S(1)}, bf16[384,384]{1,0:T(8,128)(2,1)S(1)}, u32[]{:S(2)}, u32[]{:S(2)}) collective-permute-start(bf16[384,384]{1,0:T(8,128)(2,1)S(1)} %get-tuple-element.114), channel_id=1, source_target_pairs={{0,1},{1,2},{2,3},{3,0},{4,5},{5,6},{6,7},{7,4},{8,9},{9,10},{10,1... | collective-permute-start | bytes 884744 | tf_op jit(solution)/shard_map/ppermute | solution.py:46
  558.6 23.8 %collective-permute-start.109 = (f32[96,384]{1,0:T(8,128)S(1)}, f32[96,384]{1,0:T(8,128)S(1)}, u32[]{:S(2)}, u32[]{:S(2)}) collective-permute-start(f32[96,384]{1,0:T(8,128)S(1)} %add.479), channel_id=1, source_target_pairs={{0,8},{8,0},{16,24},{24,16},{1,9},{9,1},{17,25},{25,17},{2,10},{10... | collective-permute-start | bytes 442376 | tf_op jit(solution)/shard_map/ppermute | solution.py:32
  562.3 29.7 %collective-permute-start.116 = (f32[96,384]{1,0:T(8,128)S(1)}, f32[96,384]{1,0:T(8,128)S(1)}, u32[]{:S(2)}, u32[]{:S(2)}) collective-permute-start(f32[96,384]{1,0:T(8,128)S(1)} %add.485), channel_id=1, source_target_pairs={{0,8},{8,0},{16,24},{24,16},{1,9},{9,1},{17,25},{25,17},{2,10},{10... | collective-permute-start | bytes 442376 | tf_op jit(solution)/shard_map/ppermute | solution.py:32
  562.5 20.0 %collective-permute-start.142 = (f32[384,384]{1,0:T(8,128)S(1)}, f32[384,384]{1,0:T(8,128)S(1)}, u32[]{:S(2)}, u32[]{:S(2)}) collective-permute-start(f32[384,384]{1,0:T(8,128)S(1)} %fusion.22), channel_id=1, source_target_pairs={{0,16},{8,24},{16,0},{24,8},{1,17},{9,25},{17,1},{25,9},{2,18},{10... | collective-permute-start | bytes 1769480 | tf_op jit(solution)/shard_map/ppermute | solution.py:32
  582.6 19.9 %collective-permute-start.143 = (f32[384,384]{1,0:T(8,128)S(1)}, f32[384,384]{1,0:T(8,128)S(1)}, u32[]{:S(2)}, u32[]{:S(2)}) collective-permute-start(f32[384,384]{1,0:T(8,128)S(1)} %add.509), channel_id=1, source_target_pairs={{0,8},{8,0},{16,24},{24,16},{1,9},{9,1},{17,25},{25,17},{2,10},{10... | collective-permute-start | bytes 1769480 | tf_op jit(solution)/shard_map/ppermute | solution.py:32
  (210 other events, 2720.8 us)

commit v2 on v1

v2 whole, which is shorter than its diff:
```python
import functools
import math

import jax
import jax.numpy as jnp
from jax import lax
from jax.experimental import pallas as pl
from jax.experimental.pallas import tpu as pltpu
from jax.sharding import PartitionSpec as P

D = 768
HEAD = 64
HALF = HEAD // 2
COND = 128
PIECE = 256
KEYS = 256
LANES = 128
PAD = 16
CHUNK = 128
SLICES = 4
SCORE = HEAD ** (-0.5) * math.log2(math.e)
MASKED = -1e30

precise = lax.Precision.HIGHEST
epsilon = 1e-05
f32 = jnp.float32
bf16 = jnp.bfloat16


def row_swap(value):
    return lax.ppermute(value, "row", [(0, 1), (1, 0)])


def dp_swap(value, bit):
    return lax.ppermute(value, "dp", [(i, i ^ (1 << bit)) for i in range(lax.axis_size("dp"))])


def col_swap(value, bit):
    return lax.ppermute(value, "col", [(i, i ^ (1 << bit)) for i in range(lax.axis_size("col"))])


def col_from(value, hop):
    size = lax.axis_size("col")
    return lax.ppermute(value, "col", [(i, (i + hop) % size) for i in range(size)]) if hop else value


def col_trade(value):
    return lax.all_to_all(value, "col", 0, 0, tiled=True)


def bits(axis):
    return lax.axis_size(axis).bit_length() - 1


def dp_bit(bit):
    return (lax.axis_index("dp") >> bit) % 2


def in_order(bit, mine, theirs):
    first = bit == 0
    return jnp.where(first, mine, theirs), jnp.where(first, theirs, mine)


def half_at(value, index, axis):
    size = value.shape[axis] // 2
    return lax.dynamic_slice_in_dim(value, index * size, size, axis)


def gather_halves(mine, order):
    pieces = [col_from(mine, k) for k in range(lax.axis_size("col"))]
    yield
    own = jnp.stack(order.next(pieces))
    order.done(own)
    other = row_swap(own)
    own_far = dp_swap(own, 0)
    yield
    other = order.next(other)
    order.done(other)
    yield [own, other, own_far, dp_swap(other, 0)]


def scatter_halves(mine, theirs, order):
    def added(first, second):
        return (first.astype(f32) + second.astype(f32)).astype(bf16)

    heard = dp_swap(theirs, 0)
    yield
    heard = order.next(heard)
    keep, other = added(mine[0], heard[0]), added(mine[1], heard[1])
    order.done(keep, other)
    heard = row_swap(other)
    yield
    total = added(keep, order.next(heard))
    order.done(total)
    parts = col_trade(total)
    yield
    total = jnp.sum(order.next(parts).astype(f32), 0)
    order.done(total)
    for bit in range(1, bits("dp")):
        total = total + dp_swap(total, bit)
    yield
    yield in_order(dp_bit(0), total, dp_swap(total, 0))


def after(value, *others):
    return lax.optimization_barrier((value, others))[0]


class Order:
    def __init__(self):
        self.last = ()

    def next(self, value):
        return after(value, self.last)

    def done(self, *results):
        self.last = results


def contract(first, second, first_axis, second_axis):
    return lax.dot_general(
        first, second, (((first_axis,), (second_axis,)), ((), ())), preferred_element_type=f32
    )


def turned(vectors):
    return vectors.astype(f32).T.astype(bf16)


def in_vmem(count):
    return [pl.BlockSpec(memory_space=pltpu.VMEM)] * count


def in_place(count):
    return [pl.BlockSpec(memory_space=pl.ANY)] * count


SCALARS = pl.BlockSpec(memory_space=pltpu.SMEM)


def like(shape, dtype):
    return jax.ShapeDtypeStruct(shape, dtype)


def cost(flops, moved, powers=0):
    return pl.CostEstimate(flops=flops, bytes_accessed=moved, transcendentals=powers)


def project_kernel(count, slots, scalars, h_ref, turn_ref, *refs):
    sources, w_ref, out_ref, sems = refs[:4], refs[4], refs[5], refs[6]
    part = sources[0].shape[2]
    rows = 3 * HALF
    copies = []
    for index, source in enumerate(sources):
        o, core = index % 2, index // 2
        place = scalars[2] ^ core
        for k in range(count):
            column = lax.rem(scalars[1] + count - k, count)
            for s in range(slots):
                start = pl.multiple_of(column * 3 * HEAD + place * rows, PAD)
                copies.append(
                    pltpu.make_async_copy(
                        source.at[k, pl.ds(s * rows, rows), :],
                        w_ref.at[s, pl.ds(start, rows), pl.ds(o * part, part)],
                        sems.at[len(copies)],
                    )
                )
    for copy in copies:
        copy.start()
    for copy in copies:
        copy.wait()
    h = h_ref[...]
    cosine, sine = turn_ref[0:HALF, :], turn_ref[HALF:HEAD, :]
    for s in range(slots):
        base = s * 3 * HEAD
        for k in range(count):
            values = contract(w_ref[s, k * 3 * HEAD : (k + 1) * 3 * HEAD, :], h, 1, 1)
            for i in range(2):
                low, middle, high = i * HEAD, i * HEAD + HALF, (i + 1) * HEAD
                first, second = values[low:middle], values[middle:high]
                out_ref[k, base + low : base + middle, :] = (first * cosine - second * sine).astype(bf16)
                out_ref[k, base + middle : base + high, :] = (second * cosine + first * sine).astype(bf16)
            out_ref[k, base + 2 * HEAD : base + 3 * HEAD, :] = values[2 * HEAD :].astype(bf16)


def project(scalars, h, turn, sources, slots):
    count, _, part = sources[0].shape
    width = h.shape[0]
    return pl.pallas_call(
        functools.partial(project_kernel, count, slots),
        in_specs=[SCALARS] + in_vmem(2) + in_place(len(sources)),
        out_specs=in_vmem(2),
        out_shape=[
            like((slots, count * 3 * HEAD, 2 * part), bf16),
            like((count, slots * 3 * HEAD, width), bf16),
        ],
        scratch_shapes=[pltpu.SemaphoreType.DMA((len(sources) * count * slots,))],
        cost_estimate=cost(slots * 2 * count * 3 * HEAD * 2 * part * width, 3_000_000 * slots),
        name="project",
    )(scalars, h, turn, *sources)


def pack_kernel(offset, _, own_ref, out_ref):
    for index in range(own_ref.shape[0]):
        out_ref[index] = own_ref[index, offset + HEAD : offset + 3 * HEAD, :]


def pack(scalars, own, offset):
    count, _, width = own.shape
    return pl.pallas_call(
        functools.partial(pack_kernel, offset),
        in_specs=[SCALARS] + in_vmem(1),
        out_specs=in_vmem(1)[0],
        out_shape=like((count, 2 * HEAD, width), bf16),
        cost_estimate=cost(1000, 1_000_000),
        name="pack",
    )(scalars, own)


def merge_kernel(_, d_query_ref, d_own_ref, heard_ref, out_ref):
    for index in range(out_ref.shape[0]):
        out_ref[index, :HEAD, :] = d_query_ref[index]
        out_ref[index, HEAD:, :] = (d_own_ref[index] + heard_ref[index].astype(f32)).astype(bf16)


def merge(scalars, d_query, d_own, heard):
    count, _, width = d_query.shape
    return pl.pallas_call(
        merge_kernel,
        in_specs=[SCALARS] + in_vmem(3),
        out_specs=in_vmem(1)[0],
        out_shape=like((count, 3 * HEAD, width), bf16),
        cost_estimate=cost(1000, 2_000_000),
        name="merge",
    )(scalars, d_query, d_own, heard)


def place_stripes(scalars, own_ref, offset, other_ref, keys, values_t, keys_t=None, values=None):
    row = scalars[0]
    count, _, width = own_ref.shape
    parts = width // LANES
    for place in range(count):
        for stripe, ref, base in (
            (2 * place + row, own_ref.at[place], offset + HEAD),
            (2 * place + 1 - row, other_ref.at[place], 0),
        ):
            start = pl.multiple_of(stripe * width, LANES)
            key_t = ref[base : base + HEAD, :]
            value_t = ref[base + HEAD : base + 2 * HEAD, :]
            keys[pl.ds(start, width), :] = turned(key_t)
            if values is not None:
                values[pl.ds(start, width), :] = turned(value_t)
            for part in range(parts):
                lanes = slice(part * LANES, (part + 1) * LANES)
                if values_t is not None:
                    values_t[stripe * parts + part] = value_t[:, lanes]
                if keys_t is not None:
                    keys_t[stripe * parts + part] = key_t[:, lanes]


def lane_block(ref, block):
    parts = KEYS // LANES
    return jnp.concatenate([ref[block * parts + part] for part in range(parts)], 1)


def attend_kernel(offset, earlier, scalars, own_ref, other_ref, limit_ref, *refs):
    before_ref, (out_ref, wide_ref, log_ref, keys, values_t) = refs[:earlier], refs[earlier:]
    count, _, width = own_ref.shape
    place_stripes(scalars, own_ref, offset, other_ref, keys, values_t)
    row = scalars[0]

    def stripe(place, _):
        query_t = own_ref[place, offset : offset + HEAD, :]
        limit = limit_ref[place]
        first = (2 * place + row) * width

        def step(masked, block, carry):
            top, total, mixed = carry
            start = pl.multiple_of(block * KEYS, KEYS)
            scores = jnp.dot(keys[pl.ds(start, KEYS), :], query_t, preferred_element_type=f32) * SCORE
            if masked:
                key = start + lax.broadcasted_iota(jnp.int32, scores.shape, 0)
                scores = jnp.where(key <= limit, scores, MASKED)
            new_top = jnp.maximum(top, jnp.max(scores, 0, keepdims=True))
            fade = jnp.exp2(top - new_top)
            weight = jnp.exp2(scores - new_top)
            total = total * fade + jnp.sum(weight, 0, keepdims=True)
            mixed = mixed * fade + jnp.dot(
                lane_block(values_t, block), weight.astype(bf16), preferred_element_type=f32
            )
            return new_top, total, mixed

        carry = (
            jnp.full((1, width), MASKED, f32),
            jnp.zeros((1, width), f32),
            jnp.zeros((HEAD, width), f32),
        )
        whole = first // KEYS
        carry = lax.fori_loop(0, whole, functools.partial(step, False), carry)
        top, total, mixed = lax.fori_loop(whole, scalars[3 + place], functools.partial(step, True), carry)
        mixed = mixed / total
        wide_ref[place] = mixed
        log_ref[place] = top + jnp.log2(total)
        return 0

    lax.fori_loop(0, count, stripe, 0)
    rows = out_ref.shape[1]
    for place in range(count):
        out_ref[place, rows - HEAD :, :] = wide_ref[place].astype(bf16)
        if earlier:
            out_ref[place, : rows - HEAD, :] = before_ref[0][place]


def attend(scalars, own, offset, other, limit, earlier):
    count, _, width = own.shape
    seq_len = 2 * count * width
    rows = HEAD + (earlier[0].shape[1] if earlier else 0)
    return pl.pallas_call(
        functools.partial(attend_kernel, offset, len(earlier)),
        in_specs=[SCALARS] + in_vmem(3 + len(earlier)),
        out_specs=in_vmem(3),
        out_shape=[
            like((count, rows, width), bf16),
            like((count, HEAD, width), f32),
            like((count, 1, width), f32),
        ],
        scratch_shapes=[
            pltpu.VMEM((seq_len, HEAD), bf16),
            pltpu.VMEM((seq_len // LANES, HEAD, LANES), bf16),
        ],
        cost_estimate=cost(8_000_000_000, 3_000_000, 3_000_000),
        name="attend",
    )(scalars, own, other, limit, *earlier)


def attend_back_kernel(
    offset,
    grad_offset,
    scalars,
    own_ref,
    other_ref,
    grad_ref,
    wide_ref,
    log_ref,
    limit_ref,
    turn_ref,
    d_query_ref,
    d_own_ref,
    d_other_ref,
    keys,
    values,
    keys_t,
    d_keys,
    d_values,
):
    count, _, width = own_ref.shape
    place_stripes(scalars, own_ref, offset, other_ref, keys, None, keys_t, values)
    row = scalars[0]
    d_keys[...] = jnp.zeros_like(d_keys)
    d_values[...] = jnp.zeros_like(d_values)

    def turn_back(vectors, stripe):
        cosine, sine = turn_ref[stripe, 0:HALF, :], turn_ref[stripe, HALF:HEAD, :]
        upper, lower = vectors[0:HALF], vectors[HALF:HEAD]
        return jnp.concatenate([upper * cosine + lower * sine, lower * cosine - upper * sine], 0)

    def of_stripe(place, _):
        query_t = own_ref[place, offset : offset + HEAD, :]
        grad_t = grad_ref[place, grad_offset : grad_offset + HEAD, :]
        query = turned(query_t)
        grad = turned(grad_t)
        drift = jnp.sum(grad_t.astype(f32) * wide_ref[place], 0, keepdims=True)
        log_sum = log_ref[place]
        limit = limit_ref[place]
        stripe = 2 * place + row

        def step(masked, block, d_query):
            start = pl.multiple_of(block * KEYS, KEYS)
            rows = pl.ds(start, KEYS)
            scores = jnp.dot(keys[rows, :], query_t, preferred_element_type=f32) * SCORE
            weight = jnp.exp2(scores - log_sum)
            if masked:
                key = start + lax.broadcasted_iota(jnp.int32, scores.shape, 0)
                weight = jnp.where(key <= limit, weight, 0.0)
            d_weight = jnp.dot(values[rows, :], grad_t, preferred_element_type=f32)
            d_scores = (weight * (d_weight - drift)).astype(bf16)
            d_values[rows, :] += jnp.dot(weight.astype(bf16), grad, preferred_element_type=f32)
            d_keys[rows, :] += jnp.dot(d_scores, query, preferred_element_type=f32)
            return d_query + jnp.dot(lane_block(keys_t, block), d_scores, preferred_element_type=f32)

        d_query = jnp.zeros((HEAD, width), f32)
        whole = stripe * width // KEYS
        d_query = lax.fori_loop(0, whole, functools.partial(step, False), d_query)
        d_query = lax.fori_loop(whole, scalars[3 + place], functools.partial(step, True), d_query)
        d_query_ref[place] = turn_back(d_query * HEAD ** (-0.5), stripe).astype(bf16)
        return 0

    lax.fori_loop(0, count, of_stripe, 0)

    def finish(place, _):
        for stripe, ref in ((2 * place + row, d_own_ref), (2 * place + 1 - row, d_other_ref)):
            start = pl.multiple_of(stripe * width, LANES)
            d_key = d_keys[pl.ds(start, width), :].T * HEAD ** (-0.5)
            ref[place, 0:HEAD, :] = turn_back(d_key, stripe).astype(ref.dtype)
            ref[place, HEAD : 2 * HEAD, :] = d_values[pl.ds(start, width), :].T.astype(ref.dtype)
        return 0

    lax.fori_loop(0, count, finish, 0)


def attend_back(scalars, own, offset, other, grad, grad_offset, wide, log_sum, limit, turns):
    count, _, width = own.shape
    seq_len = 2 * count * width
    return pl.pallas_call(
        functools.partial(attend_back_kernel, offset, grad_offset),
        in_specs=[SCALARS] + in_vmem(7),
        out_specs=in_vmem(3),
        out_shape=[
            like((count, HEAD, width), bf16),
            like((count, 2 * HEAD, width), f32),
            like((count, 2 * HEAD, width), bf16),
        ],
        scratch_shapes=[
            pltpu.VMEM((seq_len, HEAD), bf16),
            pltpu.VMEM((seq_len, HEAD), bf16),
            pltpu.VMEM((seq_len // LANES, HEAD, LANES), bf16),
            pltpu.VMEM((seq_len, HEAD), f32),
            pltpu.VMEM((seq_len, HEAD), f32),
        ],
        cost_estimate=cost(16_000_000_000, 4_000_000, 3_000_000),
        name="attend_back",
    )(scalars, own, other, grad, wide, log_sum, limit, turns)


SMALL = 9
SHIFT_A, SCALE_A, GATE_A, SHIFT_M, SCALE_M, GATE_M, GAIN_A, GAIN_M, BIAS_DOWN = range(SMALL)


def middle_kernel(slots, scalars, x_own, x_other, g_own, g_other, small_ref, first_ref, last_ref, source, *refs):
    block_own, block_other, d_middle_ref, h_ref, df_ref, d_att_ref, active_ref, d_hidden_ref, mixed_ref, sums_ref = refs[:10]
    d_first, d_last, w_out, up, down, bias, attended_ref, mid_ref, f_ref, dh_ref, sems = refs[10:]
    width, part = x_own.shape
    count = first_ref.shape[0]
    out_rows = slots * HEAD // SLICES
    step_rows = part // 2
    copies = {"out": [], "up": [], "down": [], "bias": []}
    used = 0

    def copy(kind, origin, target):
        nonlocal used
        copies[kind].append(pltpu.make_async_copy(origin, target, sems.at[used]))
        used += 1

    for index in range(SLICES):
        y, core = index // 2, index % 2
        for o in range(2):
            lanes = pl.ds(o * part, part)
            for k in range(count):
                b = core * count + k
                origin = source.at[index, scalars[0] ^ o, k]
                start = k * slots * HEAD + (2 * core + y) * out_rows
                copy("out", origin.at[pl.ds(0, out_rows), :], w_out.at[pl.ds(start, out_rows), lanes])
                start = y * step_rows
                copy("down", origin.at[pl.ds(out_rows, step_rows), :], down.at[b, pl.ds(start, step_rows), lanes])
                copy(
                    "up",
                    origin.at[pl.ds(out_rows + step_rows, step_rows), :],
                    up.at[b, pl.ds(o * part + start, step_rows), :],
                )
                if o == 0 and y == 0:
                    copy("bias", origin.at[pl.ds(out_rows + 2 * step_rows, PAD), :], bias.at[b])
    for kind in copies:
        for each in copies[kind]:
            each.start()
    for k in range(count):
        base = k * slots * HEAD
        mixed_ref[base : base + (slots - 1) * HEAD, :] = first_ref[k]
        mixed_ref[base + (slots - 1) * HEAD : base + slots * HEAD, :] = last_ref[k]

    def small(index):
        return small_ref[index : index + 1, :]

    def wide_rows(own, other, rows):
        return jnp.concatenate([own[rows, :].astype(f32), other[rows, :].astype(f32)], 1)

    def norm(values, rows):
        mean = jnp.mean(values, 1, keepdims=True)
        centered = values - mean
        inv_std = lax.rsqrt(jnp.mean(centered * centered, 1, keepdims=True) + epsilon)
        return centered * inv_std, inv_std

    for each in copies["out"]:
        each.wait()
    attended_ref[...] = contract(mixed_ref[...], w_out[...], 0, 0)
    f_ref[...] = jnp.zeros_like(f_ref)
    dh_ref[...] = jnp.zeros_like(dh_ref)
    sums_ref[...] = jnp.zeros_like(sums_ref)

    def before(index, _):
        rows = pl.ds(pl.multiple_of(index * CHUNK, CHUNK), CHUNK)
        middle = wide_rows(x_own, x_other, rows) + small(GATE_A) * attended_ref[rows, :]
        mid_ref[rows, :] = middle
        normed, _ = norm(middle, rows)
        h_ref[rows, :] = (normed * (small(GAIN_M) * (1.0 + small(SCALE_M))) + small(SHIFT_M)).astype(bf16)
        df_ref[rows, :] = (wide_rows(g_own, g_other, rows) * small(GATE_M)).astype(bf16)
        return 0

    lax.fori_loop(0, width // CHUNK, before, 0)
    for kind in ("up", "down", "bias"):
        for each in copies[kind]:
            each.wait()

    def feed(b, _):
        h, df = h_ref[...], df_ref[...]
        u = contract(h, up[b], 1, 0) + bias[b][0:1, :].astype(f32)
        squared = u * u
        bent = jnp.tanh(0.79788456 * u * (1.0 + 0.044715 * squared))
        active = (0.5 * u * (1.0 + bent)).astype(bf16)
        slope = 0.5 * (1.0 + bent) + 0.5 * u * (1.0 - bent * bent) * (
            0.79788456 * (1.0 + 3.0 * 0.044715 * squared)
        )
        active_ref[b] = active
        d_hidden = (slope * contract(df, down[b], 1, 1)).astype(bf16)
        d_hidden_ref[b] = d_hidden
        f_ref[...] += contract(active, down[b], 1, 0)
        dh_ref[...] += contract(d_hidden, up[b], 1, 1)
        return 0

    lax.fori_loop(0, 2 * count, feed, 0)

    def after(index, _):
        rows = pl.ds(pl.multiple_of(index * CHUNK, CHUNK), CHUNK)
        middle = mid_ref[rows, :]
        branch = f_ref[rows, :] + small(BIAS_DOWN)
        out = (middle + small(GATE_M) * branch).astype(bf16)
        block_own[rows, :] = out[:, :part]
        block_other[rows, :] = out[:, part:]
        upstream = wide_rows(g_own, g_other, rows)
        normed, inv_std = norm(middle, rows)
        dh = dh_ref[rows, :]
        scaled = dh * (small(GAIN_M) * (1.0 + small(SCALE_M)))
        mean_grad = jnp.mean(scaled, 1, keepdims=True)
        mean_proj = jnp.mean(scaled * normed, 1, keepdims=True)
        d_middle = upstream + inv_std * (scaled - mean_grad - normed * mean_proj)
        d_middle_ref[rows, :] = d_middle
        d_att_ref[rows, :] = (d_middle * small(GATE_A)).astype(bf16)
        for i, value in enumerate(
            (d_middle * attended_ref[rows, :], dh, dh * normed, upstream * branch, df_ref[rows, :].astype(f32))
        ):
            sums_ref[i : i + 1, :] += jnp.sum(value, 0, keepdims=True)
        return 0

    lax.fori_loop(0, width // CHUNK, after, 0)
    d_att = d_att_ref[...]
    for k in range(count):
        base = k * slots * HEAD
        values = contract(w_out[base : base + slots * HEAD, :], d_att, 1, 1).astype(bf16)
        d_first[k] = values[: (slots - 1) * HEAD]
        d_last[k] = values[(slots - 1) * HEAD :]


def middle(scalars, x, g, small, first, last, source, slots):
    count = first.shape[0]
    width, part = x[0].shape
    blocks = 2 * count
    heads = count * slots * HEAD
    return pl.pallas_call(
        functools.partial(middle_kernel, slots),
        in_specs=[SCALARS] + in_vmem(7) + in_place(1),
        out_specs=in_vmem(12),
        out_shape=[
            like((width, part), bf16),
            like((width, part), bf16),
            like((width, 2 * part), f32),
            like((width, 2 * part), bf16),
            like((width, 2 * part), bf16),
            like((width, 2 * part), bf16),
            like((blocks, width, part), bf16),
            like((blocks, width, part), bf16),
            like((heads, width), bf16),
            like((8, 2 * part), f32),
            like((count, (slots - 1) * HEAD, width), bf16),
            like((count, HEAD, width), bf16),
        ],
        scratch_shapes=[
            pltpu.VMEM((heads, 2 * part), bf16),
            pltpu.VMEM((blocks, 2 * part, part), bf16),
            pltpu.VMEM((blocks, part, 2 * part), bf16),
            pltpu.VMEM((blocks, PAD, part), bf16),
            pltpu.VMEM((width, 2 * part), f32),
            pltpu.VMEM((width, 2 * part), f32),
            pltpu.VMEM((width, 2 * part), f32),
            pltpu.VMEM((width, 2 * part), f32),
            pltpu.SemaphoreType.DMA(((6 * SLICES + 2) * count,)),
        ],
        cost_estimate=cost(2 * width * (4 * blocks * part * 2 * part + 2 * heads * 2 * part), 14_000_000, 2_000_000),
        name="middle",
    )(scalars, *x, *g, small, first, last, source)


def grads_kernel(slots, scalars, h_ref, df_ref, d_att_ref, active_ref, d_hidden_ref, mixed_ref, out_ref, d_out):
    part = h_ref.shape[1] // 2
    count = active_ref.shape[0] // 2
    out_rows = slots * HEAD // SLICES
    step_rows = part // 2
    d_out[...] = contract(mixed_ref[...], d_att_ref[...], 1, 0).astype(bf16)

    def of_block(b, _):
        core, k = b // count, b % count
        d_hidden = d_hidden_ref[b]
        d_up = contract(h_ref[...], d_hidden, 0, 0).astype(bf16)
        d_down = contract(active_ref[b], df_ref[...], 0, 0).astype(bf16)
        d_bias = jnp.broadcast_to(jnp.sum(d_hidden.astype(f32), 0, keepdims=True), (PAD, part)).astype(bf16)
        for y in range(2):
            start = pl.multiple_of(k * slots * HEAD + (2 * core + y) * out_rows, PAD)
            out_part = d_out[pl.ds(start, out_rows), :]
            for o in range(2):
                target = out_ref.at[2 * y + core, scalars[0] ^ o, k]
                lanes = slice(o * part, (o + 1) * part)
                start = o * part + y * step_rows
                target[:out_rows, :] = out_part[:, lanes]
                target[out_rows : out_rows + step_rows, :] = d_down[y * step_rows : (y + 1) * step_rows, lanes]
                target[out_rows + step_rows : out_rows + 2 * step_rows, :] = d_up[start : start + step_rows]
                target[out_rows + 2 * step_rows :, :] = d_bias
        return 0

    lax.fori_loop(0, 2 * count, of_block, 0)


def weight_grads(scalars, h, df, d_att, active, d_hidden, mixed, slots):
    count = active.shape[0] // 2
    width, whole = h.shape
    part = whole // 2
    return pl.pallas_call(
        functools.partial(grads_kernel, slots),
        in_specs=[SCALARS] + in_vmem(6),
        out_specs=in_vmem(1)[0],
        out_shape=like((SLICES, 2, count, slots * HEAD // SLICES + part + PAD, part), bf16),
        scratch_shapes=[pltpu.VMEM((mixed.shape[0], whole), bf16)],
        cost_estimate=cost(2 * width * (4 * count * part * whole + mixed.shape[0] * whole), 20_000_000),
        name="weight_grads",
    )(scalars, h, df, d_att, active, d_hidden, mixed)


def unproject_kernel(scalars, h_ref, w_ref, *refs):
    slots = w_ref.shape[0]
    pieces, (dh_ref, mine, theirs, grad) = refs[:slots], refs[slots:]
    count, rows, width = pieces[0].shape
    part = h_ref.shape[1] // 2
    half = rows // 2
    dh = jnp.zeros(dh_ref.shape, f32)
    for s in range(slots):
        back = pieces[s][...].reshape(count * rows, width)
        dh = dh + contract(back, w_ref[s], 0, 0)
        grad[...] = contract(back, h_ref[...], 1, 0).astype(bf16)
        for core, target in enumerate((mine, theirs)):
            place = scalars[2] ^ core
            for k in range(count):
                start = pl.multiple_of(k * rows + place * half, PAD)
                values = grad[pl.ds(start, half), :]
                for o in range(2):
                    target[o, k, s * half : (s + 1) * half, :] = values[:, o * part : (o + 1) * part]
    dh_ref[...] = dh


def unproject(scalars, h, weight, pieces):
    width, whole = h.shape
    slots = len(pieces)
    count = pieces[0].shape[0]
    shape = like((2, count, slots * 3 * HALF, whole // 2), bf16)
    return pl.pallas_call(
        unproject_kernel,
        in_specs=[SCALARS] + in_vmem(2 + slots),
        out_specs=in_vmem(3),
        out_shape=[like((width, whole), f32), shape, shape],
        scratch_shapes=[pltpu.VMEM((weight.shape[1], whole), bf16)],
        cost_estimate=cost(slots * 4 * width * whole * weight.shape[1], 5_000_000 * slots),
        name="unproject",
    )(scalars, h, weight, *pieces)


def embed_time(time_step):
    half_size = COND // 2
    frequency = jnp.exp(-math.log(10000.0) * jnp.arange(half_size, dtype=f32) / half_size)
    angles = time_step * frequency
    return jax.nn.silu(jnp.concatenate([jnp.cos(angles), jnp.sin(angles)]))


def shards(
    tokens, cotangent, timestep, piece_starts, w_mod, b_mod, gain_attn, w_qkv, w_out, gain_mlp, w_up, b_up, w_down, b_down
):
    cols = lax.axis_size("col")
    row, col, core, far = lax.axis_index("row"), lax.axis_index("col"), dp_bit(0), dp_bit(1)
    block_rows, part = tokens.shape
    width = block_rows // 2
    slots = w_qkv.shape[0] // (3 * HEAD)

    def half_rows(block):
        return half_at(block, row, 0), row_swap(half_at(block, 1 - row, 0))

    x = half_rows(tokens)

    order = Order()

    w_parts = w_qkv.reshape(slots, 3 * HEAD, part)
    groups = [(0, 1), (1, slots)]
    blocks = [half_at(w_parts[low:high], core, 1).reshape(-1, part) for low, high in groups]

    def quarter_at(block):
        return half_at(half_at(block, core, 0), far, 0)

    bias = jnp.broadcast_to(half_at(b_up[None], core, 1), (PAD, part))
    rest = jnp.concatenate(
        [quarter_at(w_out), quarter_at(w_down), half_at(half_at(w_up, core, 1), far, 0), bias], 0
    )

    condition = embed_time(timestep[0].astype(f32))
    modulation = jnp.einsum("k,kjd->jd", condition, w_mod.astype(f32), precision=precise) + b_mod
    small = jnp.concatenate([modulation, gain_attn[None], gain_mlp[None], b_down[None]], 0)
    small = jnp.concatenate([small, row_swap(small)], 1)

    residual = jnp.concatenate(x, 1).astype(f32)
    centered = residual - jnp.mean(residual, -1, keepdims=True)
    inv_std = lax.rsqrt(jnp.mean(centered * centered, -1, keepdims=True) + epsilon)
    gain_one = small[GAIN_A] * (1.0 + small[SCALE_A])
    h_one = (centered * inv_std * gain_one + small[SHIFT_A]).astype(bf16)

    lane = jnp.arange(width, dtype=jnp.int32)
    frequency = jnp.exp(-math.log(10000.0) * jnp.arange(HALF, dtype=f32) / HALF)
    places = jnp.arange(2 * cols, dtype=jnp.int32)[:, None] * width + lane[None]
    angles = places.astype(f32)[:, None, :] * frequency[None, :, None]
    turns = jnp.concatenate([jnp.cos(angles), jnp.sin(angles)], 1)
    here = lax.dynamic_index_in_dim(turns, 2 * col + row, 0, keepdims=False)
    own_stripes = 2 * jnp.arange(cols, dtype=jnp.int32) + row
    own_places = own_stripes[:, None] * width + lane[None]
    starts = piece_starts[0]
    inside = (own_places[..., None] >= starts) & (own_places[..., None] < starts + PIECE)
    limit = jnp.max(jnp.where(inside, starts + PIECE - 1, own_places[..., None]), -1)
    scalars = jnp.concatenate(
        [jnp.stack([row, col, core]), jnp.max(limit, 1) // KEYS + 1]
    ).astype(jnp.int32)
    limit = limit[:, None, :]

    soon = gather_halves(blocks[0], order)
    next(soon)
    next(soon)
    late = gather_halves(order.next(blocks[1]), order)
    next(late)
    soon = next(soon)
    next(late)
    rest = lax.all_gather(order.next(rest), ("dp", "row", "col"), axis=0, tiled=False)
    rest = rest.reshape((-1, 2, cols) + rest.shape[1:])[:SLICES]
    w_groups, own = [], []

    def begin(group, source):
        low, high = groups[group]
        weight, pieces = project(order.next(scalars), h_one, here, source, high - low)
        order.done(weight)
        w_groups.append(weight)
        pieces = col_trade(pieces)
        own.extend((pieces, 3 * HEAD * i) for i in range(high - low))

    begin(0, soon)
    begin(1, next(late))
    g = half_rows(after(cotangent, own[-1][0]))
    forward, other = [], [None] * slots
    earlier = ()

    def share(slot):
        packed = pack(order.next(scalars), *own[slot])
        order.done(packed)
        other[slot] = row_swap(packed)

    share(0)
    for slot in range(slots):
        results = attend(order.next(scalars), *own[slot], other[slot], limit, earlier if slot < slots - 1 else ())
        order.done(results[2])
        forward.append(results)
        if slot < slots - 1:
            earlier = (results[0],)
        if slot == 0:
            for later in range(1, slots):
                share(later)
    first = col_trade(forward[slots - 2][0])
    last = col_trade(forward[slots - 1][0])

    kept = middle(order.next(scalars), x, g, small, first, last, rest, slots)
    (
        block_own,
        block_other,
        d_middle,
        h_two,
        d_branch,
        d_attended,
        active,
        d_hidden,
        mixed,
        sums,
        d_first,
        d_last,
    ) = kept
    order.done(d_middle)

    d_last = col_trade(d_last)
    grads = weight_grads(order.next(scalars), h_two, d_branch, d_attended, active, d_hidden, mixed, slots)
    order.done(grads)
    extra = lax.axis_size("dp") - SLICES
    grads = jnp.pad(grads, ((0, extra),) + ((0, 0),) * 4) if extra else grads
    grads = lax.psum_scatter(
        grads.reshape((-1,) + grads.shape[3:]), ("dp", "row", "col"), scatter_dimension=0, tiled=True
    )
    d_first = col_trade(d_first)

    back, shared = {}, {}

    def pull(slot):
        grad = (d_last, 0) if slot == slots - 1 else (d_first, slot * HEAD)
        d_query, d_own, d_other = attend_back(
            order.next(scalars), *own[slot], other[slot], *grad, *forward[slot][1:], limit, turns
        )
        order.done(d_other)
        shared[slot] = d_query, d_own, row_swap(d_other)

    def send(slot):
        pieces = merge(order.next(scalars), *shared[slot])
        order.done(pieces)
        back[slot] = col_trade(pieces)

    d_hs = []

    def finish(group):
        low, high = groups[group]
        pieces = [back[slot] for slot in range(low, high)]
        d_h, mine, theirs = unproject(order.next(scalars), h_one, w_groups[group], pieces)
        order.done(d_h)
        d_hs.append(d_h)
        steps = scatter_halves(mine, theirs, order)
        next(steps)
        return steps

    for slot in reversed(range(slots)):
        pull(slot)
        if slot < slots - 1:
            send(slot + 1)
    send(0)
    late = finish(1)
    next(late)
    soon = finish(0)
    d_h_one = d_hs[0] + d_hs[1]
    normed = centered * inv_std
    scaled = d_h_one * gain_one
    mean_grad = jnp.mean(scaled, -1, keepdims=True)
    mean_proj = jnp.mean(scaled * normed, -1, keepdims=True)
    d_tokens = d_middle + inv_std * (scaled - mean_grad - normed * mean_proj)
    sums = jnp.concatenate([jnp.sum(d_h_one, 0)[None], jnp.sum(d_h_one * normed, 0)[None], sums[:5]], 0)

    order.done(d_tokens, sums)

    def whole_rows(own_part, other_part):
        return jnp.concatenate(in_order(row, own_part, row_swap(other_part)), 0)

    tokens_out = whole_rows(d_tokens[:, :part], d_tokens[:, part:])
    block_out = whole_rows(block_own, block_other)

    next(soon)
    next(late)
    next(soon)
    next(late)
    next(soon)
    late, soon = next(late), next(soon)
    d_qkv = []
    for (low, high), found in zip(groups, (soon, late)):
        parts = [half.reshape(high - low, -1, part) for half in found]
        d_qkv.append(jnp.concatenate(parts, 1).reshape(-1, part))
    d_qkv = jnp.concatenate(d_qkv, 0)

    grads = lax.all_gather(grads[0], "dp", axis=0, tiled=False)[:SLICES].astype(f32)
    rows = slots * HEAD // SLICES
    step = part // 2
    ordered = [grads[2 * y + c] for c in range(2) for y in range(2)]
    d_out_proj = jnp.concatenate([each[:rows] for each in ordered], 0)
    d_down = jnp.concatenate([each[rows : rows + step] for each in ordered], 0)
    d_up = jnp.concatenate(
        [
            jnp.concatenate([grads[2 * y + c, rows + step : rows + 2 * step] for c in range(2)], 1)
            for y in range(2)
        ],
        0,
    )
    d_bias = jnp.concatenate([grads[c, rows + 2 * step] for c in range(2)], 0)

    sums = sums[:, :part] + row_swap(sums[:, part:])
    for bit in range(bits("col")):
        sums = sums + col_swap(sums, bit)
    per_seq = jnp.concatenate(
        [
            sums[0:1],
            sums[1:2] * gain_attn,
            sums[2:4],
            sums[4:5] * gain_mlp,
            sums[5:6],
            sums[1:2] * (1.0 + modulation[1]),
            sums[4:5] * (1.0 + modulation[4]),
            sums[6:7],
            jnp.pad(condition, (0, part - COND))[None],
        ],
        0,
    )[None]
    for bit in range(bits("dp")):
        per_seq = jnp.concatenate(in_order(dp_bit(bit), per_seq, dp_swap(per_seq, bit)), 0)
    conditions = per_seq[:, SMALL, :COND]
    d_mod_w = sum(conditions[s][:, None, None] * per_seq[s, :6][None] for s in range(per_seq.shape[0]))
    totals = jnp.sum(per_seq[:, :SMALL], 0)

    return (
        block_out,
        tokens_out,
        d_mod_w,
        totals[:6],
        totals[6],
        d_qkv,
        d_out_proj,
        totals[7],
        d_up,
        d_bias,
        d_down,
        totals[8],
    )


def solution(mesh):
    blocks = P(("dp", "col"), "row")
    return jax.shard_map(
        shards,
        mesh=mesh,
        in_specs=(
            blocks,
            blocks,
            P("dp"),
            P("dp", None),
            P(None, None, "row"),
            P(None, "row"),
            P("row"),
            P("col", "row"),
            P("col", "row"),
            P("row"),
            P("row", "col"),
            P("col"),
            P("col", "row"),
            P("row"),
        ),
        out_specs=(
            blocks,
            blocks,
            P(None, None, "row"),
            P(None, "row"),
            P("row"),
            P("col", "row"),
            P("col", "row"),
            P("row"),
            P("row", "col"),
            P("col"),
            P("col", "row"),
            P("row"),
        ),
        check_vma=False,
    )
```

time: 615 us -> 501 us (0.81)
  starting transfers between devices: 211 us -> 120 us
  waiting for transfers between devices: 182 us -> 128 us
  Pallas kernels: 108 us -> 160 us
  other arithmetic: 57.1 us -> 29.8 us
  blocking collectives: 0 us -> 20.6 us
  matrix products: 13.8 us -> 0.34 us
  between operations: 4.5 us -> 15.1 us
    all_to_all x0 -> x10, waiting for transfers between devices: none -> 60.8 us  [col_trade(): return lax.all_to_all(value, 'col', 0, 0, tiled=True)]
    ppermute x39 -> x0, starting transfers between devices: 56.8 us -> none  [col_to(): lax.ppermute(value, 'col', [(i, (i - hop) % size) for i in range(size)])]
    pallas_call x7 -> x18, Pallas kernels: 108 us -> 160 us  [the longest x3 47.2 us: attend_back(): pl.pallas_call(functools.partial(attend_back_kernel, offset, grad_offset)...]
    all_to_all x0 -> x10, starting transfers between devices: none -> 49 us  [col_trade(): return lax.all_to_all(value, 'col', 0, 0, tiled=True)]
    ppermute x39 -> x6, waiting for transfers between devices: 57.5 us -> 14.5 us  [col_from(): lax.ppermute(value, 'col', [(i, (i + hop) % size) for i in range(size)])]
    ppermute x39 -> x6, starting transfers between devices: 46 us -> 6.4 us  [col_from(): lax.ppermute(value, 'col', [(i, (i + hop) % size) for i in range(size)])]
    ppermute x39 -> x0, waiting for transfers between devices: 36.5 us -> none  [col_to(): lax.ppermute(value, 'col', [(i, (i - hop) % size) for i in range(size)])]
    ppermute x30 -> x12, starting transfers between devices: 67.5 us -> 39.4 us  [dp_swap(): lax.ppermute(value, 'dp', [(i, i ^ 1 << bit) for i in range(lax.axis_size...]
  transfers between devices with their start and end apart: 144 -> 49, of which waited for: 45 -> 25; matrix products, arithmetic and copies ran while one was open for 15% -> 7% of each run, Pallas kernels for 14% -> 24%
where the time goes in v2:
time: 501 us; the launch traced here: 497 us
  Pallas kernels  160 us (32%)
  waiting for transfers between devices  128 us (26%)
  starting transfers between devices  120 us (24%)
  other arithmetic  29.8 us (6%)
  local copies, waits for them, and re-layouts  23.9 us (5%)
  blocking collectives  20.6 us (4%)
  between operations  15.1 us (3%)
    all_to_all x10, waiting for transfers between devices, col_trade(): return lax.all_to_all(value, 'col', 0, 0, tiled=True)  60.8 us
    all_to_all x10, starting transfers between devices, col_trade(): return lax.all_to_all(value, 'col', 0, 0, tiled=True)  49 us
    pallas_call x3, Pallas kernels, attend_back(): pl.pallas_call(functools.partial(attend_back_kernel, offset, grad_offset)...  47.2 us
    ppermute x16, waiting for transfers between devices, row_swap(): return lax.ppermute(value, 'row', [(0, 1), (1, 0)])  42.7 us
    pallas_call x3, Pallas kernels, attend(): pl.pallas_call(functools.partial(attend_kernel, offset, len(earlier)), in...  41.4 us
    ppermute x12, starting transfers between devices, dp_swap(): lax.ppermute(value, 'dp', [(i, i ^ 1 << bit) for i in range(lax.axis_size...  39.4 us
    pallas_call x1, Pallas kernels, middle(): pl.pallas_call(functools.partial(middle_kernel, slots), in_specs=[SCALARS...  22.9 us
    all_to_all x1, blocking collectives, col_trade(): return lax.all_to_all(value, 'col', 0, 0, tiled=True)  20.6 us
  transfers between devices with their start and end apart: 49, of which 25 were waited for; matrix products, arithmetic and copies ran while one was open for 7% of the time, Pallas kernels for 24%

profile of v2, /device:TPU:9, one launch (start us, length us, event | category | flops | bytes accessed | tf_op | source)
XLA Modules:
  0.0 497.2 jit_solution(10885980409889641905)
XLA Ops:
  12.2 1.9 collective-permute-done.1
  14.1 4.0 collective-permute-done.2
  26.3 4.7 collective-permute-done.4
  31.0 3.8 collective-permute-done.5
  41.8 2.8 collective-permute-done.9
  44.7 2.2 collective-permute-start.10
  50.8 4.3 project.2
  55.2 3.5 all-to-all-start
  59.5 2.7 collective-permute-done.7.refs_1_
  63.4 2.0 collective-permute-done.13.refs_3_
  65.4 5.7 %project.3 = (bf16[2,768,768]{2,1,0:T(8,128)(2,1)}, bf16[4,384,384]{2,1,0:T(8,128)(2,1)}) custom-call(s32[7]{0:T(128)} %pad_add_fusion.scalars._, bf16[384,768]{1,0:T(8,128)(2,1)} %fusion.7.h_ref, f32[64,384]{1,0:T(8,128)} %fusion.19.turn_ref, bf16[4,192,384]{2,1,0:T(8,128)(2,1)} %copy-done.15, bf16[4,192,384]{2,1,0:T(8,128)(2,1)} %collective-permute-done.7.refs_1_, ...), custom_call_target="tpu_custom_call" | custom-call | flops 905969664 | bytes 6000000 | tf_op jit(solution)/shard_map/project/pallas_call | solution.py:189
  71.1 9.5 %all-to-all-done.own_ref = bf16[4,192,384]{2,1,0:T(8,128)(2,1)S(1)} async-done(((bf16[4,192,384]{2,1,0:T(8,128)(2,1)}), bf16[4,192,384]{2,1,0:T(8,128)(2,1)S(1)}, u32[]{:S(2)}, u32[]{:S(2)}) %all-to-all-start) | async-done | bytes 589856 | tf_op jit(solution)/shard_map/all_to_all | solution.py:48
  81.4 6.0 %all-to-all-start.1 = ((bf16[4,384,384]{2,1,0:T(8,128)(2,1)}), bf16[4,384,384]{2,1,0:T(8,128)(2,1)S(1)}, u32[]{:S(2)}, u32[]{:S(2)}) async-start(bf16[4,384,384]{2,1,0:T(8,128)(2,1)} %get-tuple-element.109), calls=%async_computation.1 | async-start | bytes 2359296 | tf_op jit(solution)/shard_map/all_to_all | solution.py:48
  87.5 1.9 pack.3
  90.5 6.1 %collective-permute-done.14.other_ref = bf16[4,128,384]{2,1,0:T(8,128)(2,1)S(1)} collective-permute-done((bf16[4,128,384]{2,1,0:T(8,128)(2,1)}, bf16[4,128,384]{2,1,0:T(8,128)(2,1)S(1)}, u32[]{:S(2)}, u32[]{:S(2)}) %collective-permute-start.14) | collective-permute-done | bytes 393248 | tf_op jit(solution)/shard_map/ppermute | solution.py:31
  97.4 13.6 %attend.3 = (bf16[4,64,384]{2,1,0:T(8,128)(2,1)}, f32[4,64,384]{2,1,0:T(8,128)}, f32[4,1,384]{2,1,0:T(1,128)}) custom-call(s32[7]{0:T(128)} %pad_add_fusion.scalars._, bf16[4,192,384]{2,1,0:T(8,128)(2,1)} %copy-done.7, bf16[4,128,384]{2,1,0:T(8,128)(2,1)} %copy-done.50, s32[4,1,384]{2,1,0:T(1,128)} %broadcast_in_dim.32.limit_ref), custom_call_target="tpu_custom_call" | custom-call | flops 8000000000 | bytes 3000000 | tf_op jit(solution)/shard_map/attend/pallas_call | solution.py:318
  111.0 12.9 %all-to-all-done.1.own_ref = bf16[4,384,384]{2,1,0:T(8,128)(2,1)S(1)} async-done(((bf16[4,384,384]{2,1,0:T(8,128)(2,1)}), bf16[4,384,384]{2,1,0:T(8,128)(2,1)S(1)}, u32[]{:S(2)}, u32[]{:S(2)}) %all-to-all-start.1) | async-done | bytes 1179680 | tf_op jit(solution)/shard_map/all_to_all | solution.py:48
  124.9 2.1 pack.4
  127.5 2.1 pack.5
  130.5 3.3 collective-permute-done.15.other_ref
  134.6 14.1 %attend.4 = (bf16[4,128,384]{2,1,0:T(8,128)(2,1)}, f32[4,64,384]{2,1,0:T(8,128)}, f32[4,1,384]{2,1,0:T(1,128)}) custom-call(s32[7]{0:T(128)} %pad_add_fusion.scalars._, bf16[4,384,384]{2,1,0:T(8,128)(2,1)} %copy-done.4, bf16[4,128,384]{2,1,0:T(8,128)(2,1)} %copy-done.51, s32[4,1,384]{2,1,0:T(1,128)} %broadcast_in_dim.32.limit_ref, ...), custom_call_target="tpu_custom_call" | custom-call | flops 8000000000 | bytes 3000000 | tf_op jit(solution)/shard_map/attend/pallas_call | solution.py:318
  149.4 13.8 %attend.5 = (bf16[4,64,384]{2,1,0:T(8,128)(2,1)}, f32[4,64,384]{2,1,0:T(8,128)}, f32[4,1,384]{2,1,0:T(1,128)}) custom-call(s32[7]{0:T(128)} %pad_add_fusion.scalars._, bf16[4,384,384]{2,1,0:T(8,128)(2,1)} %copy-done.4, bf16[4,128,384]{2,1,0:T(8,128)(2,1)} %copy-done.52, s32[4,1,384]{2,1,0:T(1,128)} %broadcast_in_dim.32.limit_ref), custom_call_target="tpu_custom_call" | custom-call | flops 8000000000 | bytes 3000000 | tf_op jit(solution)/shard_map/attend/pallas_call | solution.py:318
  163.2 20.6 %all_to_all.55.last_ref = bf16[4,64,384]{2,1,0:T(8,128)(2,1)} all-to-all(bf16[4,64,384]{2,1,0:T(8,128)(2,1)} %get-tuple-element.119), channel_id=1, replica_groups=mesh['dp'=4,'row'=2,'col'=4] {'col'}, dimensions={0} | all-to-all | bytes 393216 | tf_op jit(solution)/shard_map/all_to_all | solution.py:48
  183.8 4.3 all-to-all-start.2
  188.8 3.3 collective-permute-start.17
  192.1 4.5 collective-permute-done.17.g_other
  197.4 22.9 %middle.1 = (bf16[384,384]{1,0:T(8,128)(2,1)}, bf16[384,384]{1,0:T(8,128)(2,1)}, f32[384,768]{1,0:T(8,128)}, bf16[384,768]{1,0:T(8,128)(2,1)}, bf16[384,768]{1,0...) custom-call(s32[7]{0:T(128)} %pad_add_fusion.scalars._, ...), custom_call_target="tpu_custom_call" | custom-call | flops 8153726976 | bytes 14000000 | tf_op jit(solution)/shard_map/middle/pallas_call | solution.py:567
  220.4 15.4 %weight_grads.1 = bf16[4,2,4,448,384]{4,3,2,1,0:T(8,128)(2,1)} custom-call(s32[7]{0:T(128)} %pad_add_fusion.scalars._, bf16[384,768]{1,0:T(8,128)(2,1)} %get-tuple-element.125.h_ref, bf16[384,768]{1,0:T(8,128)(2,1)} %get-tuple-element.126.df_ref, bf16[384,768]{1,0:T(8,128)(2,1)} %get-tuple-element.127.d_att_ref, ...), custom_call_target="tpu_custom_call" | custom-call | flops 4076863488 | bytes 20000000 | tf_op jit(solution)/shard_map/weight_grads/pallas_call | solution.py:634
  235.7 4.9 all-to-all-start.4
  241.5 3.9 all-to-all-done.4.grad_ref
  245.4 3.7 all-to-all-start.5
  249.1 15.7 %attend_back.3 = (bf16[4,64,384]{2,1,0:T(8,128)(2,1)}, f32[4,128,384]{2,1,0:T(8,128)}, bf16[4,128,384]{2,1,0:T(8,128)(2,1)}) custom-call(s32[7]{0:T(128)} %pad_add_fusion.scalars._, bf16[4,384,384]{2,1,0:T(8,128)(2,1)} %copy-done.4, bf16[4,128,384]{2,1,0:T(8,128)(2,1)} %copy-done.52, bf16[4,64,384]{2,1,0:T(8,128)(2,1)} %copy-done.34, ...), custom_call_target="tpu_custom_call" | custom-call | flops 16000000000 | bytes 4000000 | tf_op jit(solution)/shard_map/attend_back/pallas_call | solution.py:414
  264.8 4.5 collective-permute-start.19
  270.1 15.9 %attend_back.4 = (bf16[4,64,384]{2,1,0:T(8,128)(2,1)}, f32[4,128,384]{2,1,0:T(8,128)}, bf16[4,128,384]{2,1,0:T(8,128)(2,1)}) custom-call(s32[7]{0:T(128)} %pad_add_fusion.scalars._, bf16[4,384,384]{2,1,0:T(8,128)(2,1)} %copy-done.4, bf16[4,128,384]{2,1,0:T(8,128)(2,1)} %copy-done.51, bf16[4,128,384]{2,1,0:T(8,128)(2,1)} %copy-done.21, ...), custom_call_target="tpu_custom_call" | custom-call | flops 16000000000 | bytes 4000000 | tf_op jit(solution)/shard_map/attend_back/pallas_call | solution.py:414
  288.4 2.3 merge.3
  290.7 4.5 all-to-all-start.7
  295.2 15.6 %attend_back.5 = (bf16[4,64,384]{2,1,0:T(8,128)(2,1)}, f32[4,128,384]{2,1,0:T(8,128)}, bf16[4,128,384]{2,1,0:T(8,128)(2,1)}) custom-call(s32[7]{0:T(128)} %pad_add_fusion.scalars._, bf16[4,192,384]{2,1,0:T(8,128)(2,1)} %copy-done.7, bf16[4,128,384]{2,1,0:T(8,128)(2,1)} %copy-done.50, bf16[4,128,384]{2,1,0:T(8,128)(2,1)} %copy-done.21, ...), custom_call_target="tpu_custom_call" | custom-call | flops 16000000000 | bytes 4000000 | tf_op jit(solution)/shard_map/attend_back/pallas_call | solution.py:414
  311.5 2.2 merge.4
  313.8 4.5 all-to-all-start.6
  320.0 5.5 %collective-permute-done.21.heard_ref = bf16[4,128,384]{2,1,0:T(8,128)(2,1)S(1)} collective-permute-done((bf16[4,128,384]{2,1,0:T(8,128)(2,1)S(1)}, bf16[4,128,384]{2,1,0:T(8,128)(2,1)S(1)}, u32[]{:S(2)}, u32[]{:S(2)}) %collective-permute-start.21) | collective-permute-done | bytes 393248 | tf_op jit(solution)/shard_map/ppermute | solution.py:31
  326.2 2.2 merge.5
  328.4 15.6 %all-to-all-done.6.refs_0_ = bf16[4,192,384]{2,1,0:T(8,128)(2,1)S(1)} async-done(((bf16[4,192,384]{2,1,0:T(8,128)(2,1)}), bf16[4,192,384]{2,1,0:T(8,128)(2,1)S(1)}, u32[]{:S(2)}, u32[]{:S(2)}) %all-to-all-start.6) | async-done | bytes 589856 | tf_op jit(solution)/shard_map/all_to_all | solution.py:48
  344.9 6.0 %unproject.2 = (f32[384,768]{1,0:T(8,128)}, bf16[2,4,192,384]{3,2,1,0:T(8,128)(2,1)}, bf16[2,4,192,384]{3,2,1,0:T(8,128)(2,1)}) custom-call(s32[7]{0:T(128)} %pad_add_fusion.scalars._, bf16[384,768]{1,0:T(8,128)(2,1)} %fusion.7.h_ref, bf16[2,768,768]{2,1,0:T(8,128)(2,1)} %get-tuple-element.103.w_ref, bf16[4,192,384]{2,1,0:T(8,128)(2,1)} %copy-done.18, ...), custom_call_target="tpu_custom_call" | custom-call | flops 1811939328 | bytes 10000000 | tf_op jit(solution)/shard_map/unproject/pallas_call | solution.py:671
  350.8 18.2 %collective-permute-start.22 = (bf16[2,4,192,384]{3,2,1,0:T(8,128)(2,1)}, bf16[2,4,192,384]{3,2,1,0:T(8,128)(2,1)S(1)}, u32[]{:S(2)}, u32[]{:S(2)}) collective-permute-start(bf16[2,4,192,384]{3,2,1,0:T(8,128)(2,1)} %get-tuple-element.154), channel_id=1, source_target_pairs={{0,8},{8,0},{16,24},{24,16},{1,9},{9,1},{17,25},{25,17},{2,10},{10... | collective-permute-start | bytes 3538952 | tf_op jit(solution)/shard_map/ppermute | solution.py:35
  369.0 5.6 %all-to-all-start.8 = ((bf16[4,192,384]{2,1,0:T(8,128)(2,1)}), bf16[4,192,384]{2,1,0:T(8,128)(2,1)S(1)}, u32[]{:S(2)}, u32[]{:S(2)}) async-start(bf16[4,192,384]{2,1,0:T(8,128)(2,1)} %merge.5), calls=%async_computation.8 | async-start | bytes 1179648 | tf_op jit(solution)/shard_map/all_to_all | solution.py:48
  375.8 9.3 %collective-permute-done.18 = bf16[384,384]{1,0:T(8,128)(2,1)S(1)} collective-permute-done((bf16[384,384]{1,0:T(8,128)(2,1)}, bf16[384,384]{1,0:T(8,128)(2,1)S(1)}, u32[]{:S(2)}, u32[]{:S(2)}) %collective-permute-start.18) | collective-permute-done | bytes 294944 | tf_op jit(solution)/shard_map/ppermute | solution.py:31
  387.2 11.5 %all-to-all-done.8.refs_0_ = bf16[4,192,384]{2,1,0:T(8,128)(2,1)S(1)} async-done(((bf16[4,192,384]{2,1,0:T(8,128)(2,1)}), bf16[4,192,384]{2,1,0:T(8,128)(2,1)S(1)}, u32[]{:S(2)}, u32[]{:S(2)}) %all-to-all-start.8) | async-done | bytes 589856 | tf_op jit(solution)/shard_map/all_to_all | solution.py:48
  399.4 4.0 unproject.3
  403.5 2.0 fusion.12
  408.3 4.5 collective-permute-start.25
  415.4 2.9 collective-permute-start.29
  419.6 2.3 collective-permute-start.27
  421.9 1.7 fusion.11
  426.9 1.9 fusion.17
  428.8 2.0 add_convert_fusion
  430.8 5.6 %all-to-all-start.10 = ((bf16[4,192,384]{2,1,0:T(8,128)(2,1)}), bf16[4,192,384]{2,1,0:T(8,128)(2,1)S(1)}, u32[]{:S(2)}, u32[]{:S(2)}) async-start(bf16[4,192,384]{2,1,0:T(8,128)(2,1)} %add_convert_fusion), calls=%async_computation.10 | async-start | bytes 1179648 | tf_op jit(solution)/shard_map/all_to_all | solution.py:48
  437.8 6.7 %collective-permute-done.30 = bf16[4,96,384]{2,1,0:T(8,128)(2,1)S(1)} collective-permute-done((bf16[4,96,384]{2,1,0:T(8,128)(2,1)}, bf16[4,96,384]{2,1,0:T(8,128)(2,1)S(1)}, u32[]{:S(2)}, u32[]{:S(2)}) %collective-permute-start.30) | collective-permute-done | bytes 294944 | tf_op jit(solution)/shard_map/ppermute | solution.py:31
  445.2 3.6 all-to-all-done.10
  448.8 6.4 %all-to-all-start.9 = ((bf16[4,96,384]{2,1,0:T(8,128)(2,1)}), bf16[4,96,384]{2,1,0:T(8,128)(2,1)S(1)}, u32[]{:S(2)}, u32[]{:S(2)}) async-start(bf16[4,96,384]{2,1,0:T(8,128)(2,1)} %add_convert_fusion.3), calls=%async_computation.9 | async-start | bytes 589824 | tf_op jit(solution)/shard_map/all_to_all | solution.py:48
  457.8 3.8 all-to-all-done.9
  461.9 2.2 multiply_add_fusion
  466.7 6.4 %collective-permute-start.33 = (f32[96,384]{1,0:T(8,128)S(1)}, f32[96,384]{1,0:T(8,128)S(1)}, u32[]{:S(2)}, u32[]{:S(2)}) collective-permute-start(f32[96,384]{1,0:T(8,128)S(1)} %add.258), channel_id=1, source_target_pairs={{0,8},{8,0},{16,24},{24,16},{1,9},{9,1},{17,25},{25,17},{2,10},{10... | collective-permute-start | bytes 442376 | tf_op jit(solution)/shard_map/ppermute | solution.py:35
  474.3 6.3 %collective-permute-done.34 = f32[192,384]{1,0:T(8,128)S(1)} collective-permute-done((f32[192,384]{1,0:T(8,128)S(1)}, f32[192,384]{1,0:T(8,128)S(1)}, u32[]{:S(2)}, u32[]{:S(2)}) %collective-permute-start.34) | collective-permute-done | bytes 294944 | tf_op jit(solution)/shard_map/ppermute | solution.py:35
  480.6 2.5 collective-permute-start.35
  (262 shorter events, 71.9 us)
Async XLA Ops:
  7.2 189.4 %all-gather.6.cloned.1.call-start = ((), (), s32[]{:S(2)}) async-start(), calls=%async_computation.14 | async-start | bytes 11354112 | tf_op jit(solution)/shard_map/all_gather | solution.py:751
  8.3 15.5 %copy-start.48 = (bf16[768]{0:T(1024)(128)(2,1)S(1)}, bf16[768]{0:T(1024)(128)(2,1)}, u32[]{:S(2)}) copy-start(bf16[768]{0:T(1024)(128)(2,1)} %param.25) | copy-start | bytes 4612
  8.3 3.9 collective-permute-start
  9.7 4.4 collective-permute-start.1
  10.7 7.4 %collective-permute-start.2 = (bf16[96,384]{1,0:T(8,128)(2,1)S(1)}, bf16[96,384]{1,0:T(8,128)(2,1)S(1)}, u32[]{:S(2)}, u32[]{:S(2)}) collective-permute-start(bf16[96,384]{1,0:T(8,128)(2,1)S(1)} %constant_dynamic-slice_fusion.6), channel_id=1, source_target_pairs={{0,3},{1,0},{2,1},{3,2},{4,7},{5,4},{6,5},{7,6},{8,11},{9,8},{10,9... | collective-permute-start | bytes 221192 | tf_op jit(solution)/shard_map/ppermute | solution.py:44
  18.2 26.5 %copy-start.10 = (bf16[4,96,384]{2,1,0:T(8,128)(2,1)}, bf16[4,96,384]{2,1,0:T(8,128)(2,1)S(1)}, u32[]{:S(2)}) copy-start(bf16[4,96,384]{2,1,0:T(8,128)(2,1)S(1)} %pad_maximum_fusion.9.refs_0_) | copy-start | bytes 884740
  18.2 8.1 %collective-permute-start.6 = (bf16[4,96,384]{2,1,0:T(8,128)(2,1)S(1)}, bf16[4,96,384]{2,1,0:T(8,128)(2,1)S(1)}, u32[]{:S(2)}, u32[]{:S(2)}) collective-permute-start(bf16[4,96,384]{2,1,0:T(8,128)(2,1)S(1)} %pad_maximum_fusion.9.refs_0_), channel_id=1, source_target_pairs={{0,4},{4,0},{1,5},{5,1},{2,6},{6,2},{3,7},{7,3},{8,12},{12,8},{9,1... | collective-permute-start | bytes 884744 | tf_op jit(solution)/shard_map/ppermute | solution.py:31
  19.3 7.0 %collective-permute-start.3 = (bf16[192,384]{1,0:T(8,128)(2,1)S(1)}, bf16[192,384]{1,0:T(8,128)(2,1)S(1)}, u32[]{:S(2)}, u32[]{:S(2)}) collective-permute-start(bf16[192,384]{1,0:T(8,128)(2,1)S(1)} %bitcast.93), channel_id=1, source_target_pairs={{0,1},{1,2},{2,3},{3,0},{4,5},{5,6},{6,7},{7,4},{8,9},{9,10},{10,1... | collective-permute-start | bytes 442376 | tf_op jit(solution)/shard_map/ppermute | solution.py:44
  19.4 11.6 %collective-permute-start.4 = (bf16[192,384]{1,0:T(8,128)(2,1)S(1)}, bf16[192,384]{1,0:T(8,128)(2,1)S(1)}, u32[]{:S(2)}, u32[]{:S(2)}) collective-permute-start(bf16[192,384]{1,0:T(8,128)(2,1)S(1)} %bitcast.94), channel_id=1, source_target_pairs={{0,2},{1,3},{2,0},{3,1},{4,6},{5,7},{6,4},{7,5},{8,10},{9,11},{10,... | collective-permute-start | bytes 442376 | tf_op jit(solution)/shard_map/ppermute | solution.py:44
  21.1 13.8 %collective-permute-start.5 = (bf16[192,384]{1,0:T(8,128)(2,1)S(1)}, bf16[192,384]{1,0:T(8,128)(2,1)S(1)}, u32[]{:S(2)}, u32[]{:S(2)}) collective-permute-start(bf16[192,384]{1,0:T(8,128)(2,1)S(1)} %bitcast.95), channel_id=1, source_target_pairs={{0,3},{1,0},{2,1},{3,2},{4,7},{5,4},{6,5},{7,6},{8,11},{9,8},{10,9... | collective-permute-start | bytes 442376 | tf_op jit(solution)/shard_map/ppermute | solution.py:44
  26.3 21.1 %copy-start.30 = (bf16[4,96,384]{2,1,0:T(8,128)(2,1)}, bf16[4,96,384]{2,1,0:T(8,128)(2,1)S(1)}, u32[]{:S(2)}) copy-start(bf16[4,96,384]{2,1,0:T(8,128)(2,1)S(1)} %collective-permute-done.6.refs_1_) | copy-start | bytes 884740
  35.0 23.7 %copy-start.15 = (bf16[4,192,384]{2,1,0:T(8,128)(2,1)}, bf16[4,192,384]{2,1,0:T(8,128)(2,1)S(1)}, u32[]{:S(2)}) copy-start(bf16[4,192,384]{2,1,0:T(8,128)(2,1)S(1)} %pad_maximum_fusion.4.refs_0_) | copy-start | bytes 1769476
  35.8 12.5 %copy-start.2 = (bf16[384,384]{1,0:T(8,128)(2,1)}, bf16[384,384]{1,0:T(8,128)(2,1)S(1)}, u32[]{:S(2)}) copy-start(bf16[384,384]{1,0:T(8,128)(2,1)S(1)} %get-tuple-element.204.x_own) | copy-start | bytes 884740
  35.8 11.1 %collective-permute-start.8 = (bf16[384,384]{1,0:T(8,128)(2,1)}, bf16[384,384]{1,0:T(8,128)(2,1)S(1)}, u32[]{:S(2)}, u32[]{:S(2)}) collective-permute-start(bf16[384,384]{1,0:T(8,128)(2,1)} %get-tuple-element.205), channel_id=1, source_target_pairs={{0,4},{4,0},{1,5},{5,1},{2,6},{6,2},{3,7},{7,3},{8,12},{12,8},{9,1... | collective-permute-start | bytes 884744 | tf_op jit(solution)/shard_map/ppermute | solution.py:31
  37.5 7.1 %collective-permute-start.9 = (f32[9,384]{1,0:T(8,128)S(1)}, f32[9,384]{1,0:T(8,128)S(1)}, u32[]{:S(2)}, u32[]{:S(2)}) collective-permute-start(f32[9,384]{1,0:T(8,128)S(1)} %pad_maximum_fusion.14), channel_id=1, source_target_pairs={{0,4},{4,0},{1,5},{5,1},{2,6},{6,2},{3,7},{7,3},{8,12},{12,8},{9,1... | collective-permute-start | bytes 41480 | tf_op jit(solution)/shard_map/ppermute | solution.py:31
  44.7 4.7 collective-permute-start.10
  47.4 2.0 collective-permute-start.11
  47.5 14.6 %collective-permute-start.7 = (bf16[4,192,384]{2,1,0:T(8,128)(2,1)S(1)}, bf16[4,192,384]{2,1,0:T(8,128)(2,1)}, u32[]{:S(2)}, u32[]{:S(2)}) collective-permute-start(bf16[4,192,384]{2,1,0:T(8,128)(2,1)S(1)} %pad_maximum_fusion.4.refs_0_), channel_id=1, source_target_pairs={{0,4},{4,0},{1,5},{5,1},{2,6},{6,2},{3,7},{7,3},{8,12},{12,8},{9,1... | collective-permute-start | bytes 1769480 | tf_op jit(solution)/shard_map/ppermute | solution.py:31
  55.2 25.5 %all-to-all-start = ((bf16[4,192,384]{2,1,0:T(8,128)(2,1)}), bf16[4,192,384]{2,1,0:T(8,128)(2,1)S(1)}, u32[]{:S(2)}, u32[]{:S(2)}) async-start(bf16[4,192,384]{2,1,0:T(8,128)(2,1)} %get-tuple-element.105), calls=%async_computation | async-start | bytes 1179648 | tf_op jit(solution)/shard_map/all_to_all | solution.py:48
  58.7 4.8 collective-permute-start.12
  62.1 3.3 collective-permute-start.13
  81.4 42.5 %all-to-all-start.1 = ((bf16[4,384,384]{2,1,0:T(8,128)(2,1)}), bf16[4,384,384]{2,1,0:T(8,128)(2,1)S(1)}, u32[]{:S(2)}, u32[]{:S(2)}) async-start(bf16[4,384,384]{2,1,0:T(8,128)(2,1)} %get-tuple-element.109), calls=%async_computation.1 | async-start | bytes 2359296 | tf_op jit(solution)/shard_map/all_to_all | solution.py:48
  89.3 7.3 %collective-permute-start.14 = (bf16[4,128,384]{2,1,0:T(8,128)(2,1)}, bf16[4,128,384]{2,1,0:T(8,128)(2,1)S(1)}, u32[]{:S(2)}, u32[]{:S(2)}) collective-permute-start(bf16[4,128,384]{2,1,0:T(8,128)(2,1)} %pack.3), channel_id=1, source_target_pairs={{0,4},{4,0},{1,5},{5,1},{2,6},{6,2},{3,7},{7,3},{8,12},{12,8},{9,1... | collective-permute-start | bytes 1179656 | tf_op jit(solution)/shard_map/ppermute | solution.py:31
  127.0 6.8 %collective-permute-start.15 = (bf16[4,128,384]{2,1,0:T(8,128)(2,1)}, bf16[4,128,384]{2,1,0:T(8,128)(2,1)S(1)}, u32[]{:S(2)}, u32[]{:S(2)}) collective-permute-start(bf16[4,128,384]{2,1,0:T(8,128)(2,1)} %pack.4), channel_id=1, source_target_pairs={{0,4},{4,0},{1,5},{5,1},{2,6},{6,2},{3,7},{7,3},{8,12},{12,8},{9,1... | collective-permute-start | bytes 1179656 | tf_op jit(solution)/shard_map/ppermute | solution.py:31
  129.6 19.1 %collective-permute-start.16 = (bf16[4,128,384]{2,1,0:T(8,128)(2,1)}, bf16[4,128,384]{2,1,0:T(8,128)(2,1)S(1)}, u32[]{:S(2)}, u32[]{:S(2)}) collective-permute-start(bf16[4,128,384]{2,1,0:T(8,128)(2,1)} %pack.5), channel_id=1, source_target_pairs={{0,4},{4,0},{1,5},{5,1},{2,6},{6,2},{3,7},{7,3},{8,12},{12,8},{9,1... | collective-permute-start | bytes 1179656 | tf_op jit(solution)/shard_map/ppermute | solution.py:31
  163.2 24.8 %copy-start.20 = (bf16[768,384]{1,0:T(8,128)(2,1)S(1)}, bf16[768,384]{1,0:T(8,128)(2,1)}, u32[]{:S(2)}) copy-start(bf16[768,384]{1,0:T(8,128)(2,1)} %param.15) | copy-start | bytes 1769476
  183.8 12.8 %all-to-all-start.2 = ((bf16[4,128,384]{2,1,0:T(8,128)(2,1)}), bf16[4,128,384]{2,1,0:T(8,128)(2,1)S(1)}, u32[]{:S(2)}, u32[]{:S(2)}) async-start(bf16[4,128,384]{2,1,0:T(8,128)(2,1)} %get-tuple-element.118), calls=%async_computation.2 | async-start | bytes 786432 | tf_op jit(solution)/shard_map/all_to_all | solution.py:48
  188.0 268.5 %reduce-scatter.2.cloned.1.call-start = ((), (), s32[]{:S(2)}) async-start(), calls=%async_computation.12 | async-start | bytes 11354112 | tf_op jit(solution)/shard_map/reduce_scatter | solution.py:809
  188.8 7.8 %collective-permute-start.17 = (bf16[384,384]{1,0:T(8,128)(2,1)S(1)}, bf16[384,384]{1,0:T(8,128)(2,1)S(1)}, u32[]{:S(2)}, u32[]{:S(2)}) collective-permute-start(bf16[384,384]{1,0:T(8,128)(2,1)S(1)} %get-tuple-element.202), channel_id=1, source_target_pairs={{0,4},{4,0},{1,5},{5,1},{2,6},{6,2},{3,7},{7,3},{8,12},{12,8},{9,1... | collective-permute-start | bytes 884744 | tf_op jit(solution)/shard_map/ppermute | solution.py:31
  235.7 9.7 %all-to-all-start.4 = ((bf16[4,64,384]{2,1,0:T(8,128)(2,1)}), bf16[4,64,384]{2,1,0:T(8,128)(2,1)S(1)}, u32[]{:S(2)}, u32[]{:S(2)}) async-start(bf16[4,64,384]{2,1,0:T(8,128)(2,1)} %get-tuple-element.132), calls=%async_computation.4 | async-start | bytes 393216 | tf_op jit(solution)/shard_map/all_to_all | solution.py:48
  245.4 24.0 %all-to-all-start.5 = ((bf16[4,128,384]{2,1,0:T(8,128)(2,1)}), bf16[4,128,384]{2,1,0:T(8,128)(2,1)S(1)}, u32[]{:S(2)}, u32[]{:S(2)}) async-start(bf16[4,128,384]{2,1,0:T(8,128)(2,1)} %get-tuple-element.136), calls=%async_computation.5 | async-start | bytes 786432 | tf_op jit(solution)/shard_map/all_to_all | solution.py:48
  264.8 22.8 %collective-permute-start.19 = (bf16[4,128,384]{2,1,0:T(8,128)(2,1)}, bf16[4,128,384]{2,1,0:T(8,128)(2,1)S(1)}, u32[]{:S(2)}, u32[]{:S(2)}) collective-permute-start(bf16[4,128,384]{2,1,0:T(8,128)(2,1)} %get-tuple-element.134), channel_id=1, source_target_pairs={{0,4},{4,0},{1,5},{5,1},{2,6},{6,2},{3,7},{7,3},{8,12},{12,8},{9,1... | collective-permute-start | bytes 1179656 | tf_op jit(solution)/shard_map/ppermute | solution.py:31
  286.0 24.8 %collective-permute-start.20 = (bf16[4,128,384]{2,1,0:T(8,128)(2,1)}, bf16[4,128,384]{2,1,0:T(8,128)(2,1)S(1)}, u32[]{:S(2)}, u32[]{:S(2)}) collective-permute-start(bf16[4,128,384]{2,1,0:T(8,128)(2,1)} %get-tuple-element.138), channel_id=1, source_target_pairs={{0,4},{4,0},{1,5},{5,1},{2,6},{6,2},{3,7},{7,3},{8,12},{12,8},{9,1... | collective-permute-start | bytes 1179656 | tf_op jit(solution)/shard_map/ppermute | solution.py:31
  290.7 23.1 %all-to-all-start.7 = ((bf16[4,192,384]{2,1,0:T(8,128)(2,1)}), bf16[4,192,384]{2,1,0:T(8,128)(2,1)S(1)}, u32[]{:S(2)}, u32[]{:S(2)}) async-start(bf16[4,192,384]{2,1,0:T(8,128)(2,1)} %merge.3), calls=%async_computation.7 | async-start | bytes 1179648 | tf_op jit(solution)/shard_map/all_to_all | solution.py:48
  313.8 14.6 %copy-start.16 = (bf16[4,192,384]{2,1,0:T(8,128)(2,1)}, bf16[4,192,384]{2,1,0:T(8,128)(2,1)S(1)}, u32[]{:S(2)}) copy-start(bf16[4,192,384]{2,1,0:T(8,128)(2,1)S(1)} %all-to-all-done.7.refs_1_) | copy-start | bytes 1769476
  313.8 30.2 %all-to-all-start.6 = ((bf16[4,192,384]{2,1,0:T(8,128)(2,1)}), bf16[4,192,384]{2,1,0:T(8,128)(2,1)S(1)}, u32[]{:S(2)}, u32[]{:S(2)}) async-start(bf16[4,192,384]{2,1,0:T(8,128)(2,1)} %merge.4), calls=%async_computation.6 | async-start | bytes 1179648 | tf_op jit(solution)/shard_map/all_to_all | solution.py:48
  318.3 7.1 %collective-permute-start.21 = (bf16[4,128,384]{2,1,0:T(8,128)(2,1)S(1)}, bf16[4,128,384]{2,1,0:T(8,128)(2,1)S(1)}, u32[]{:S(2)}, u32[]{:S(2)}) collective-permute-start(bf16[4,128,384]{2,1,0:T(8,128)(2,1)S(1)} %copy-done.53), channel_id=1, source_target_pairs={{0,4},{4,0},{1,5},{5,1},{2,6},{6,2},{3,7},{7,3},{8,12},{12,8},{9,1... | collective-permute-start | bytes 1179656 | tf_op jit(solution)/shard_map/ppermute | solution.py:31
  350.8 34.3 %copy-start.31 = (bf16[384,384]{1,0:T(8,128)(2,1)S(1)}, bf16[384,384]{1,0:T(8,128)(2,1)}, u32[]{:S(2)}) copy-start(bf16[384,384]{1,0:T(8,128)(2,1)} %get-tuple-element.121) | copy-start | bytes 884740
  350.8 35.2 %copy-start.9 = (bf16[2,4,192,384]{3,2,1,0:T(8,128)(2,1)S(1)}, bf16[2,4,192,384]{3,2,1,0:T(8,128)(2,1)}, u32[]{:S(2)}) copy-start(bf16[2,4,192,384]{3,2,1,0:T(8,128)(2,1)} %get-tuple-element.153) | copy-start | bytes 3538948
  350.8 35.2 %collective-permute-start.22 = (bf16[2,4,192,384]{3,2,1,0:T(8,128)(2,1)}, bf16[2,4,192,384]{3,2,1,0:T(8,128)(2,1)S(1)}, u32[]{:S(2)}, u32[]{:S(2)}) collective-permute-start(bf16[2,4,192,384]{3,2,1,0:T(8,128)(2,1)} %get-tuple-element.154), channel_id=1, source_target_pairs={{0,8},{8,0},{16,24},{24,16},{1,9},{9,1},{17,25},{25,17},{2,10},{10... | collective-permute-start | bytes 3538952 | tf_op jit(solution)/shard_map/ppermute | solution.py:35
  369.0 29.6 %all-to-all-start.8 = ((bf16[4,192,384]{2,1,0:T(8,128)(2,1)}), bf16[4,192,384]{2,1,0:T(8,128)(2,1)S(1)}, u32[]{:S(2)}, u32[]{:S(2)}) async-start(bf16[4,192,384]{2,1,0:T(8,128)(2,1)} %merge.5), calls=%async_computation.8 | async-start | bytes 1179648 | tf_op jit(solution)/shard_map/all_to_all | solution.py:48
  374.6 10.5 %collective-permute-start.18 = (bf16[384,384]{1,0:T(8,128)(2,1)}, bf16[384,384]{1,0:T(8,128)(2,1)S(1)}, u32[]{:S(2)}, u32[]{:S(2)}) collective-permute-start(bf16[384,384]{1,0:T(8,128)(2,1)} %get-tuple-element.122), channel_id=1, source_target_pairs={{0,4},{4,0},{1,5},{5,1},{2,6},{6,2},{3,7},{7,3},{8,12},{12,8},{9,1... | collective-permute-start | bytes 884744 | tf_op jit(solution)/shard_map/ppermute | solution.py:31
  387.2 16.3 %copy-start.3 = (bf16[384,384]{1,0:T(8,128)(2,1)S(1)}, bf16[384,384]{1,0:T(8,128)(2,1)}, u32[]{:S(2)}) copy-start(bf16[384,384]{1,0:T(8,128)(2,1)} %copy-done.2) | copy-start | bytes 884740
  387.2 16.3 %copy-start.6 = (bf16[384,384]{1,0:T(8,128)(2,1)S(1)}, bf16[384,384]{1,0:T(8,128)(2,1)}, u32[]{:S(2)}) copy-start(bf16[384,384]{1,0:T(8,128)(2,1)} %copy-done.5) | copy-start | bytes 884740
  387.2 16.3 %copy-start.8 = (f32[384,768]{1,0:T(8,128)S(1)}, f32[384,768]{1,0:T(8,128)}, u32[]{:S(2)}) copy-start(f32[384,768]{1,0:T(8,128)} %get-tuple-element.152) | copy-start | bytes 3538948
  405.5 12.9 %copy-start.41 = (f32[384]{0:T(512)S(1)}, f32[384]{0:T(512)}, u32[]{:S(2)}) copy-start(f32[384]{0:T(512)} %param.23) | copy-start | bytes 4612
  405.5 12.9 %copy-start.43 = (f32[384]{0:T(512)S(1)}, f32[384]{0:T(512)}, u32[]{:S(2)}) copy-start(f32[384]{0:T(512)} %param.20) | copy-start | bytes 4612
  405.5 12.9 %copy-start.44 = (f32[1,384]{1,0:T(1,128)S(1)}, f32[1,384]{1,0:T(1,128)}, u32[]{:S(2)}) copy-start(f32[1,384]{1,0:T(1,128)} %broadcast_in_dim.36) | copy-start | bytes 4612
  405.6 2.8 collective-permute-start.24
  408.1 20.7 %collective-permute-start.31 = (bf16[4,192,384]{2,1,0:T(8,128)(2,1)}, bf16[4,192,384]{2,1,0:T(8,128)(2,1)}, u32[]{:S(2)}, u32[]{:S(2)}) collective-permute-start(bf16[4,192,384]{2,1,0:T(8,128)(2,1)} %get-tuple-element.192), channel_id=1, source_target_pairs={{0,4},{4,0},{1,5},{5,1},{2,6},{6,2},{3,7},{7,3},{8,12},{12,8},{9,1... | collective-permute-start | bytes 1769480 | tf_op jit(solution)/shard_map/ppermute | solution.py:31
  408.3 6.0 %collective-permute-start.25 = (f32[7,384]{1,0:T(8,128)S(1)}, f32[7,384]{1,0:T(8,128)S(1)}, u32[]{:S(2)}, u32[]{:S(2)}) collective-permute-start(f32[7,384]{1,0:T(8,128)S(1)} %slice_add_fusion), channel_id=1, source_target_pairs={{0,1},{1,0},{2,3},{3,2},{4,5},{5,4},{6,7},{7,6},{8,9},{9,8},{10,11... | collective-permute-start | bytes 32264 | tf_op jit(solution)/shard_map/ppermute | solution.py:39
  414.3 4.0 collective-permute-start.26
  415.4 11.4 %collective-permute-start.29 = (bf16[2,4,96,384]{3,2,1,0:T(8,128)(2,1)}, bf16[2,4,96,384]{3,2,1,0:T(8,128)(2,1)}, u32[]{:S(2)}, u32[]{:S(2)}) collective-permute-start(bf16[2,4,96,384]{3,2,1,0:T(8,128)(2,1)} %get-tuple-element.160), channel_id=1, source_target_pairs={{0,8},{8,0},{16,24},{24,16},{1,9},{9,1},{17,25},{25,17},{2,10},{10... | collective-permute-start | bytes 1769480 | tf_op jit(solution)/shard_map/ppermute | solution.py:35
  419.6 5.2 %collective-permute-start.27 = (f32[1,10,384]{2,1,0:T(8,128)}, f32[1,10,384]{2,1,0:T(8,128)S(1)}, u32[]{:S(2)}, u32[]{:S(2)}) collective-permute-start(f32[1,10,384]{2,1,0:T(8,128)} %bitcast.21), channel_id=1, source_target_pairs={{0,8},{8,0},{16,24},{24,16},{1,9},{9,1},{17,25},{25,17},{2,10},{10... | collective-permute-start | bytes 46088 | tf_op jit(solution)/shard_map/ppermute | solution.py:35
  423.7 49.4 %collective-permute-start.23 = (f32[384,384]{1,0:T(8,128)S(1)}, f32[384,384]{1,0:T(8,128)S(1)}, u32[]{:S(2)}, u32[]{:S(2)}) collective-permute-start(f32[384,384]{1,0:T(8,128)S(1)} %slice.280), channel_id=1, source_target_pairs={{0,4},{4,0},{1,5},{5,1},{2,6},{6,2},{3,7},{7,3},{8,12},{12,8},{9,1... | collective-permute-start | bytes 1769480 | tf_op jit(solution)/shard_map/ppermute | solution.py:31
  425.6 10.8 %collective-permute-start.28 = (f32[2,10,384]{2,1,0:T(8,128)S(1)}, f32[2,10,384]{2,1,0:T(8,128)S(1)}, u32[]{:S(2)}, u32[]{:S(2)}) collective-permute-start(f32[2,10,384]{2,1,0:T(8,128)S(1)} %pad_maximum_fusion.13), channel_id=1, source_target_pairs={{0,16},{8,24},{16,0},{24,8},{1,17},{9,25},{17,1},{25,9},{2,18},{10... | collective-permute-start | bytes 92168 | tf_op jit(solution)/shard_map/ppermute | solution.py:35
  430.8 18.0 %all-to-all-start.10 = ((bf16[4,192,384]{2,1,0:T(8,128)(2,1)}), bf16[4,192,384]{2,1,0:T(8,128)(2,1)S(1)}, u32[]{:S(2)}, u32[]{:S(2)}) async-start(bf16[4,192,384]{2,1,0:T(8,128)(2,1)} %add_convert_fusion), calls=%async_computation.10 | async-start | bytes 1179648 | tf_op jit(solution)/shard_map/all_to_all | solution.py:48
  436.4 8.0 %collective-permute-start.30 = (bf16[4,96,384]{2,1,0:T(8,128)(2,1)}, bf16[4,96,384]{2,1,0:T(8,128)(2,1)S(1)}, u32[]{:S(2)}, u32[]{:S(2)}) collective-permute-start(bf16[4,96,384]{2,1,0:T(8,128)(2,1)} %get-tuple-element.196), channel_id=1, source_target_pairs={{0,4},{4,0},{1,5},{5,1},{2,6},{6,2},{3,7},{7,3},{8,12},{12,8},{9,1... | collective-permute-start | bytes 884744 | tf_op jit(solution)/shard_map/ppermute | solution.py:31
  448.8 12.8 %all-to-all-start.9 = ((bf16[4,96,384]{2,1,0:T(8,128)(2,1)}), bf16[4,96,384]{2,1,0:T(8,128)(2,1)S(1)}, u32[]{:S(2)}, u32[]{:S(2)}) async-start(bf16[4,96,384]{2,1,0:T(8,128)(2,1)} %add_convert_fusion.3), calls=%async_computation.9 | async-start | bytes 589824 | tf_op jit(solution)/shard_map/all_to_all | solution.py:48
  455.3 30.1 %all-gather.4.cloned.1.call-start = ((), (), s32[]{:S(2)}) async-start(), calls=%async_computation.13 | async-start | bytes 1720320 | tf_op jit(solution)/shard_map/all_gather | solution.py:877
  461.7 5.0 %collective-permute-start.32 = (f32[96,384]{1,0:T(8,128)S(1)}, f32[96,384]{1,0:T(8,128)S(1)}, u32[]{:S(2)}, u32[]{:S(2)}) collective-permute-start(f32[96,384]{1,0:T(8,128)S(1)} %convert_reduce_fusion.2), channel_id=1, source_target_pairs={{0,16},{8,24},{16,0},{24,8},{1,17},{9,25},{17,1},{25,9},{2,18},{10... | collective-permute-start | bytes 442376 | tf_op jit(solution)/shard_map/ppermute | solution.py:35
  465.3 15.2 %collective-permute-start.34 = (f32[192,384]{1,0:T(8,128)S(1)}, f32[192,384]{1,0:T(8,128)S(1)}, u32[]{:S(2)}, u32[]{:S(2)}) collective-permute-start(f32[192,384]{1,0:T(8,128)S(1)} %convert_reduce_fusion.1), channel_id=1, source_target_pairs={{0,16},{8,24},{16,0},{24,8},{1,17},{9,25},{17,1},{25,9},{2,18},{10... | collective-permute-start | bytes 884744 | tf_op jit(solution)/shard_map/ppermute | solution.py:35
  466.7 16.5 %collective-permute-start.33 = (f32[96,384]{1,0:T(8,128)S(1)}, f32[96,384]{1,0:T(8,128)S(1)}, u32[]{:S(2)}, u32[]{:S(2)}) collective-permute-start(f32[96,384]{1,0:T(8,128)S(1)} %add.258), channel_id=1, source_target_pairs={{0,8},{8,0},{16,24},{24,16},{1,9},{9,1},{17,25},{25,17},{2,10},{10... | collective-permute-start | bytes 442376 | tf_op jit(solution)/shard_map/ppermute | solution.py:35
  480.6 3.7 collective-permute-start.35
  (41 other events, 145.2 us)
Sparse Core Ops, SparseCore 0:
  35.1 108.3 all-gather.5
  235.9 184.5 reduce-scatter.1
  457.6 25.9 all-gather.3

commit v3 on v2

--- a/solution.py
+++ b/solution.py
@@ -35,6 +35,26 @@
     return lax.ppermute(value, "dp", [(i, i ^ (1 << bit)) for i in range(lax.axis_size("dp"))])
 
 
+def pair_moves(hop):
+    moves = []
+    for source in range(lax.axis_size("dp")):
+        for x in range(2):
+            target = (source & ~1) | (x ^ hop)
+            moves.append((2 * source + x, 2 * target + (source & 1)))
+    return moves
+
+
+def pair_to(first, second):
+    return [lax.ppermute(v, ("dp", "row"), pair_moves(hop)) for hop, v in enumerate((first, second))]
+
+
+def pair_from(first, second):
+    return [
+        lax.ppermute(v, ("dp", "row"), [(b, a) for a, b in pair_moves(hop)])
+        for hop, v in enumerate((first, second))
+    ]
+
+
 def col_swap(value, bit):
     return lax.ppermute(value, "col", [(i, i ^ (1 << bit)) for i in range(lax.axis_size("col"))])
 
@@ -79,7 +99,7 @@
     yield [own, other, own_far, dp_swap(other, 0)]
 
 
-def scatter_halves(mine, theirs, order):
+def scatter_halves(mine, theirs, order, hops):
     def added(first, second):
         return (first.astype(f32) + second.astype(f32)).astype(bf16)
 
@@ -92,7 +112,11 @@
     yield
     total = added(keep, order.next(heard))
     order.done(total)
-    parts = col_trade(total)
+    if hops:
+        size, col = lax.axis_size("col"), lax.axis_index("col")
+        parts = jnp.stack([col_from(total[lax.rem(col + k, size)], k) for k in range(size)])
+    else:
+        parts = col_trade(total)
     yield
     total = jnp.sum(order.next(parts).astype(f32), 0)
     order.done(total)
@@ -236,13 +260,13 @@
 
 
 def place_stripes(scalars, own_ref, offset, other_ref, keys, values_t, keys_t=None, values=None):
-    row = scalars[0]
+    side = scalars[2]
     count, _, width = own_ref.shape
     parts = width // LANES
     for place in range(count):
         for stripe, ref, base in (
-            (2 * place + row, own_ref.at[place], offset + HEAD),
-            (2 * place + 1 - row, other_ref.at[place], 0),
+            (2 * place + side, own_ref.at[place], offset + HEAD),
+            (2 * place + 1 - side, other_ref.at[place], 0),
         ):
             start = pl.multiple_of(stripe * width, LANES)
             key_t = ref[base : base + HEAD, :]
@@ -267,12 +291,12 @@
     before_ref, (out_ref, wide_ref, log_ref, keys, values_t) = refs[:earlier], refs[earlier:]
     count, _, width = own_ref.shape
     place_stripes(scalars, own_ref, offset, other_ref, keys, values_t)
-    row = scalars[0]
+    side = scalars[2]
 
     def stripe(place, _):
         query_t = own_ref[place, offset : offset + HEAD, :]
         limit = limit_ref[place]
-        first = (2 * place + row) * width
+        first = (2 * place + side) * width
 
         def step(masked, block, carry):
             top, total, mixed = carry
@@ -355,7 +379,7 @@
 ):
     count, _, width = own_ref.shape
     place_stripes(scalars, own_ref, offset, other_ref, keys, None, keys_t, values)
-    row = scalars[0]
+    side = scalars[2]
     d_keys[...] = jnp.zeros_like(d_keys)
     d_values[...] = jnp.zeros_like(d_values)
 
@@ -372,7 +396,7 @@
         drift = jnp.sum(grad_t.astype(f32) * wide_ref[place], 0, keepdims=True)
         log_sum = log_ref[place]
         limit = limit_ref[place]
-        stripe = 2 * place + row
+        stripe = 2 * place + side
 
         def step(masked, block, d_query):
             start = pl.multiple_of(block * KEYS, KEYS)
@@ -398,7 +422,7 @@
     lax.fori_loop(0, count, of_stripe, 0)
 
     def finish(place, _):
-        for stripe, ref in ((2 * place + row, d_own_ref), (2 * place + 1 - row, d_other_ref)):
+        for stripe, ref in ((2 * place + side, d_own_ref), (2 * place + 1 - side, d_other_ref)):
             start = pl.multiple_of(stripe * width, LANES)
             d_key = d_keys[pl.ds(start, width), :].T * HEAD ** (-0.5)
             ref[place, 0:HEAD, :] = turn_back(d_key, stripe).astype(ref.dtype)
@@ -695,8 +719,11 @@
     width = block_rows // 2
     slots = w_qkv.shape[0] // (3 * HEAD)
 
+    def relative(heard):
+        return in_order(core ^ row, *heard)
+
     def half_rows(block):
-        return half_at(block, row, 0), row_swap(half_at(block, 1 - row, 0))
+        return relative(pair_to(half_at(block, row, 0), half_at(block, 1 - row, 0)))
 
     x = half_rows(tokens)
 
@@ -716,8 +743,12 @@
 
     condition = embed_time(timestep[0].astype(f32))
     modulation = jnp.einsum("k,kjd->jd", condition, w_mod.astype(f32), precision=precise) + b_mod
-    small = jnp.concatenate([modulation, gain_attn[None], gain_mlp[None], b_down[None]], 0)
-    small = jnp.concatenate([small, row_swap(small)], 1)
+    known = jnp.concatenate([condition, piece_starts[0].astype(f32)])
+    known = jnp.pad(known, (0, part - known.shape[0]))
+    small = jnp.concatenate([modulation, gain_attn[None], gain_mlp[None], b_down[None], known[None]], 0)
+    small = jnp.concatenate(relative(pair_to(small, small)), 1)
+    condition = small[SMALL, :COND]
+    starts = small[SMALL, COND : COND + piece_starts.shape[1]].astype(jnp.int32)
 
     residual = jnp.concatenate(x, 1).astype(f32)
     centered = residual - jnp.mean(residual, -1, keepdims=True)
@@ -730,10 +761,9 @@
     places = jnp.arange(2 * cols, dtype=jnp.int32)[:, None] * width + lane[None]
     angles = places.astype(f32)[:, None, :] * frequency[None, :, None]
     turns = jnp.concatenate([jnp.cos(angles), jnp.sin(angles)], 1)
-    here = lax.dynamic_index_in_dim(turns, 2 * col + row, 0, keepdims=False)
-    own_stripes = 2 * jnp.arange(cols, dtype=jnp.int32) + row
+    here = lax.dynamic_index_in_dim(turns, 2 * col + core, 0, keepdims=False)
+    own_stripes = 2 * jnp.arange(cols, dtype=jnp.int32) + core
     own_places = own_stripes[:, None] * width + lane[None]
-    starts = piece_starts[0]
     inside = (own_places[..., None] >= starts) & (own_places[..., None] < starts + PIECE)
     limit = jnp.max(jnp.where(inside, starts + PIECE - 1, own_places[..., None]), -1)
     scalars = jnp.concatenate(
@@ -744,6 +774,7 @@
     soon = gather_halves(blocks[0], order)
     next(soon)
     next(soon)
+    order.done(*order.last, *x, small)
     late = gather_halves(order.next(blocks[1]), order)
     next(late)
     soon = next(soon)
@@ -762,19 +793,19 @@
 
     begin(0, soon)
     begin(1, next(late))
-    g = half_rows(after(cotangent, own[-1][0]))
+    g = half_rows(after(cotangent, w_groups[0]))
     forward, other = [], [None] * slots
     earlier = ()
 
     def share(slot):
         packed = pack(order.next(scalars), *own[slot])
         order.done(packed)
-        other[slot] = row_swap(packed)
+        other[slot] = dp_swap(packed, 0)
 
     share(0)
     for slot in range(slots):
         results = attend(order.next(scalars), *own[slot], other[slot], limit, earlier if slot < slots - 1 else ())
-        order.done(results[2])
+        order.done(results[2], *(g if slot == 1 else ()))
         forward.append(results)
         if slot < slots - 1:
             earlier = (results[0],)
@@ -782,7 +813,7 @@
             for later in range(1, slots):
                 share(later)
     first = col_trade(forward[slots - 2][0])
-    last = col_trade(forward[slots - 1][0])
+    last = col_trade(after(forward[slots - 1][0], first))
 
     kept = middle(order.next(scalars), x, g, small, first, last, rest, slots)
     (
@@ -801,15 +832,20 @@
     ) = kept
     order.done(d_middle)
 
+    def whole_rows(own_part, other_part):
+        return jnp.concatenate(in_order(row, *pair_from(*in_order(core ^ row, own_part, other_part))), 0)
+
     d_last = col_trade(d_last)
     grads = weight_grads(order.next(scalars), h_two, d_branch, d_attended, active, d_hidden, mixed, slots)
     order.done(grads)
+    grads = after(grads, d_last)
     extra = lax.axis_size("dp") - SLICES
     grads = jnp.pad(grads, ((0, extra),) + ((0, 0),) * 4) if extra else grads
     grads = lax.psum_scatter(
         grads.reshape((-1,) + grads.shape[3:]), ("dp", "row", "col"), scatter_dimension=0, tiled=True
     )
     d_first = col_trade(d_first)
+    block_out = whole_rows(block_own, block_other)
 
     back, shared = {}, {}
 
@@ -818,8 +854,8 @@
         d_query, d_own, d_other = attend_back(
             order.next(scalars), *own[slot], other[slot], *grad, *forward[slot][1:], limit, turns
         )
-        order.done(d_other)
-        shared[slot] = d_query, d_own, row_swap(d_other)
+        order.done(d_other, *((block_out,) if slot == slots - 2 else ()))
+        shared[slot] = d_query, d_own, dp_swap(d_other, 0)
 
     def send(slot):
         pieces = merge(order.next(scalars), *shared[slot])
@@ -834,7 +870,7 @@
         d_h, mine, theirs = unproject(order.next(scalars), h_one, w_groups[group], pieces)
         order.done(d_h)
         d_hs.append(d_h)
-        steps = scatter_halves(mine, theirs, order)
+        steps = scatter_halves(mine, theirs, order, group > 0)
         next(steps)
         return steps
 
@@ -844,6 +880,7 @@
             send(slot + 1)
     send(0)
     late = finish(1)
+    next(late)
     next(late)
     soon = finish(0)
     d_h_one = d_hs[0] + d_hs[1]
@@ -855,18 +892,37 @@
     sums = jnp.concatenate([jnp.sum(d_h_one, 0)[None], jnp.sum(d_h_one * normed, 0)[None], sums[:5]], 0)
 
     order.done(d_tokens, sums)
-
-    def whole_rows(own_part, other_part):
-        return jnp.concatenate(in_order(row, own_part, row_swap(other_part)), 0)
-
+    next(soon)
     tokens_out = whole_rows(d_tokens[:, :part], d_tokens[:, part:])
-    block_out = whole_rows(block_own, block_other)
-
+
+    sums = order.next(sums)
+    sums = sums + dp_swap(sums, 0)
+    for bit in range(bits("col")):
+        sums = sums + col_swap(sums, bit)
+        order.done(sums)
+        if bit == 0:
+            next(soon)
+            next(late)
+            sums = order.next(sums)
+    per_seq = jnp.concatenate(
+        [
+            sums[0:1],
+            sums[1:2] * small[GAIN_A],
+            sums[2:4],
+            sums[4:5] * small[GAIN_M],
+            sums[5:6],
+            sums[1:2] * (1.0 + small[SCALE_A]),
+            sums[4:5] * (1.0 + small[SCALE_M]),
+            sums[6:7],
+            jnp.tile(jnp.pad(condition, (0, part - COND)), 2)[None],
+        ],
+        0,
+    )[None]
+    per_seq = jnp.concatenate(in_order(row, per_seq[..., :part], row_swap(per_seq[..., part:])), 0)
+    order.done(per_seq)
     next(soon)
-    next(late)
-    next(soon)
-    next(late)
-    next(soon)
+    for bit in range(1, bits("dp")):
+        per_seq = jnp.concatenate(in_order(dp_bit(bit), per_seq, dp_swap(per_seq, bit)), 0)
     late, soon = next(late), next(soon)
     d_qkv = []
     for (low, high), found in zip(groups, (soon, late)):
@@ -889,25 +945,6 @@
     )
     d_bias = jnp.concatenate([grads[c, rows + 2 * step] for c in range(2)], 0)
 
-    sums = sums[:, :part] + row_swap(sums[:, part:])
-    for bit in range(bits("col")):
-        sums = sums + col_swap(sums, bit)
-    per_seq = jnp.concatenate(
-        [
-            sums[0:1],
-            sums[1:2] * gain_attn,
-            sums[2:4],
-            sums[4:5] * gain_mlp,
-            sums[5:6],
-            sums[1:2] * (1.0 + modulation[1]),
-            sums[4:5] * (1.0 + modulation[4]),
-            sums[6:7],
-            jnp.pad(condition, (0, part - COND))[None],
-        ],
-        0,
-    )[None]
-    for bit in range(bits("dp")):
-        per_seq = jnp.concatenate(in_order(dp_bit(bit), per_seq, dp_swap(per_seq, bit)), 0)
     conditions = per_seq[:, SMALL, :COND]
     d_mod_w = sum(conditions[s][:, None, None] * per_seq[s, :6][None] for s in range(per_seq.shape[0]))
     totals = jnp.sum(per_seq[:, :SMALL], 0)

time: 501 us -> 477 us (0.952)
  blocking collectives: 20.6 us -> 0 us
  Pallas kernels: 160 us -> 170 us
  starting transfers between devices: 120 us -> 112 us
  other arithmetic: 29.8 us -> 24.3 us
    all_to_all x1 -> x0, blocking collectives: 20.6 us -> none  [col_trade(): return lax.all_to_all(value, 'col', 0, 0, tiled=True)]
    ppermute x12 -> x18, starting transfers between devices: 39.4 us -> 20.4 us  [dp_swap(): lax.ppermute(value, 'dp', [(i, i ^ 1 << bit) for i in range(lax.axis_size...]
    ppermute x16 -> x5, waiting for transfers between devices: 42.7 us -> 23.9 us  [row_swap(): return lax.ppermute(value, 'row', [(0, 1), (1, 0)])]
    ppermute x0 -> x10, starting transfers between devices: none -> 15.5 us  [the longest x6 8.4 us: pair_to(): lax.ppermute(v, ('dp', 'row'), pair_moves(hop))]
    ppermute x16 -> x5, starting transfers between devices: 19.6 us -> 6.03 us  [row_swap(): return lax.ppermute(value, 'row', [(0, 1), (1, 0)])]
    ppermute x6 -> x9, waiting for transfers between devices: 14.5 us -> 22.3 us  [col_from(): lax.ppermute(value, 'col', [(i, (i + hop) % size) for i in range(size)])]
    ppermute x6 -> x9, starting transfers between devices: 6.4 us -> 14.1 us  [col_from(): lax.ppermute(value, 'col', [(i, (i + hop) % size) for i in range(size)])]
    ppermute x0 -> x10, waiting for transfers between devices: none -> 5.64 us  [the longest x6 5.63 us: pair_to(): lax.ppermute(v, ('dp', 'row'), pair_moves(hop))]
  transfers between devices with their start and end apart: 49 -> 57, of which waited for: 25 -> 24; matrix products, arithmetic and copies ran while one was open for 7% -> 5% of each run, Pallas kernels for 24% -> 31%
where the time goes in v3:
time: 477 us; the launch traced here: 472 us
  Pallas kernels  170 us (36%)
  waiting for transfers between devices  130 us (27%)
  starting transfers between devices  112 us (23%)
  other arithmetic  24.3 us (5%)
  local copies, waits for them, and re-layouts  20.1 us (4%)
  between operations  15.5 us (3%)
    all_to_all x10, waiting for transfers between devices, col_trade(): return lax.all_to_all(value, 'col', 0, 0, tiled=True)  56 us
    all_to_all x10, starting transfers between devices, col_trade(): return lax.all_to_all(value, 'col', 0, 0, tiled=True)  52.7 us
    pallas_call x3, Pallas kernels, attend_back(): pl.pallas_call(functools.partial(attend_back_kernel, offset, grad_offset)...  52.3 us
    pallas_call x3, Pallas kernels, attend(): pl.pallas_call(functools.partial(attend_kernel, offset, len(earlier)), in...  46.6 us
    ppermute x5, waiting for transfers between devices, row_swap(): return lax.ppermute(value, 'row', [(0, 1), (1, 0)])  23.9 us
    pallas_call x1, Pallas kernels, middle(): pl.pallas_call(functools.partial(middle_kernel, slots), in_specs=[SCALARS...  22.9 us
    ppermute x9, waiting for transfers between devices, col_from(): lax.ppermute(value, 'col', [(i, (i + hop) % size) for i in range(size)])  22.3 us
    ppermute x18, starting transfers between devices, dp_swap(): lax.ppermute(value, 'dp', [(i, i ^ 1 << bit) for i in range(lax.axis_size...  20.4 us
  transfers between devices with their start and end apart: 57, of which 24 were waited for; matrix products, arithmetic and copies ran while one was open for 5% of the time, Pallas kernels for 31%

profile of v3, /device:TPU:9, one launch (start us, length us, event | category | flops | bytes accessed | tf_op | source)
XLA Modules:
  0.0 472.5 jit_solution(16372724860294098775)
XLA Ops:
  13.1 3.7 collective-permute-start
  21.8 2.8 collective-permute-start.5
  25.3 2.3 collective-permute-done.4
  27.9 2.0 collective-permute-done.5
  29.9 3.6 collective-permute-done.6
  34.2 3.7 collective-permute-start.8
  40.7 6.5 %collective-permute-done.8 = bf16[192,384]{1,0:T(8,128)(2,1)S(1)} collective-permute-done((bf16[192,384]{1,0:T(8,128)(2,1)S(1)}, bf16[192,384]{1,0:T(8,128)(2,1)S(1)}, u32[]{:S(2)}, u32[]{:S(2)}) %collective-permute-start.8) | collective-permute-done | bytes 147488 | tf_op jit(solution)/shard_map/ppermute | solution.py:64
  47.2 2.9 collective-permute-done.9
  50.4 1.4 multiply_sine_fusion
  55.9 2.1 collective-permute-start.11
  59.8 4.4 project.2
  64.1 3.5 all-to-all-start
  68.4 5.4 %collective-permute-done.11.refs_1_ = bf16[4,192,384]{2,1,0:T(8,128)(2,1)} collective-permute-done((bf16[4,192,384]{2,1,0:T(8,128)(2,1)S(1)}, bf16[4,192,384]{2,1,0:T(8,128)(2,1)}, u32[]{:S(2)}, u32[]{:S(2)}) %collective-permute-start.11) | collective-permute-done | bytes 589856 | tf_op jit(solution)/shard_map/ppermute | solution.py:31
  74.8 1.8 collective-permute-done.15.refs_3_
  77.5 5.7 %project.3 = (bf16[2,768,768]{2,1,0:T(8,128)(2,1)}, bf16[4,384,384]{2,1,0:T(8,128)(2,1)}) custom-call(s32[7]{0:T(128)} %pad_add_fusion.scalars._, bf16[384,768]{1,0:T(8,128)(2,1)} %fusion.7.h_ref, f32[64,384]{1,0:T(8,128)} %fusion.19.turn_ref, bf16[4,192,384]{2,1,0:T(8,128)(2,1)} %copy-done.13, bf16[4,192,384]{2,1,0:T(8,128)(2,1)} %collective-permute-done.11.refs_1_, ...), custom_call_target="tpu_custom_call" | custom-call | flops 905969664 | bytes 6000000 | tf_op jit(solution)/shard_map/project/pallas_call | solution.py:213
  84.6 6.3 %all-to-all-start.1 = ((bf16[4,384,384]{2,1,0:T(8,128)(2,1)}), bf16[4,384,384]{2,1,0:T(8,128)(2,1)S(1)}, u32[]{:S(2)}, u32[]{:S(2)}) async-start(bf16[4,384,384]{2,1,0:T(8,128)(2,1)} %get-tuple-element.113), calls=%async_computation.1 | async-start | bytes 2359296 | tf_op jit(solution)/shard_map/all_to_all | solution.py:68
  91.0 1.9 pack.3
  95.2 1.9 collective-permute-start.18
  97.2 15.3 %attend.3 = (bf16[4,64,384]{2,1,0:T(8,128)(2,1)}, f32[4,64,384]{2,1,0:T(8,128)}, f32[4,1,384]{2,1,0:T(1,128)}) custom-call(s32[7]{0:T(128)} %pad_add_fusion.scalars._, bf16[4,192,384]{2,1,0:T(8,128)(2,1)} %copy-done.7, bf16[4,128,384]{2,1,0:T(8,128)(2,1)} %collective-permute-done.16.other_ref, s32[4,1,384]{2,1,0:T(1,128)} %broadcast_in_dim.33.limit_ref), custom_call_target="tpu_custom_call" | custom-call | flops 8000000000 | bytes 3000000 | tf_op jit(solution)/shard_map/attend/pallas_call | solution.py:342
  112.5 29.0 %all-to-all-done.1.own_ref = bf16[4,384,384]{2,1,0:T(8,128)(2,1)S(1)} async-done(((bf16[4,384,384]{2,1,0:T(8,128)(2,1)}), bf16[4,384,384]{2,1,0:T(8,128)(2,1)S(1)}, u32[]{:S(2)}, u32[]{:S(2)}) %all-to-all-start.1) | async-done | bytes 1179680 | tf_op jit(solution)/shard_map/all_to_all | solution.py:68
  142.5 2.1 pack.4
  146.5 2.1 pack.5
  149.3 15.8 %attend.4 = (bf16[4,128,384]{2,1,0:T(8,128)(2,1)}, f32[4,64,384]{2,1,0:T(8,128)}, f32[4,1,384]{2,1,0:T(1,128)}) custom-call(s32[7]{0:T(128)} %pad_add_fusion.scalars._, bf16[4,384,384]{2,1,0:T(8,128)(2,1)} %copy-done.6, bf16[4,128,384]{2,1,0:T(8,128)(2,1)} %copy-done.40, s32[4,1,384]{2,1,0:T(1,128)} %broadcast_in_dim.33.limit_ref, ...), custom_call_target="tpu_custom_call" | custom-call | flops 8000000000 | bytes 3000000 | tf_op jit(solution)/shard_map/attend/pallas_call | solution.py:342
  165.1 6.8 %all-to-all-start.2 = ((bf16[4,128,384]{2,1,0:T(8,128)(2,1)}), bf16[4,128,384]{2,1,0:T(8,128)(2,1)S(1)}, u32[]{:S(2)}, u32[]{:S(2)}) async-start(bf16[4,128,384]{2,1,0:T(8,128)(2,1)} %get-tuple-element.122), calls=%async_computation.2 | async-start | bytes 786432 | tf_op jit(solution)/shard_map/all_to_all | solution.py:68
  172.7 15.5 %attend.5 = (bf16[4,64,384]{2,1,0:T(8,128)(2,1)}, f32[4,64,384]{2,1,0:T(8,128)}, f32[4,1,384]{2,1,0:T(1,128)}) custom-call(s32[7]{0:T(128)} %pad_add_fusion.scalars._, bf16[4,384,384]{2,1,0:T(8,128)(2,1)} %copy-done.6, bf16[4,128,384]{2,1,0:T(8,128)(2,1)} %copy-done.41, s32[4,1,384]{2,1,0:T(1,128)} %broadcast_in_dim.33.limit_ref), custom_call_target="tpu_custom_call" | custom-call | flops 8000000000 | bytes 3000000 | tf_op jit(solution)/shard_map/attend/pallas_call | solution.py:342
  188.2 4.6 all-to-all-start.3
  192.8 4.9 %all-to-all-done.3.last_ref = bf16[4,64,384]{2,1,0:T(8,128)(2,1)S(1)} async-done(((bf16[4,64,384]{2,1,0:T(8,128)(2,1)}), bf16[4,64,384]{2,1,0:T(8,128)(2,1)S(1)}, u32[]{:S(2)}, u32[]{:S(2)}) %all-to-all-start.3) | async-done | bytes 196640 | tf_op jit(solution)/shard_map/all_to_all | solution.py:68
  198.4 22.9 %middle.1 = (bf16[384,384]{1,0:T(8,128)(2,1)}, bf16[384,384]{1,0:T(8,128)(2,1)}, f32[384,768]{1,0:T(8,128)}, bf16[384,768]{1,0:T(8,128)(2,1)}, bf16[384,768]{1,0...) custom-call(s32[7]{0:T(128)} %pad_add_fusion.scalars._, ...), custom_call_target="tpu_custom_call" | custom-call | flops 8153726976 | bytes 14000000 | tf_op jit(solution)/shard_map/middle/pallas_call | solution.py:591
  221.3 4.6 all-to-all-start.4
  225.9 15.3 %weight_grads.1 = bf16[4,2,4,448,384]{4,3,2,1,0:T(8,128)(2,1)} custom-call(s32[7]{0:T(128)} %pad_add_fusion.scalars._, bf16[384,768]{1,0:T(8,128)(2,1)} %get-tuple-element.130.h_ref, bf16[384,768]{1,0:T(8,128)(2,1)} %get-tuple-element.131.df_ref, bf16[384,768]{1,0:T(8,128)(2,1)} %get-tuple-element.132.d_att_ref, ...), custom_call_target="tpu_custom_call" | custom-call | flops 4076863488 | bytes 20000000 | tf_op jit(solution)/shard_map/weight_grads/pallas_call | solution.py:658
  242.8 4.5 all-to-all-start.5
  247.4 4.6 collective-permute-start.21
  252.0 17.5 %attend_back.3 = (bf16[4,64,384]{2,1,0:T(8,128)(2,1)}, f32[4,128,384]{2,1,0:T(8,128)}, bf16[4,128,384]{2,1,0:T(8,128)(2,1)}) custom-call(s32[7]{0:T(128)} %pad_add_fusion.scalars._, bf16[4,384,384]{2,1,0:T(8,128)(2,1)} %copy-done.6, bf16[4,128,384]{2,1,0:T(8,128)(2,1)} %copy-done.41, bf16[4,64,384]{2,1,0:T(8,128)(2,1)} %copy-done.31, ...), custom_call_target="tpu_custom_call" | custom-call | flops 16000000000 | bytes 4000000 | tf_op jit(solution)/shard_map/attend_back/pallas_call | solution.py:438
  271.3 17.6 %attend_back.4 = (bf16[4,64,384]{2,1,0:T(8,128)(2,1)}, f32[4,128,384]{2,1,0:T(8,128)}, bf16[4,128,384]{2,1,0:T(8,128)(2,1)}) custom-call(s32[7]{0:T(128)} %pad_add_fusion.scalars._, bf16[4,384,384]{2,1,0:T(8,128)(2,1)} %copy-done.6, bf16[4,128,384]{2,1,0:T(8,128)(2,1)} %copy-done.40, bf16[4,128,384]{2,1,0:T(8,128)(2,1)} %copy-done.18, ...), custom_call_target="tpu_custom_call" | custom-call | flops 16000000000 | bytes 4000000 | tf_op jit(solution)/shard_map/attend_back/pallas_call | solution.py:438
  289.6 2.2 merge.3
  291.8 4.5 all-to-all-start.7
  296.3 17.2 %attend_back.5 = (bf16[4,64,384]{2,1,0:T(8,128)(2,1)}, f32[4,128,384]{2,1,0:T(8,128)}, bf16[4,128,384]{2,1,0:T(8,128)(2,1)}) custom-call(s32[7]{0:T(128)} %pad_add_fusion.scalars._, bf16[4,192,384]{2,1,0:T(8,128)(2,1)} %copy-done.7, bf16[4,128,384]{2,1,0:T(8,128)(2,1)} %collective-permute-done.16.other_ref, bf16[4,128,384]{2,1,0:T(8,128)(2,1)} %copy-done.18, ...), custom_call_target="tpu_custom_call" | custom-call | flops 16000000000 | bytes 4000000 | tf_op jit(solution)/shard_map/attend_back/pallas_call | solution.py:438
  314.3 2.2 merge.4
  316.5 7.8 %all-to-all-done.7.refs_1_ = bf16[4,192,384]{2,1,0:T(8,128)(2,1)S(1)} async-done(((bf16[4,192,384]{2,1,0:T(8,128)(2,1)}), bf16[4,192,384]{2,1,0:T(8,128)(2,1)S(1)}, u32[]{:S(2)}, u32[]{:S(2)}) %all-to-all-start.7) | async-done | bytes 589856 | tf_op jit(solution)/shard_map/all_to_all | solution.py:68
  324.4 7.1 %all-to-all-start.6 = ((bf16[4,192,384]{2,1,0:T(8,128)(2,1)}), bf16[4,192,384]{2,1,0:T(8,128)(2,1)S(1)}, u32[]{:S(2)}, u32[]{:S(2)}) async-start(bf16[4,192,384]{2,1,0:T(8,128)(2,1)} %merge.4), calls=%async_computation.6 | async-start | bytes 1179648 | tf_op jit(solution)/shard_map/all_to_all | solution.py:68
  331.5 2.4 collective-permute-start.25
  336.0 2.2 merge.5
  338.2 10.9 %all-to-all-done.6.refs_0_ = bf16[4,192,384]{2,1,0:T(8,128)(2,1)S(1)} async-done(((bf16[4,192,384]{2,1,0:T(8,128)(2,1)}), bf16[4,192,384]{2,1,0:T(8,128)(2,1)S(1)}, u32[]{:S(2)}, u32[]{:S(2)}) %all-to-all-start.6) | async-done | bytes 589856 | tf_op jit(solution)/shard_map/all_to_all | solution.py:68
  350.0 6.0 %unproject.2 = (f32[384,768]{1,0:T(8,128)}, bf16[2,4,192,384]{3,2,1,0:T(8,128)(2,1)}, bf16[2,4,192,384]{3,2,1,0:T(8,128)(2,1)}) custom-call(s32[7]{0:T(128)} %pad_add_fusion.scalars._, bf16[384,768]{1,0:T(8,128)(2,1)} %fusion.7.h_ref, bf16[2,768,768]{2,1,0:T(8,128)(2,1)} %get-tuple-element.107.w_ref, bf16[4,192,384]{2,1,0:T(8,128)(2,1)} %copy-done.15, ...), custom_call_target="tpu_custom_call" | custom-call | flops 1811939328 | bytes 10000000 | tf_op jit(solution)/shard_map/unproject/pallas_call | solution.py:695
  356.8 7.4 %all-to-all-start.8 = ((bf16[4,192,384]{2,1,0:T(8,128)(2,1)}), bf16[4,192,384]{2,1,0:T(8,128)(2,1)}, u32[]{:S(2)}, u32[]{:S(2)}) async-start(bf16[4,192,384]{2,1,0:T(8,128)(2,1)} %merge.5), calls=%async_computation.8 | async-start | bytes 1179648 | tf_op jit(solution)/shard_map/all_to_all | solution.py:68
  367.0 17.0 %collective-permute-done.27 = bf16[4,192,384]{2,1,0:T(8,128)(2,1)S(1)} collective-permute-done((bf16[4,192,384]{2,1,0:T(8,128)(2,1)S(1)}, bf16[4,192,384]{2,1,0:T(8,128)(2,1)S(1)}, u32[]{:S(2)}, u32[]{:S(2)}) %collective-permute-start.27) | collective-permute-done | bytes 589856 | tf_op jit(solution)/shard_map/ppermute | solution.py:31
  384.2 2.7 all-to-all-done.8.refs_0_
  386.9 4.0 unproject.3
  390.9 2.0 fusion.12
  393.0 2.5 collective-permute-start.30
  396.9 4.6 collective-permute-start.34
  405.8 2.4 collective-permute-start.28
  408.2 5.6 %collective-permute-done.34 = bf16[192,384]{1,0:T(8,128)(2,1)S(1)} collective-permute-done((bf16[192,384]{1,0:T(8,128)(2,1)S(1)}, bf16[192,384]{1,0:T(8,128)(2,1)S(1)}, u32[]{:S(2)}, u32[]{:S(2)}) %collective-permute-start.34) | collective-permute-done | bytes 147488 | tf_op jit(solution)/shard_map/ppermute | solution.py:64
  413.8 2.7 collective-permute-start.32
  416.5 5.0 %collective-permute-done.35 = bf16[192,384]{1,0:T(8,128)(2,1)S(1)} collective-permute-done((bf16[192,384]{1,0:T(8,128)(2,1)S(1)}, bf16[192,384]{1,0:T(8,128)(2,1)S(1)}, u32[]{:S(2)}, u32[]{:S(2)}) %collective-permute-start.35) | collective-permute-done | bytes 147488 | tf_op jit(solution)/shard_map/ppermute | solution.py:64
  422.7 3.5 collective-permute-done.37
  431.5 3.4 all-to-all-start.9
  435.7 5.2 %collective-permute-done.42 = f32[192,384]{1,0:T(8,128)S(1)} collective-permute-done((f32[192,384]{1,0:T(8,128)S(1)}, f32[192,384]{1,0:T(8,128)S(1)}, u32[]{:S(2)}, u32[]{:S(2)}) %collective-permute-start.42) | collective-permute-done | bytes 294944 | tf_op jit(solution)/shard_map/ppermute | solution.py:35
  440.9 4.8 %collective-permute-start.43 = (f32[192,384]{1,0:T(8,128)S(1)}, f32[192,384]{1,0:T(8,128)S(1)}, u32[]{:S(2)}, u32[]{:S(2)}) collective-permute-start(f32[192,384]{1,0:T(8,128)S(1)} %add.281), channel_id=1, source_target_pairs={{0,8},{8,0},{16,24},{24,16},{1,9},{9,1},{17,25},{25,17},{2,10},{10... | collective-permute-start | bytes 884744 | tf_op jit(solution)/shard_map/ppermute | solution.py:35
  446.1 1.5 multiply_add_fusion
  448.8 3.2 collective-permute-done.40
  452.0 1.8 collective-permute-start.41
  455.8 4.8 %all-gather.4.cloned.1.call-done = bf16[4,448,384]{2,1,0:T(8,128)(2,1)} async-done(((bf16[1,448,384]{2,1,0:T(8,128)(2,1)}), bf16[4,448,384]{2,1,0:T(8,128)(2,1)}) %all-gather.4.cloned.1.call-update) | async-done | bytes 1376272 | tf_op jit(solution)/shard_map/all_gather | solution.py:933
  460.7 1.5 convert_element_type.161
  (265 shorter events, 63.7 us)
Async XLA Ops:
  7.2 190.5 %all-gather.6.cloned.1.call-start = ((), (), s32[]{:S(2)}) async-start(), calls=%async_computation.13 | async-start | bytes 11354112 | tf_op jit(solution)/shard_map/all_gather | solution.py:782
  13.1 8.7 %collective-permute-start = (f32[10,384]{1,0:T(8,128)S(1)}, f32[10,384]{1,0:T(8,128)S(1)}, u32[]{:S(2)}, u32[]{:S(2)}) collective-permute-start(f32[10,384]{1,0:T(8,128)S(1)} %concatenate.71), channel_id=1, source_target_pairs={{0,0},{4,8},{8,4},{12,12},{16,16},{20,24},{24,20},{28,28},{1,1},{5... | collective-permute-start | bytes 46088 | tf_op jit(solution)/shard_map/ppermute | solution.py:48
  16.7 7.8 %collective-permute-start.1 = (f32[10,384]{1,0:T(8,128)S(1)}, f32[10,384]{1,0:T(8,128)S(1)}, u32[]{:S(2)}, u32[]{:S(2)}) collective-permute-start(f32[10,384]{1,0:T(8,128)S(1)} %concatenate.71), channel_id=1, source_target_pairs={{0,8},{4,0},{8,12},{12,4},{16,24},{20,16},{24,28},{28,20},{1,9},{5... | collective-permute-start | bytes 46088 | tf_op jit(solution)/shard_map/ppermute | solution.py:48
  17.7 7.5 %collective-permute-start.2 = (bf16[96,384]{1,0:T(8,128)(2,1)S(1)}, bf16[96,384]{1,0:T(8,128)(2,1)S(1)}, u32[]{:S(2)}, u32[]{:S(2)}) collective-permute-start(bf16[96,384]{1,0:T(8,128)(2,1)S(1)} %constant_dynamic-slice_fusion.7), channel_id=1, source_target_pairs={{0,1},{1,2},{2,3},{3,0},{4,5},{5,6},{6,7},{7,4},{8,9},{9,10},{10,1... | collective-permute-start | bytes 221192 | tf_op jit(solution)/shard_map/ppermute | solution.py:64
  19.1 6.2 %collective-permute-start.3 = (bf16[96,384]{1,0:T(8,128)(2,1)S(1)}, bf16[96,384]{1,0:T(8,128)(2,1)S(1)}, u32[]{:S(2)}, u32[]{:S(2)}) collective-permute-start(bf16[96,384]{1,0:T(8,128)(2,1)S(1)} %constant_dynamic-slice_fusion.7), channel_id=1, source_target_pairs={{0,2},{1,3},{2,0},{3,1},{4,6},{5,7},{6,4},{7,5},{8,10},{9,11},{10,... | collective-permute-start | bytes 221192 | tf_op jit(solution)/shard_map/ppermute | solution.py:64
  20.2 7.4 %collective-permute-start.4 = (bf16[96,384]{1,0:T(8,128)(2,1)S(1)}, bf16[96,384]{1,0:T(8,128)(2,1)S(1)}, u32[]{:S(2)}, u32[]{:S(2)}) collective-permute-start(bf16[96,384]{1,0:T(8,128)(2,1)S(1)} %constant_dynamic-slice_fusion.7), channel_id=1, source_target_pairs={{0,3},{1,0},{2,1},{3,2},{4,7},{5,4},{6,5},{7,6},{8,11},{9,8},{10,9... | collective-permute-start | bytes 221192 | tf_op jit(solution)/shard_map/ppermute | solution.py:64
  21.8 18.0 %copy-start.36 = (bf16[768]{0:T(1024)(128)(2,1)S(1)}, bf16[768]{0:T(1024)(128)(2,1)}, u32[]{:S(2)}) copy-start(bf16[768]{0:T(1024)(128)(2,1)} %param.25) | copy-start | bytes 4612
  21.8 8.0 %collective-permute-start.5 = (bf16[384,384]{1,0:T(8,128)(2,1)S(1)}, bf16[384,384]{1,0:T(8,128)(2,1)S(1)}, u32[]{:S(2)}, u32[]{:S(2)}) collective-permute-start(bf16[384,384]{1,0:T(8,128)(2,1)S(1)} %get-tuple-element.226), channel_id=1, source_target_pairs={{0,0},{4,8},{8,4},{12,12},{16,16},{20,24},{24,20},{28,28},{1,1},{5... | collective-permute-start | bytes 884744 | tf_op jit(solution)/shard_map/ppermute | solution.py:48
  24.6 8.9 %collective-permute-start.6 = (bf16[384,384]{1,0:T(8,128)(2,1)S(1)}, bf16[384,384]{1,0:T(8,128)(2,1)S(1)}, u32[]{:S(2)}, u32[]{:S(2)}) collective-permute-start(bf16[384,384]{1,0:T(8,128)(2,1)S(1)} %get-tuple-element.225), channel_id=1, source_target_pairs={{0,8},{4,0},{8,12},{12,4},{16,24},{20,16},{24,28},{28,20},{1,9},{5... | collective-permute-start | bytes 884744 | tf_op jit(solution)/shard_map/ppermute | solution.py:48
  24.6 28.8 %copy-start.23 = (f32[10,384]{1,0:T(8,128)}, f32[10,384]{1,0:T(8,128)S(1)}, u32[]{:S(2)}) copy-start(f32[10,384]{1,0:T(8,128)S(1)} %get-tuple-element.244) | copy-start | bytes 46084
  24.6 28.8 %copy-start.25 = (f32[10,384]{1,0:T(8,128)}, f32[10,384]{1,0:T(8,128)S(1)}, u32[]{:S(2)}) copy-start(f32[10,384]{1,0:T(8,128)S(1)} %get-tuple-element.245) | copy-start | bytes 46084
  27.6 26.4 %copy-start.11 = (bf16[4,96,384]{2,1,0:T(8,128)(2,1)}, bf16[4,96,384]{2,1,0:T(8,128)(2,1)S(1)}, u32[]{:S(2)}) copy-start(bf16[4,96,384]{2,1,0:T(8,128)(2,1)S(1)} %pad_maximum_fusion.10.refs_0_) | copy-start | bytes 884740
  27.6 13.0 %collective-permute-start.10 = (bf16[4,96,384]{2,1,0:T(8,128)(2,1)S(1)}, bf16[4,96,384]{2,1,0:T(8,128)(2,1)S(1)}, u32[]{:S(2)}, u32[]{:S(2)}) collective-permute-start(bf16[4,96,384]{2,1,0:T(8,128)(2,1)S(1)} %pad_maximum_fusion.10.refs_0_), channel_id=1, source_target_pairs={{0,4},{4,0},{1,5},{5,1},{2,6},{6,2},{3,7},{7,3},{8,12},{12,8},{9,1... | collective-permute-start | bytes 884744 | tf_op jit(solution)/shard_map/ppermute | solution.py:31
  33.5 24.4 %copy-start.2 = (bf16[384,384]{1,0:T(8,128)(2,1)}, bf16[384,384]{1,0:T(8,128)(2,1)S(1)}, u32[]{:S(2)}) copy-start(bf16[384,384]{1,0:T(8,128)(2,1)S(1)} %get-tuple-element.223.x_other) | copy-start | bytes 884740
  33.6 24.4 %copy-start.4 = (bf16[384,384]{1,0:T(8,128)(2,1)}, bf16[384,384]{1,0:T(8,128)(2,1)S(1)}, u32[]{:S(2)}) copy-start(bf16[384,384]{1,0:T(8,128)(2,1)S(1)} %get-tuple-element.224.x_own) | copy-start | bytes 884740
  33.6 7.1 %collective-permute-start.7 = (bf16[192,384]{1,0:T(8,128)(2,1)S(1)}, bf16[192,384]{1,0:T(8,128)(2,1)S(1)}, u32[]{:S(2)}, u32[]{:S(2)}) collective-permute-start(bf16[192,384]{1,0:T(8,128)(2,1)S(1)} %bitcast.111), channel_id=1, source_target_pairs={{0,1},{1,2},{2,3},{3,0},{4,5},{5,6},{6,7},{7,4},{8,9},{9,10},{10,1... | collective-permute-start | bytes 442376 | tf_op jit(solution)/shard_map/ppermute | solution.py:64
  34.2 13.0 %collective-permute-start.8 = (bf16[192,384]{1,0:T(8,128)(2,1)S(1)}, bf16[192,384]{1,0:T(8,128)(2,1)S(1)}, u32[]{:S(2)}, u32[]{:S(2)}) collective-permute-start(bf16[192,384]{1,0:T(8,128)(2,1)S(1)} %bitcast.112), channel_id=1, source_target_pairs={{0,2},{1,3},{2,0},{3,1},{4,6},{5,7},{6,4},{7,5},{8,10},{9,11},{10,... | collective-permute-start | bytes 442376 | tf_op jit(solution)/shard_map/ppermute | solution.py:64
  37.9 12.2 %collective-permute-start.9 = (bf16[192,384]{1,0:T(8,128)(2,1)S(1)}, bf16[192,384]{1,0:T(8,128)(2,1)S(1)}, u32[]{:S(2)}, u32[]{:S(2)}) collective-permute-start(bf16[192,384]{1,0:T(8,128)(2,1)S(1)} %bitcast.113), channel_id=1, source_target_pairs={{0,3},{1,0},{2,1},{3,2},{4,7},{5,4},{6,5},{7,6},{8,11},{9,8},{10,9... | collective-permute-start | bytes 442376 | tf_op jit(solution)/shard_map/ppermute | solution.py:64
  50.2 17.4 %copy-start.13 = (bf16[4,192,384]{2,1,0:T(8,128)(2,1)}, bf16[4,192,384]{2,1,0:T(8,128)(2,1)S(1)}, u32[]{:S(2)}) copy-start(bf16[4,192,384]{2,1,0:T(8,128)(2,1)S(1)} %pad_maximum_fusion.4.refs_0_) | copy-start | bytes 1769476
  54.0 5.1 %collective-permute-start.12 = (bf16[4,96,384]{2,1,0:T(8,128)(2,1)S(1)}, bf16[4,96,384]{2,1,0:T(8,128)(2,1)S(1)}, u32[]{:S(2)}, u32[]{:S(2)}) collective-permute-start(bf16[4,96,384]{2,1,0:T(8,128)(2,1)S(1)} %pad_maximum_fusion.10.refs_0_), channel_id=1, source_target_pairs={{0,8},{8,0},{16,24},{24,16},{1,9},{9,1},{17,25},{25,17},{2,10},{10... | collective-permute-start | bytes 884744 | tf_op jit(solution)/shard_map/ppermute | solution.py:35
  55.8 3.3 collective-permute-start.13
  55.9 17.9 %collective-permute-start.11 = (bf16[4,192,384]{2,1,0:T(8,128)(2,1)S(1)}, bf16[4,192,384]{2,1,0:T(8,128)(2,1)}, u32[]{:S(2)}, u32[]{:S(2)}) collective-permute-start(bf16[4,192,384]{2,1,0:T(8,128)(2,1)S(1)} %pad_maximum_fusion.4.refs_0_), channel_id=1, source_target_pairs={{0,4},{4,0},{1,5},{5,1},{2,6},{6,2},{3,7},{7,3},{8,12},{12,8},{9,1... | collective-permute-start | bytes 1769480 | tf_op jit(solution)/shard_map/ppermute | solution.py:31
  64.1 19.7 %all-to-all-start = ((bf16[4,192,384]{2,1,0:T(8,128)(2,1)}), bf16[4,192,384]{2,1,0:T(8,128)(2,1)S(1)}, u32[]{:S(2)}, u32[]{:S(2)}) async-start(bf16[4,192,384]{2,1,0:T(8,128)(2,1)} %get-tuple-element.109), calls=%async_computation | async-start | bytes 1179648 | tf_op jit(solution)/shard_map/all_to_all | solution.py:68
  67.6 7.2 %collective-permute-start.14 = (bf16[4,192,384]{2,1,0:T(8,128)(2,1)S(1)}, bf16[4,192,384]{2,1,0:T(8,128)(2,1)S(1)}, u32[]{:S(2)}, u32[]{:S(2)}) collective-permute-start(bf16[4,192,384]{2,1,0:T(8,128)(2,1)S(1)} %pad_maximum_fusion.4.refs_0_), channel_id=1, source_target_pairs={{0,8},{8,0},{16,24},{24,16},{1,9},{9,1},{17,25},{25,17},{2,10},{10... | collective-permute-start | bytes 1769480 | tf_op jit(solution)/shard_map/ppermute | solution.py:35
  73.8 2.8 collective-permute-start.15
  84.6 56.8 %all-to-all-start.1 = ((bf16[4,384,384]{2,1,0:T(8,128)(2,1)}), bf16[4,384,384]{2,1,0:T(8,128)(2,1)S(1)}, u32[]{:S(2)}, u32[]{:S(2)}) async-start(bf16[4,384,384]{2,1,0:T(8,128)(2,1)} %get-tuple-element.113), calls=%async_computation.1 | async-start | bytes 2359296 | tf_op jit(solution)/shard_map/all_to_all | solution.py:68
  92.8 4.3 collective-permute-start.16
  95.2 50.4 %collective-permute-start.18 = (bf16[384,384]{1,0:T(8,128)(2,1)}, bf16[384,384]{1,0:T(8,128)(2,1)S(1)}, u32[]{:S(2)}, u32[]{:S(2)}) collective-permute-start(bf16[384,384]{1,0:T(8,128)(2,1)} %get-tuple-element.222), channel_id=1, source_target_pairs={{0,0},{4,8},{8,4},{12,12},{16,16},{20,24},{24,20},{28,28},{1,1},{5... | collective-permute-start | bytes 884744 | tf_op jit(solution)/shard_map/ppermute | solution.py:48
  97.1 48.5 %collective-permute-start.19 = (bf16[384,384]{1,0:T(8,128)(2,1)S(1)}, bf16[384,384]{1,0:T(8,128)(2,1)S(1)}, u32[]{:S(2)}, u32[]{:S(2)}) collective-permute-start(bf16[384,384]{1,0:T(8,128)(2,1)S(1)} %get-tuple-element.221), channel_id=1, source_target_pairs={{0,8},{4,0},{8,12},{12,4},{16,24},{20,16},{24,28},{28,20},{1,9},{5... | collective-permute-start | bytes 884744 | tf_op jit(solution)/shard_map/ppermute | solution.py:48
  144.6 4.0 collective-permute-start.17
  148.6 23.4 %collective-permute-start.20 = (bf16[4,128,384]{2,1,0:T(8,128)(2,1)}, bf16[4,128,384]{2,1,0:T(8,128)(2,1)S(1)}, u32[]{:S(2)}, u32[]{:S(2)}) collective-permute-start(bf16[4,128,384]{2,1,0:T(8,128)(2,1)} %pack.5), channel_id=1, source_target_pairs={{0,8},{8,0},{16,24},{24,16},{1,9},{9,1},{17,25},{25,17},{2,10},{10... | collective-permute-start | bytes 1179656 | tf_op jit(solution)/shard_map/ppermute | solution.py:35
  165.1 23.1 %all-to-all-start.2 = ((bf16[4,128,384]{2,1,0:T(8,128)(2,1)}), bf16[4,128,384]{2,1,0:T(8,128)(2,1)S(1)}, u32[]{:S(2)}, u32[]{:S(2)}) async-start(bf16[4,128,384]{2,1,0:T(8,128)(2,1)} %get-tuple-element.122), calls=%async_computation.2 | async-start | bytes 786432 | tf_op jit(solution)/shard_map/all_to_all | solution.py:68
  188.2 9.5 %all-to-all-start.3 = ((bf16[4,64,384]{2,1,0:T(8,128)(2,1)}), bf16[4,64,384]{2,1,0:T(8,128)(2,1)S(1)}, u32[]{:S(2)}, u32[]{:S(2)}) async-start(bf16[4,64,384]{2,1,0:T(8,128)(2,1)} %get-tuple-element.124), calls=%async_computation.3 | async-start | bytes 393216 | tf_op jit(solution)/shard_map/all_to_all | solution.py:68
  221.3 19.9 %all-to-all-start.4 = ((bf16[4,64,384]{2,1,0:T(8,128)(2,1)}), bf16[4,64,384]{2,1,0:T(8,128)(2,1)S(1)}, u32[]{:S(2)}, u32[]{:S(2)}) async-start(bf16[4,64,384]{2,1,0:T(8,128)(2,1)} %get-tuple-element.137), calls=%async_computation.4 | async-start | bytes 393216 | tf_op jit(solution)/shard_map/all_to_all | solution.py:68
  225.8 209.5 %reduce-scatter.2.cloned.1.call-start = ((), (), s32[]{:S(2)}) async-start(), calls=%async_computation.11 | async-start | bytes 11354112 | tf_op jit(solution)/shard_map/reduce_scatter | solution.py:844
  242.8 27.7 %all-to-all-start.5 = ((bf16[4,128,384]{2,1,0:T(8,128)(2,1)}), bf16[4,128,384]{2,1,0:T(8,128)(2,1)S(1)}, u32[]{:S(2)}, u32[]{:S(2)}) async-start(bf16[4,128,384]{2,1,0:T(8,128)(2,1)} %get-tuple-element.141), calls=%async_computation.5 | async-start | bytes 786432 | tf_op jit(solution)/shard_map/all_to_all | solution.py:68
  247.4 22.2 %collective-permute-start.21 = (bf16[384,384]{1,0:T(8,128)(2,1)S(1)}, bf16[384,384]{1,0:T(8,128)(2,1)S(1)}, u32[]{:S(2)}, u32[]{:S(2)}) collective-permute-start(bf16[384,384]{1,0:T(8,128)(2,1)S(1)} %get-tuple-element.217), channel_id=1, source_target_pairs={{0,0},{8,4},{4,8},{12,12},{16,16},{24,20},{20,24},{28,28},{1,1},{9... | collective-permute-start | bytes 884744 | tf_op jit(solution)/shard_map/ppermute | solution.py:53
  252.0 17.6 %collective-permute-start.22 = (bf16[384,384]{1,0:T(8,128)(2,1)S(1)}, bf16[384,384]{1,0:T(8,128)(2,1)S(1)}, u32[]{:S(2)}, u32[]{:S(2)}) collective-permute-start(bf16[384,384]{1,0:T(8,128)(2,1)S(1)} %get-tuple-element.218), channel_id=1, source_target_pairs={{8,0},{0,4},{12,8},{4,12},{24,16},{16,20},{28,24},{20,28},{9,1},{1... | collective-permute-start | bytes 884744 | tf_op jit(solution)/shard_map/ppermute | solution.py:53
  269.6 19.3 %collective-permute-start.23 = (bf16[4,128,384]{2,1,0:T(8,128)(2,1)}, bf16[4,128,384]{2,1,0:T(8,128)(2,1)S(1)}, u32[]{:S(2)}, u32[]{:S(2)}) collective-permute-start(bf16[4,128,384]{2,1,0:T(8,128)(2,1)} %get-tuple-element.139), channel_id=1, source_target_pairs={{0,8},{8,0},{16,24},{24,16},{1,9},{9,1},{17,25},{25,17},{2,10},{10... | collective-permute-start | bytes 1179656 | tf_op jit(solution)/shard_map/ppermute | solution.py:35
  288.8 24.7 %collective-permute-start.24 = (bf16[4,128,384]{2,1,0:T(8,128)(2,1)}, bf16[4,128,384]{2,1,0:T(8,128)(2,1)S(1)}, u32[]{:S(2)}, u32[]{:S(2)}) collective-permute-start(bf16[4,128,384]{2,1,0:T(8,128)(2,1)} %get-tuple-element.143), channel_id=1, source_target_pairs={{0,8},{8,0},{16,24},{24,16},{1,9},{9,1},{17,25},{25,17},{2,10},{10... | collective-permute-start | bytes 1179656 | tf_op jit(solution)/shard_map/ppermute | solution.py:35
  291.8 32.5 %all-to-all-start.7 = ((bf16[4,192,384]{2,1,0:T(8,128)(2,1)}), bf16[4,192,384]{2,1,0:T(8,128)(2,1)S(1)}, u32[]{:S(2)}, u32[]{:S(2)}) async-start(bf16[4,192,384]{2,1,0:T(8,128)(2,1)} %merge.3), calls=%async_computation.7 | async-start | bytes 1179648 | tf_op jit(solution)/shard_map/all_to_all | solution.py:68
  324.4 24.8 %all-to-all-start.6 = ((bf16[4,192,384]{2,1,0:T(8,128)(2,1)}), bf16[4,192,384]{2,1,0:T(8,128)(2,1)S(1)}, u32[]{:S(2)}, u32[]{:S(2)}) async-start(bf16[4,192,384]{2,1,0:T(8,128)(2,1)} %merge.4), calls=%async_computation.6 | async-start | bytes 1179648 | tf_op jit(solution)/shard_map/all_to_all | solution.py:68
  331.5 3.8 collective-permute-start.25
  355.9 8.2 %collective-permute-start.26 = (bf16[2,4,192,384]{3,2,1,0:T(8,128)(2,1)}, bf16[2,4,192,384]{3,2,1,0:T(8,128)(2,1)S(1)}, u32[]{:S(2)}, u32[]{:S(2)}) collective-permute-start(bf16[2,4,192,384]{3,2,1,0:T(8,128)(2,1)} %get-tuple-element.159), channel_id=1, source_target_pairs={{0,8},{8,0},{16,24},{24,16},{1,9},{9,1},{17,25},{25,17},{2,10},{10... | collective-permute-start | bytes 3538952 | tf_op jit(solution)/shard_map/ppermute | solution.py:35
  356.8 30.1 %all-to-all-start.8 = ((bf16[4,192,384]{2,1,0:T(8,128)(2,1)}), bf16[4,192,384]{2,1,0:T(8,128)(2,1)}, u32[]{:S(2)}, u32[]{:S(2)}) async-start(bf16[4,192,384]{2,1,0:T(8,128)(2,1)} %merge.5), calls=%async_computation.8 | async-start | bytes 1179648 | tf_op jit(solution)/shard_map/all_to_all | solution.py:68
  364.5 19.6 %collective-permute-start.27 = (bf16[4,192,384]{2,1,0:T(8,128)(2,1)S(1)}, bf16[4,192,384]{2,1,0:T(8,128)(2,1)S(1)}, u32[]{:S(2)}, u32[]{:S(2)}) collective-permute-start(bf16[4,192,384]{2,1,0:T(8,128)(2,1)S(1)} %get-tuple-element.202), channel_id=1, source_target_pairs={{0,4},{4,0},{1,5},{5,1},{2,6},{6,2},{3,7},{7,3},{8,12},{12,8},{9,1... | collective-permute-start | bytes 1769480 | tf_op jit(solution)/shard_map/ppermute | solution.py:31
  393.0 9.0 %collective-permute-start.30 = (bf16[2,4,96,384]{3,2,1,0:T(8,128)(2,1)S(1)}, bf16[2,4,96,384]{3,2,1,0:T(8,128)(2,1)S(1)}, u32[]{:S(2)}, u32[]{:S(2)}) collective-permute-start(bf16[2,4,96,384]{3,2,1,0:T(8,128)(2,1)S(1)} %copy-done.37), channel_id=1, source_target_pairs={{0,8},{8,0},{16,24},{24,16},{1,9},{9,1},{17,25},{25,17},{2,10},{10... | collective-permute-start | bytes 1769480 | tf_op jit(solution)/shard_map/ppermute | solution.py:35
  395.6 12.6 %collective-permute-start.33 = (bf16[192,384]{1,0:T(8,128)(2,1)S(1)}, bf16[192,384]{1,0:T(8,128)(2,1)S(1)}, u32[]{:S(2)}, u32[]{:S(2)}) collective-permute-start(bf16[192,384]{1,0:T(8,128)(2,1)S(1)} %get-tuple-element.214), channel_id=1, source_target_pairs={{0,1},{1,2},{2,3},{3,0},{4,5},{5,6},{6,7},{7,4},{8,9},{9,10},{10,1... | collective-permute-start | bytes 442376 | tf_op jit(solution)/shard_map/ppermute | solution.py:64
  396.9 16.9 %collective-permute-start.34 = (bf16[192,384]{1,0:T(8,128)(2,1)S(1)}, bf16[192,384]{1,0:T(8,128)(2,1)S(1)}, u32[]{:S(2)}, u32[]{:S(2)}) collective-permute-start(bf16[192,384]{1,0:T(8,128)(2,1)S(1)} %get-tuple-element.213), channel_id=1, source_target_pairs={{0,2},{1,3},{2,0},{3,1},{4,6},{5,7},{6,4},{7,5},{8,10},{9,11},{10,... | collective-permute-start | bytes 442376 | tf_op jit(solution)/shard_map/ppermute | solution.py:64
  401.5 20.0 %collective-permute-start.35 = (bf16[192,384]{1,0:T(8,128)(2,1)S(1)}, bf16[192,384]{1,0:T(8,128)(2,1)S(1)}, u32[]{:S(2)}, u32[]{:S(2)}) collective-permute-start(bf16[192,384]{1,0:T(8,128)(2,1)S(1)} %get-tuple-element.212), channel_id=1, source_target_pairs={{0,3},{1,0},{2,1},{3,2},{4,7},{5,4},{6,5},{7,6},{8,11},{9,8},{10,9... | collective-permute-start | bytes 442376 | tf_op jit(solution)/shard_map/ppermute | solution.py:64
  402.8 18.9 %collective-permute-start.36 = (bf16[4,96,384]{2,1,0:T(8,128)(2,1)S(1)}, bf16[4,96,384]{2,1,0:T(8,128)(2,1)S(1)}, u32[]{:S(2)}, u32[]{:S(2)}) collective-permute-start(bf16[4,96,384]{2,1,0:T(8,128)(2,1)S(1)} %get-tuple-element.203), channel_id=1, source_target_pairs={{0,4},{4,0},{1,5},{5,1},{2,6},{6,2},{3,7},{7,3},{8,12},{12,8},{9,1... | collective-permute-start | bytes 884744 | tf_op jit(solution)/shard_map/ppermute | solution.py:31
  404.0 1.7 collective-permute-start.31
  405.8 21.8 %collective-permute-start.28 = (f32[384,384]{1,0:T(8,128)S(1)}, f32[384,384]{1,0:T(8,128)S(1)}, u32[]{:S(2)}, u32[]{:S(2)}) collective-permute-start(f32[384,384]{1,0:T(8,128)S(1)} %get-tuple-element.207), channel_id=1, source_target_pairs={{0,0},{8,4},{4,8},{12,12},{16,16},{24,20},{20,24},{28,28},{1,1},{9... | collective-permute-start | bytes 1769480 | tf_op jit(solution)/shard_map/ppermute | solution.py:53
  408.2 19.4 %collective-permute-start.29 = (f32[384,384]{1,0:T(8,128)S(1)}, f32[384,384]{1,0:T(8,128)S(1)}, u32[]{:S(2)}, u32[]{:S(2)}) collective-permute-start(f32[384,384]{1,0:T(8,128)S(1)} %get-tuple-element.208), channel_id=1, source_target_pairs={{8,0},{0,4},{12,8},{4,12},{24,16},{16,20},{28,24},{20,28},{9,1},{1... | collective-permute-start | bytes 1769480 | tf_op jit(solution)/shard_map/ppermute | solution.py:53
  413.8 7.8 %collective-permute-start.32 = (f32[7,768]{1,0:T(8,128)S(1)}, f32[7,768]{1,0:T(8,128)S(1)}, u32[]{:S(2)}, u32[]{:S(2)}) collective-permute-start(f32[7,768]{1,0:T(8,128)S(1)} %add.265), channel_id=1, source_target_pairs={{0,1},{1,0},{2,3},{3,2},{4,5},{5,4},{6,7},{7,6},{8,9},{9,8},{10,11... | collective-permute-start | bytes 64520 | tf_op jit(solution)/shard_map/ppermute | solution.py:59
  422.6 3.6 collective-permute-start.37
  426.4 2.7 collective-permute-start.38
  429.1 6.2 %collective-permute-start.39 = (f32[2,10,384]{2,1,0:T(8,128)S(1)}, f32[2,10,384]{2,1,0:T(8,128)S(1)}, u32[]{:S(2)}, u32[]{:S(2)}) collective-permute-start(f32[2,10,384]{2,1,0:T(8,128)S(1)} %pad_maximum_fusion.14), channel_id=1, source_target_pairs={{0,16},{8,24},{16,0},{24,8},{1,17},{9,25},{17,1},{25,9},{2,18},{10... | collective-permute-start | bytes 92168 | tf_op jit(solution)/shard_map/ppermute | solution.py:35
  431.5 14.2 %all-to-all-start.9 = ((bf16[4,96,384]{2,1,0:T(8,128)(2,1)}), bf16[4,96,384]{2,1,0:T(8,128)(2,1)S(1)}, u32[]{:S(2)}, u32[]{:S(2)}) async-start(bf16[4,96,384]{2,1,0:T(8,128)(2,1)} %add_convert_fusion.3), calls=%async_computation.9 | async-start | bytes 589824 | tf_op jit(solution)/shard_map/all_to_all | solution.py:68
  434.9 25.8 %all-gather.4.cloned.1.call-start = ((), (), s32[]{:S(2)}) async-start(), calls=%async_computation.12 | async-start | bytes 1720320 | tf_op jit(solution)/shard_map/all_gather | solution.py:933
  435.0 5.9 %collective-permute-start.42 = (f32[192,384]{1,0:T(8,128)S(1)}, f32[192,384]{1,0:T(8,128)S(1)}, u32[]{:S(2)}, u32[]{:S(2)}) collective-permute-start(f32[192,384]{1,0:T(8,128)S(1)} %convert_reduce_fusion.1), channel_id=1, source_target_pairs={{0,16},{8,24},{16,0},{24,8},{1,17},{9,25},{17,1},{25,9},{2,18},{10... | collective-permute-start | bytes 884744 | tf_op jit(solution)/shard_map/ppermute | solution.py:35
  440.9 12.9 %collective-permute-start.43 = (f32[192,384]{1,0:T(8,128)S(1)}, f32[192,384]{1,0:T(8,128)S(1)}, u32[]{:S(2)}, u32[]{:S(2)}) collective-permute-start(f32[192,384]{1,0:T(8,128)S(1)} %add.281), channel_id=1, source_target_pairs={{0,8},{8,0},{16,24},{24,16},{1,9},{9,1},{17,25},{25,17},{2,10},{10... | collective-permute-start | bytes 884744 | tf_op jit(solution)/shard_map/ppermute | solution.py:35
  445.7 6.2 %collective-permute-start.40 = (f32[96,384]{1,0:T(8,128)S(1)}, f32[96,384]{1,0:T(8,128)S(1)}, u32[]{:S(2)}, u32[]{:S(2)}) collective-permute-start(f32[96,384]{1,0:T(8,128)S(1)} %convert_reduce_fusion.2), channel_id=1, source_target_pairs={{0,16},{8,24},{16,0},{24,8},{1,17},{9,25},{17,1},{25,9},{2,18},{10... | collective-permute-start | bytes 442376 | tf_op jit(solution)/shard_map/ppermute | solution.py:35
  452.0 2.8 collective-permute-start.41
  (37 other events, 197.8 us)
Sparse Core Ops, SparseCore 0:
  50.4 109.2 all-gather.5
  241.3 179.7 reduce-scatter.1
  437.3 23.3 all-gather.3

commit v4 on v3

--- a/solution.py
+++ b/solution.py
@@ -774,13 +774,13 @@
     soon = gather_halves(blocks[0], order)
     next(soon)
     next(soon)
+    rest = lax.all_gather(order.next(rest), ("dp", "row", "col"), axis=0, tiled=False)
+    rest = rest.reshape((-1, 2, cols) + rest.shape[1:])[:SLICES]
     order.done(*order.last, *x, small)
     late = gather_halves(order.next(blocks[1]), order)
     next(late)
     soon = next(soon)
     next(late)
-    rest = lax.all_gather(order.next(rest), ("dp", "row", "col"), axis=0, tiled=False)
-    rest = rest.reshape((-1, 2, cols) + rest.shape[1:])[:SLICES]
     w_groups, own = [], []
 
     def begin(group, source):

time: 477 us -> 473 us (level)
  starting transfers between devices: 112 us -> 117 us
    ppermute x18, starting transfers between devices: 20.4 us -> 30.2 us  [dp_swap(): lax.ppermute(value, 'dp', [(i, i ^ 1 << bit) for i in range(lax.axis_size...]
    unnamed x88 -> x98, local copies, waits for them, and re-layouts: 10.7 us -> 10.7 us
  transfers between devices with their start and end apart: 57 -> 57, of which waited for: 24 -> 26; matrix products, arithmetic and copies ran while one was open for 5% -> 5% of each run, Pallas kernels for 31% -> 31%
where the time goes in v4:
time: 473 us; the launch traced here: 471 us
  Pallas kernels  170 us (36%)
  waiting for transfers between devices  126 us (27%)
  starting transfers between devices  117 us (25%)
  other arithmetic  23 us (5%)
  local copies, waits for them, and re-layouts  18.8 us (4%)
  between operations  15.4 us (3%)
    all_to_all x10, waiting for transfers between devices, col_trade(): return lax.all_to_all(value, 'col', 0, 0, tiled=True)  54.8 us
    pallas_call x3, Pallas kernels, attend_back(): pl.pallas_call(functools.partial(attend_back_kernel, offset, grad_offset)...  52.5 us
    all_to_all x10, starting transfers between devices, col_trade(): return lax.all_to_all(value, 'col', 0, 0, tiled=True)  50.8 us
    pallas_call x3, Pallas kernels, attend(): pl.pallas_call(functools.partial(attend_kernel, offset, len(earlier)), in...  46.4 us
    ppermute x18, starting transfers between devices, dp_swap(): lax.ppermute(value, 'dp', [(i, i ^ 1 << bit) for i in range(lax.axis_size...  30.2 us
    pallas_call x1, Pallas kernels, middle(): pl.pallas_call(functools.partial(middle_kernel, slots), in_specs=[SCALARS...  22.9 us
    ppermute x5, waiting for transfers between devices, row_swap(): return lax.ppermute(value, 'row', [(0, 1), (1, 0)])  22.4 us
    ppermute x9, waiting for transfers between devices, col_from(): lax.ppermute(value, 'col', [(i, (i + hop) % size) for i in range(size)])  21.8 us
  transfers between devices with their start and end apart: 57, of which 26 were waited for; matrix products, arithmetic and copies ran while one was open for 5% of the time, Pallas kernels for 31%

profile of v4, /device:TPU:9, one launch (start us, length us, event | category | flops | bytes accessed | tf_op | source)
XLA Modules:
  0.0 470.6 jit_solution(12121403178895082507)
XLA Ops:
  15.7 2.4 collective-permute-done.4
  19.5 3.5 collective-permute-start
  23.2 2.1 collective-permute-start.5
  31.7 2.8 collective-permute-done.5
  34.5 2.1 collective-permute-done.6
  36.8 1.7 collective-permute-start.8
  40.8 4.5 collective-permute-start.13
  45.4 3.8 collective-permute-done.8
  49.2 5.0 %collective-permute-done.9 = bf16[192,384]{1,0:T(8,128)(2,1)S(1)} collective-permute-done((bf16[192,384]{1,0:T(8,128)(2,1)S(1)}, bf16[192,384]{1,0:T(8,128)(2,1)S(1)}, u32[]{:S(2)}, u32[]{:S(2)}) %collective-permute-start.9) | collective-permute-done | bytes 147488 | tf_op jit(solution)/shard_map/ppermute | solution.py:64
  54.3 4.3 collective-permute-start.11
  61.2 4.3 project.2
  65.5 3.5 all-to-all-start
  69.0 2.8 collective-permute-start.14
  71.8 2.0 collective-permute-done.11.refs_1_
  75.2 2.0 collective-permute-done.15.refs_3_
  77.2 5.7 %project.3 = (bf16[2,768,768]{2,1,0:T(8,128)(2,1)}, bf16[4,384,384]{2,1,0:T(8,128)(2,1)}) custom-call(s32[7]{0:T(128)} %pad_add_fusion.scalars._, bf16[384,768]{1,0:T(8,128)(2,1)} %fusion.7.h_ref, f32[64,384]{1,0:T(8,128)} %fusion.19.turn_ref, bf16[4,192,384]{2,1,0:T(8,128)(2,1)} %copy-done.15, bf16[4,192,384]{2,1,0:T(8,128)(2,1)} %collective-permute-done.11.refs_1_, ...), custom_call_target="tpu_custom_call" | custom-call | flops 905969664 | bytes 6000000 | tf_op jit(solution)/shard_map/project/pallas_call | solution.py:213
  84.3 6.5 %all-to-all-start.1 = ((bf16[4,384,384]{2,1,0:T(8,128)(2,1)}), bf16[4,384,384]{2,1,0:T(8,128)(2,1)S(1)}, u32[]{:S(2)}, u32[]{:S(2)}) async-start(bf16[4,384,384]{2,1,0:T(8,128)(2,1)} %get-tuple-element.113), calls=%async_computation.1 | async-start | bytes 2359296 | tf_op jit(solution)/shard_map/all_to_all | solution.py:68
  90.8 1.9 pack.3
  95.5 1.9 collective-permute-start.18
  97.4 15.3 %attend.3 = (bf16[4,64,384]{2,1,0:T(8,128)(2,1)}, f32[4,64,384]{2,1,0:T(8,128)}, f32[4,1,384]{2,1,0:T(1,128)}) custom-call(s32[7]{0:T(128)} %pad_add_fusion.scalars._, bf16[4,192,384]{2,1,0:T(8,128)(2,1)} %copy-done.7, bf16[4,128,384]{2,1,0:T(8,128)(2,1)} %collective-permute-done.16.other_ref, s32[4,1,384]{2,1,0:T(1,128)} %broadcast_in_dim.33.limit_ref), custom_call_target="tpu_custom_call" | custom-call | flops 8000000000 | bytes 3000000 | tf_op jit(solution)/shard_map/attend/pallas_call | solution.py:342
  112.7 26.6 %all-to-all-done.1.own_ref = bf16[4,384,384]{2,1,0:T(8,128)(2,1)S(1)} async-done(((bf16[4,384,384]{2,1,0:T(8,128)(2,1)}), bf16[4,384,384]{2,1,0:T(8,128)(2,1)S(1)}, u32[]{:S(2)}, u32[]{:S(2)}) %all-to-all-start.1) | async-done | bytes 1179680 | tf_op jit(solution)/shard_map/all_to_all | solution.py:68
  140.4 2.1 pack.4
  144.2 2.1 pack.5
  147.1 15.6 %attend.4 = (bf16[4,128,384]{2,1,0:T(8,128)(2,1)}, f32[4,64,384]{2,1,0:T(8,128)}, f32[4,1,384]{2,1,0:T(1,128)}) custom-call(s32[7]{0:T(128)} %pad_add_fusion.scalars._, bf16[4,384,384]{2,1,0:T(8,128)(2,1)} %copy-done.6, bf16[4,128,384]{2,1,0:T(8,128)(2,1)} %copy-done.44, s32[4,1,384]{2,1,0:T(1,128)} %broadcast_in_dim.33.limit_ref, ...), custom_call_target="tpu_custom_call" | custom-call | flops 8000000000 | bytes 3000000 | tf_op jit(solution)/shard_map/attend/pallas_call | solution.py:342
  162.7 6.6 %all-to-all-start.2 = ((bf16[4,128,384]{2,1,0:T(8,128)(2,1)}), bf16[4,128,384]{2,1,0:T(8,128)(2,1)S(1)}, u32[]{:S(2)}, u32[]{:S(2)}) async-start(bf16[4,128,384]{2,1,0:T(8,128)(2,1)} %get-tuple-element.122), calls=%async_computation.2 | async-start | bytes 786432 | tf_op jit(solution)/shard_map/all_to_all | solution.py:68
  170.0 15.5 %attend.5 = (bf16[4,64,384]{2,1,0:T(8,128)(2,1)}, f32[4,64,384]{2,1,0:T(8,128)}, f32[4,1,384]{2,1,0:T(1,128)}) custom-call(s32[7]{0:T(128)} %pad_add_fusion.scalars._, bf16[4,384,384]{2,1,0:T(8,128)(2,1)} %copy-done.6, bf16[4,128,384]{2,1,0:T(8,128)(2,1)} %copy-done.45, s32[4,1,384]{2,1,0:T(1,128)} %broadcast_in_dim.33.limit_ref), custom_call_target="tpu_custom_call" | custom-call | flops 8000000000 | bytes 3000000 | tf_op jit(solution)/shard_map/attend/pallas_call | solution.py:342
  185.5 4.5 all-to-all-start.3
  190.1 4.9 %all-to-all-done.3.last_ref = bf16[4,64,384]{2,1,0:T(8,128)(2,1)S(1)} async-done(((bf16[4,64,384]{2,1,0:T(8,128)(2,1)}), bf16[4,64,384]{2,1,0:T(8,128)(2,1)S(1)}, u32[]{:S(2)}, u32[]{:S(2)}) %all-to-all-start.3) | async-done | bytes 196640 | tf_op jit(solution)/shard_map/all_to_all | solution.py:68
  195.7 22.9 %middle.1 = (bf16[384,384]{1,0:T(8,128)(2,1)}, bf16[384,384]{1,0:T(8,128)(2,1)}, f32[384,768]{1,0:T(8,128)}, bf16[384,768]{1,0:T(8,128)(2,1)}, bf16[384,768]{1,0...) custom-call(s32[7]{0:T(128)} %pad_add_fusion.scalars._, ...), custom_call_target="tpu_custom_call" | custom-call | flops 8153726976 | bytes 14000000 | tf_op jit(solution)/shard_map/middle/pallas_call | solution.py:591
  218.6 4.6 all-to-all-start.4
  223.2 15.3 %weight_grads.1 = bf16[4,2,4,448,384]{4,3,2,1,0:T(8,128)(2,1)} custom-call(s32[7]{0:T(128)} %pad_add_fusion.scalars._, bf16[384,768]{1,0:T(8,128)(2,1)} %get-tuple-element.130.h_ref, bf16[384,768]{1,0:T(8,128)(2,1)} %get-tuple-element.131.df_ref, bf16[384,768]{1,0:T(8,128)(2,1)} %get-tuple-element.132.d_att_ref, ...), custom_call_target="tpu_custom_call" | custom-call | flops 4076863488 | bytes 20000000 | tf_op jit(solution)/shard_map/weight_grads/pallas_call | solution.py:658
  240.2 4.5 all-to-all-start.5
  244.8 1.9 collective-permute-start.21
  246.7 17.5 %attend_back.3 = (bf16[4,64,384]{2,1,0:T(8,128)(2,1)}, f32[4,128,384]{2,1,0:T(8,128)}, bf16[4,128,384]{2,1,0:T(8,128)(2,1)}) custom-call(s32[7]{0:T(128)} %pad_add_fusion.scalars._, bf16[4,384,384]{2,1,0:T(8,128)(2,1)} %copy-done.6, bf16[4,128,384]{2,1,0:T(8,128)(2,1)} %copy-done.45, bf16[4,64,384]{2,1,0:T(8,128)(2,1)} %copy-done.33, ...), custom_call_target="tpu_custom_call" | custom-call | flops 16000000000 | bytes 4000000 | tf_op jit(solution)/shard_map/attend_back/pallas_call | solution.py:438
  266.4 17.5 %attend_back.4 = (bf16[4,64,384]{2,1,0:T(8,128)(2,1)}, f32[4,128,384]{2,1,0:T(8,128)}, bf16[4,128,384]{2,1,0:T(8,128)(2,1)}) custom-call(s32[7]{0:T(128)} %pad_add_fusion.scalars._, bf16[4,384,384]{2,1,0:T(8,128)(2,1)} %copy-done.6, bf16[4,128,384]{2,1,0:T(8,128)(2,1)} %copy-done.44, bf16[4,128,384]{2,1,0:T(8,128)(2,1)} %copy-done.19, ...), custom_call_target="tpu_custom_call" | custom-call | flops 16000000000 | bytes 4000000 | tf_op jit(solution)/shard_map/attend_back/pallas_call | solution.py:438
  284.7 2.2 merge.3
  286.9 4.5 all-to-all-start.7
  291.4 17.4 %attend_back.5 = (bf16[4,64,384]{2,1,0:T(8,128)(2,1)}, f32[4,128,384]{2,1,0:T(8,128)}, bf16[4,128,384]{2,1,0:T(8,128)(2,1)}) custom-call(s32[7]{0:T(128)} %pad_add_fusion.scalars._, bf16[4,192,384]{2,1,0:T(8,128)(2,1)} %copy-done.7, bf16[4,128,384]{2,1,0:T(8,128)(2,1)} %collective-permute-done.16.other_ref, bf16[4,128,384]{2,1,0:T(8,128)(2,1)} %copy-done.19, ...), custom_call_target="tpu_custom_call" | custom-call | flops 16000000000 | bytes 4000000 | tf_op jit(solution)/shard_map/attend_back/pallas_call | solution.py:438
  309.6 2.3 merge.4
  311.9 6.9 %all-to-all-done.7.refs_1_ = bf16[4,192,384]{2,1,0:T(8,128)(2,1)S(1)} async-done(((bf16[4,192,384]{2,1,0:T(8,128)(2,1)}), bf16[4,192,384]{2,1,0:T(8,128)(2,1)S(1)}, u32[]{:S(2)}, u32[]{:S(2)}) %all-to-all-start.7) | async-done | bytes 589856 | tf_op jit(solution)/shard_map/all_to_all | solution.py:68
  318.8 5.5 %all-to-all-start.6 = ((bf16[4,192,384]{2,1,0:T(8,128)(2,1)}), bf16[4,192,384]{2,1,0:T(8,128)(2,1)S(1)}, u32[]{:S(2)}, u32[]{:S(2)}) async-start(bf16[4,192,384]{2,1,0:T(8,128)(2,1)} %merge.4), calls=%async_computation.6 | async-start | bytes 1179648 | tf_op jit(solution)/shard_map/all_to_all | solution.py:68
  324.3 2.8 collective-permute-start.25
  329.2 2.2 merge.5
  331.4 15.1 %all-to-all-done.6.refs_0_ = bf16[4,192,384]{2,1,0:T(8,128)(2,1)S(1)} async-done(((bf16[4,192,384]{2,1,0:T(8,128)(2,1)}), bf16[4,192,384]{2,1,0:T(8,128)(2,1)S(1)}, u32[]{:S(2)}, u32[]{:S(2)}) %all-to-all-start.6) | async-done | bytes 589856 | tf_op jit(solution)/shard_map/all_to_all | solution.py:68
  347.4 6.0 %unproject.2 = (f32[384,768]{1,0:T(8,128)}, bf16[2,4,192,384]{3,2,1,0:T(8,128)(2,1)}, bf16[2,4,192,384]{3,2,1,0:T(8,128)(2,1)}) custom-call(s32[7]{0:T(128)} %pad_add_fusion.scalars._, bf16[384,768]{1,0:T(8,128)(2,1)} %fusion.7.h_ref, bf16[2,768,768]{2,1,0:T(8,128)(2,1)} %get-tuple-element.107.w_ref, bf16[4,192,384]{2,1,0:T(8,128)(2,1)} %copy-done.16, ...), custom_call_target="tpu_custom_call" | custom-call | flops 1811939328 | bytes 10000000 | tf_op jit(solution)/shard_map/unproject/pallas_call | solution.py:695
  354.3 7.0 %all-to-all-start.8 = ((bf16[4,192,384]{2,1,0:T(8,128)(2,1)}), bf16[4,192,384]{2,1,0:T(8,128)(2,1)}, u32[]{:S(2)}, u32[]{:S(2)}) async-start(bf16[4,192,384]{2,1,0:T(8,128)(2,1)} %merge.5), calls=%async_computation.8 | async-start | bytes 1179648 | tf_op jit(solution)/shard_map/all_to_all | solution.py:68
  364.0 17.2 %collective-permute-done.27 = bf16[4,192,384]{2,1,0:T(8,128)(2,1)S(1)} collective-permute-done((bf16[4,192,384]{2,1,0:T(8,128)(2,1)S(1)}, bf16[4,192,384]{2,1,0:T(8,128)(2,1)S(1)}, u32[]{:S(2)}, u32[]{:S(2)}) %collective-permute-start.27) | collective-permute-done | bytes 589856 | tf_op jit(solution)/shard_map/ppermute | solution.py:31
  381.9 4.0 unproject.3
  386.0 2.0 fusion.12
  388.1 3.0 collective-permute-start.30
  391.1 1.8 collective-permute-start.33
  392.9 4.9 %collective-permute-start.34 = (bf16[192,384]{1,0:T(8,128)(2,1)S(1)}, bf16[192,384]{1,0:T(8,128)(2,1)S(1)}, u32[]{:S(2)}, u32[]{:S(2)}) collective-permute-start(bf16[192,384]{1,0:T(8,128)(2,1)S(1)} %get-tuple-element.213), channel_id=1, source_target_pairs={{0,2},{1,3},{2,0},{3,1},{4,6},{5,7},{6,4},{7,5},{8,10},{9,11},{10,... | collective-permute-start | bytes 442376 | tf_op jit(solution)/shard_map/ppermute | solution.py:64
  401.6 2.8 collective-permute-start.28
  404.5 5.6 %collective-permute-done.34 = bf16[192,384]{1,0:T(8,128)(2,1)S(1)} collective-permute-done((bf16[192,384]{1,0:T(8,128)(2,1)S(1)}, bf16[192,384]{1,0:T(8,128)(2,1)S(1)}, u32[]{:S(2)}, u32[]{:S(2)}) %collective-permute-start.34) | collective-permute-done | bytes 147488 | tf_op jit(solution)/shard_map/ppermute | solution.py:64
  410.1 2.0 collective-permute-start.32
  412.1 5.0 %collective-permute-done.35 = bf16[192,384]{1,0:T(8,128)(2,1)S(1)} collective-permute-done((bf16[192,384]{1,0:T(8,128)(2,1)S(1)}, bf16[192,384]{1,0:T(8,128)(2,1)S(1)}, u32[]{:S(2)}, u32[]{:S(2)}) %collective-permute-start.35) | collective-permute-done | bytes 147488 | tf_op jit(solution)/shard_map/ppermute | solution.py:64
  418.2 3.5 collective-permute-done.37
  422.3 2.4 collective-permute-done.38
  427.2 3.4 all-to-all-start.9
  431.5 4.9 %collective-permute-done.42 = f32[192,384]{1,0:T(8,128)S(1)} collective-permute-done((f32[192,384]{1,0:T(8,128)S(1)}, f32[192,384]{1,0:T(8,128)S(1)}, u32[]{:S(2)}, u32[]{:S(2)}) %collective-permute-start.42) | collective-permute-done | bytes 294944 | tf_op jit(solution)/shard_map/ppermute | solution.py:35
  436.4 7.4 %collective-permute-start.43 = (f32[192,384]{1,0:T(8,128)S(1)}, f32[192,384]{1,0:T(8,128)S(1)}, u32[]{:S(2)}, u32[]{:S(2)}) collective-permute-start(f32[192,384]{1,0:T(8,128)S(1)} %add.281), channel_id=1, source_target_pairs={{0,8},{8,0},{16,24},{24,16},{1,9},{9,1},{17,25},{25,17},{2,10},{10... | collective-permute-start | bytes 884744 | tf_op jit(solution)/shard_map/ppermute | solution.py:35
  446.7 3.4 collective-permute-done.40
  450.1 1.8 collective-permute-start.41
  454.0 4.8 %all-gather.4.cloned.1.call-done = bf16[4,448,384]{2,1,0:T(8,128)(2,1)} async-done(((bf16[1,448,384]{2,1,0:T(8,128)(2,1)}), bf16[4,448,384]{2,1,0:T(8,128)(2,1)}) %all-gather.4.cloned.1.call-update) | async-done | bytes 1376272 | tf_op jit(solution)/shard_map/all_gather | solution.py:933
  (275 shorter events, 62.7 us)
Async XLA Ops:
  7.2 187.8 %all-gather.6.cloned.1.call-start = ((), (), s32[]{:S(2)}) async-start(), calls=%async_computation.13 | async-start | bytes 11354112 | tf_op jit(solution)/shard_map/all_gather | solution.py:777
  8.3 7.4 %collective-permute-start.2 = (bf16[96,384]{1,0:T(8,128)(2,1)S(1)}, bf16[96,384]{1,0:T(8,128)(2,1)S(1)}, u32[]{:S(2)}, u32[]{:S(2)}) collective-permute-start(bf16[96,384]{1,0:T(8,128)(2,1)S(1)} %constant_dynamic-slice_fusion.7), channel_id=1, source_target_pairs={{0,1},{1,2},{2,3},{3,0},{4,5},{5,6},{6,7},{7,4},{8,9},{9,10},{10,1... | collective-permute-start | bytes 221192 | tf_op jit(solution)/shard_map/ppermute | solution.py:64
  9.6 6.1 %collective-permute-start.3 = (bf16[96,384]{1,0:T(8,128)(2,1)S(1)}, bf16[96,384]{1,0:T(8,128)(2,1)S(1)}, u32[]{:S(2)}, u32[]{:S(2)}) collective-permute-start(bf16[96,384]{1,0:T(8,128)(2,1)S(1)} %constant_dynamic-slice_fusion.7), channel_id=1, source_target_pairs={{0,2},{1,3},{2,0},{3,1},{4,6},{5,7},{6,4},{7,5},{8,10},{9,11},{10,... | collective-permute-start | bytes 221192 | tf_op jit(solution)/shard_map/ppermute | solution.py:64
  10.7 7.4 %collective-permute-start.4 = (bf16[96,384]{1,0:T(8,128)(2,1)S(1)}, bf16[96,384]{1,0:T(8,128)(2,1)S(1)}, u32[]{:S(2)}, u32[]{:S(2)}) collective-permute-start(bf16[96,384]{1,0:T(8,128)(2,1)S(1)} %constant_dynamic-slice_fusion.7), channel_id=1, source_target_pairs={{0,3},{1,0},{2,1},{3,2},{4,7},{5,4},{6,5},{7,6},{8,11},{9,8},{10,9... | collective-permute-start | bytes 221192 | tf_op jit(solution)/shard_map/ppermute | solution.py:64
  18.2 13.2 %copy-start.11 = (bf16[4,96,384]{2,1,0:T(8,128)(2,1)}, bf16[4,96,384]{2,1,0:T(8,128)(2,1)S(1)}, u32[]{:S(2)}) copy-start(bf16[4,96,384]{2,1,0:T(8,128)(2,1)S(1)} %pad_maximum_fusion.10.refs_0_) | copy-start | bytes 884740
  19.5 8.1 %collective-permute-start = (f32[10,384]{1,0:T(8,128)S(1)}, f32[10,384]{1,0:T(8,128)S(1)}, u32[]{:S(2)}, u32[]{:S(2)}) collective-permute-start(f32[10,384]{1,0:T(8,128)S(1)} %concatenate.71), channel_id=1, source_target_pairs={{0,0},{4,8},{8,4},{12,12},{16,16},{20,24},{24,20},{28,28},{1,1},{5... | collective-permute-start | bytes 46088 | tf_op jit(solution)/shard_map/ppermute | solution.py:48
  23.0 4.6 collective-permute-start.1
  23.2 11.3 %collective-permute-start.5 = (bf16[384,384]{1,0:T(8,128)(2,1)S(1)}, bf16[384,384]{1,0:T(8,128)(2,1)S(1)}, u32[]{:S(2)}, u32[]{:S(2)}) collective-permute-start(bf16[384,384]{1,0:T(8,128)(2,1)S(1)} %get-tuple-element.226), channel_id=1, source_target_pairs={{0,0},{4,8},{8,4},{12,12},{16,16},{20,24},{24,20},{28,28},{1,1},{5... | collective-permute-start | bytes 884744 | tf_op jit(solution)/shard_map/ppermute | solution.py:48
  25.2 11.4 %collective-permute-start.6 = (bf16[384,384]{1,0:T(8,128)(2,1)S(1)}, bf16[384,384]{1,0:T(8,128)(2,1)S(1)}, u32[]{:S(2)}, u32[]{:S(2)}) collective-permute-start(bf16[384,384]{1,0:T(8,128)(2,1)S(1)} %get-tuple-element.225), channel_id=1, source_target_pairs={{0,8},{4,0},{8,12},{12,4},{16,24},{20,16},{24,28},{28,20},{1,9},{5... | collective-permute-start | bytes 884744 | tf_op jit(solution)/shard_map/ppermute | solution.py:48
  29.7 11.1 %collective-permute-start.10 = (bf16[4,96,384]{2,1,0:T(8,128)(2,1)S(1)}, bf16[4,96,384]{2,1,0:T(8,128)(2,1)S(1)}, u32[]{:S(2)}, u32[]{:S(2)}) collective-permute-start(bf16[4,96,384]{2,1,0:T(8,128)(2,1)S(1)} %pad_maximum_fusion.10.refs_0_), channel_id=1, source_target_pairs={{0,4},{4,0},{1,5},{5,1},{2,6},{6,2},{3,7},{7,3},{8,12},{12,8},{9,1... | collective-permute-start | bytes 884744 | tf_op jit(solution)/shard_map/ppermute | solution.py:31
  31.4 28.3 %collective-permute-start.12 = (bf16[4,96,384]{2,1,0:T(8,128)(2,1)S(1)}, bf16[4,96,384]{2,1,0:T(8,128)(2,1)S(1)}, u32[]{:S(2)}, u32[]{:S(2)}) collective-permute-start(bf16[4,96,384]{2,1,0:T(8,128)(2,1)S(1)} %pad_maximum_fusion.10.refs_0_), channel_id=1, source_target_pairs={{0,8},{8,0},{16,24},{24,16},{1,9},{9,1},{17,25},{25,17},{2,10},{10... | collective-permute-start | bytes 884744 | tf_op jit(solution)/shard_map/ppermute | solution.py:35
  36.7 21.9 %copy-start.2 = (bf16[384,384]{1,0:T(8,128)(2,1)}, bf16[384,384]{1,0:T(8,128)(2,1)S(1)}, u32[]{:S(2)}) copy-start(bf16[384,384]{1,0:T(8,128)(2,1)S(1)} %get-tuple-element.223.x_other) | copy-start | bytes 884740
  36.7 21.9 %copy-start.4 = (bf16[384,384]{1,0:T(8,128)(2,1)}, bf16[384,384]{1,0:T(8,128)(2,1)S(1)}, u32[]{:S(2)}) copy-start(bf16[384,384]{1,0:T(8,128)(2,1)S(1)} %get-tuple-element.224.x_own) | copy-start | bytes 884740
  36.7 8.7 %collective-permute-start.7 = (bf16[192,384]{1,0:T(8,128)(2,1)S(1)}, bf16[192,384]{1,0:T(8,128)(2,1)S(1)}, u32[]{:S(2)}, u32[]{:S(2)}) collective-permute-start(bf16[192,384]{1,0:T(8,128)(2,1)S(1)} %bitcast.111), channel_id=1, source_target_pairs={{0,1},{1,2},{2,3},{3,0},{4,5},{5,6},{6,7},{7,4},{8,9},{9,10},{10,1... | collective-permute-start | bytes 442376 | tf_op jit(solution)/shard_map/ppermute | solution.py:64
  36.8 12.4 %collective-permute-start.8 = (bf16[192,384]{1,0:T(8,128)(2,1)S(1)}, bf16[192,384]{1,0:T(8,128)(2,1)S(1)}, u32[]{:S(2)}, u32[]{:S(2)}) collective-permute-start(bf16[192,384]{1,0:T(8,128)(2,1)S(1)} %bitcast.112), channel_id=1, source_target_pairs={{0,2},{1,3},{2,0},{3,1},{4,6},{5,7},{6,4},{7,5},{8,10},{9,11},{10,... | collective-permute-start | bytes 442376 | tf_op jit(solution)/shard_map/ppermute | solution.py:64
  38.5 15.7 %collective-permute-start.9 = (bf16[192,384]{1,0:T(8,128)(2,1)S(1)}, bf16[192,384]{1,0:T(8,128)(2,1)S(1)}, u32[]{:S(2)}, u32[]{:S(2)}) collective-permute-start(bf16[192,384]{1,0:T(8,128)(2,1)S(1)} %bitcast.113), channel_id=1, source_target_pairs={{0,3},{1,0},{2,1},{3,2},{4,7},{5,4},{6,5},{7,6},{8,11},{9,8},{10,9... | collective-permute-start | bytes 442376 | tf_op jit(solution)/shard_map/ppermute | solution.py:64
  40.8 18.9 %copy-start.28 = (bf16[4,96,384]{2,1,0:T(8,128)(2,1)}, bf16[4,96,384]{2,1,0:T(8,128)(2,1)S(1)}, u32[]{:S(2)}) copy-start(bf16[4,96,384]{2,1,0:T(8,128)(2,1)S(1)} %collective-permute-done.10.refs_1_) | copy-start | bytes 884740
  40.8 18.9 %collective-permute-start.13 = (bf16[4,96,384]{2,1,0:T(8,128)(2,1)S(1)}, bf16[4,96,384]{2,1,0:T(8,128)(2,1)S(1)}, u32[]{:S(2)}, u32[]{:S(2)}) collective-permute-start(bf16[4,96,384]{2,1,0:T(8,128)(2,1)S(1)} %collective-permute-done.10.refs_1_), channel_id=1, source_target_pairs={{0,8},{8,0},{16,24},{24,16},{1,9},{9,1},{17,25},{25,17},{2,10},{10... | collective-permute-start | bytes 884744 | tf_op jit(solution)/shard_map/ppermute | solution.py:35
  54.3 14.7 %copy-start.15 = (bf16[4,192,384]{2,1,0:T(8,128)(2,1)}, bf16[4,192,384]{2,1,0:T(8,128)(2,1)S(1)}, u32[]{:S(2)}) copy-start(bf16[4,192,384]{2,1,0:T(8,128)(2,1)S(1)} %pad_maximum_fusion.4.refs_0_) | copy-start | bytes 1769476
  54.3 19.6 %collective-permute-start.11 = (bf16[4,192,384]{2,1,0:T(8,128)(2,1)S(1)}, bf16[4,192,384]{2,1,0:T(8,128)(2,1)}, u32[]{:S(2)}, u32[]{:S(2)}) collective-permute-start(bf16[4,192,384]{2,1,0:T(8,128)(2,1)S(1)} %pad_maximum_fusion.4.refs_0_), channel_id=1, source_target_pairs={{0,4},{4,0},{1,5},{5,1},{2,6},{6,2},{3,7},{7,3},{8,12},{12,8},{9,1... | collective-permute-start | bytes 1769480 | tf_op jit(solution)/shard_map/ppermute | solution.py:31
  65.5 18.0 %all-to-all-start = ((bf16[4,192,384]{2,1,0:T(8,128)(2,1)}), bf16[4,192,384]{2,1,0:T(8,128)(2,1)S(1)}, u32[]{:S(2)}, u32[]{:S(2)}) async-start(bf16[4,192,384]{2,1,0:T(8,128)(2,1)} %get-tuple-element.109), calls=%async_computation | async-start | bytes 1179648 | tf_op jit(solution)/shard_map/all_to_all | solution.py:68
  69.0 6.2 %collective-permute-start.14 = (bf16[4,192,384]{2,1,0:T(8,128)(2,1)S(1)}, bf16[4,192,384]{2,1,0:T(8,128)(2,1)S(1)}, u32[]{:S(2)}, u32[]{:S(2)}) collective-permute-start(bf16[4,192,384]{2,1,0:T(8,128)(2,1)S(1)} %pad_maximum_fusion.4.refs_0_), channel_id=1, source_target_pairs={{0,8},{8,0},{16,24},{24,16},{1,9},{9,1},{17,25},{25,17},{2,10},{10... | collective-permute-start | bytes 1769480 | tf_op jit(solution)/shard_map/ppermute | solution.py:35
  73.9 3.3 collective-permute-start.15
  84.3 55.1 %all-to-all-start.1 = ((bf16[4,384,384]{2,1,0:T(8,128)(2,1)}), bf16[4,384,384]{2,1,0:T(8,128)(2,1)S(1)}, u32[]{:S(2)}, u32[]{:S(2)}) async-start(bf16[4,384,384]{2,1,0:T(8,128)(2,1)} %get-tuple-element.113), calls=%async_computation.1 | async-start | bytes 2359296 | tf_op jit(solution)/shard_map/all_to_all | solution.py:68
  92.7 4.8 %collective-permute-start.16 = (bf16[4,128,384]{2,1,0:T(8,128)(2,1)}, bf16[4,128,384]{2,1,0:T(8,128)(2,1)}, u32[]{:S(2)}, u32[]{:S(2)}) collective-permute-start(bf16[4,128,384]{2,1,0:T(8,128)(2,1)} %pack.3), channel_id=1, source_target_pairs={{0,8},{8,0},{16,24},{24,16},{1,9},{9,1},{17,25},{25,17},{2,10},{10... | collective-permute-start | bytes 1179656 | tf_op jit(solution)/shard_map/ppermute | solution.py:35
  95.5 47.8 %collective-permute-start.18 = (bf16[384,384]{1,0:T(8,128)(2,1)}, bf16[384,384]{1,0:T(8,128)(2,1)S(1)}, u32[]{:S(2)}, u32[]{:S(2)}) collective-permute-start(bf16[384,384]{1,0:T(8,128)(2,1)} %get-tuple-element.222), channel_id=1, source_target_pairs={{0,0},{4,8},{8,4},{12,12},{16,16},{20,24},{24,20},{28,28},{1,1},{5... | collective-permute-start | bytes 884744 | tf_op jit(solution)/shard_map/ppermute | solution.py:48
  97.4 45.9 %collective-permute-start.19 = (bf16[384,384]{1,0:T(8,128)(2,1)S(1)}, bf16[384,384]{1,0:T(8,128)(2,1)S(1)}, u32[]{:S(2)}, u32[]{:S(2)}) collective-permute-start(bf16[384,384]{1,0:T(8,128)(2,1)S(1)} %get-tuple-element.221), channel_id=1, source_target_pairs={{0,8},{4,0},{8,12},{12,4},{16,24},{20,16},{24,28},{28,20},{1,9},{5... | collective-permute-start | bytes 884744 | tf_op jit(solution)/shard_map/ppermute | solution.py:48
  142.5 3.8 collective-permute-start.17
  146.3 23.0 %collective-permute-start.20 = (bf16[4,128,384]{2,1,0:T(8,128)(2,1)}, bf16[4,128,384]{2,1,0:T(8,128)(2,1)S(1)}, u32[]{:S(2)}, u32[]{:S(2)}) collective-permute-start(bf16[4,128,384]{2,1,0:T(8,128)(2,1)} %pack.5), channel_id=1, source_target_pairs={{0,8},{8,0},{16,24},{24,16},{1,9},{9,1},{17,25},{25,17},{2,10},{10... | collective-permute-start | bytes 1179656 | tf_op jit(solution)/shard_map/ppermute | solution.py:35
  162.7 22.9 %all-to-all-start.2 = ((bf16[4,128,384]{2,1,0:T(8,128)(2,1)}), bf16[4,128,384]{2,1,0:T(8,128)(2,1)S(1)}, u32[]{:S(2)}, u32[]{:S(2)}) async-start(bf16[4,128,384]{2,1,0:T(8,128)(2,1)} %get-tuple-element.122), calls=%async_computation.2 | async-start | bytes 786432 | tf_op jit(solution)/shard_map/all_to_all | solution.py:68
  185.5 9.5 %all-to-all-start.3 = ((bf16[4,64,384]{2,1,0:T(8,128)(2,1)}), bf16[4,64,384]{2,1,0:T(8,128)(2,1)S(1)}, u32[]{:S(2)}, u32[]{:S(2)}) async-start(bf16[4,64,384]{2,1,0:T(8,128)(2,1)} %get-tuple-element.124), calls=%async_computation.3 | async-start | bytes 393216 | tf_op jit(solution)/shard_map/all_to_all | solution.py:68
  218.6 19.9 %all-to-all-start.4 = ((bf16[4,64,384]{2,1,0:T(8,128)(2,1)}), bf16[4,64,384]{2,1,0:T(8,128)(2,1)S(1)}, u32[]{:S(2)}, u32[]{:S(2)}) async-start(bf16[4,64,384]{2,1,0:T(8,128)(2,1)} %get-tuple-element.137), calls=%async_computation.4 | async-start | bytes 393216 | tf_op jit(solution)/shard_map/all_to_all | solution.py:68
  223.2 207.7 %reduce-scatter.2.cloned.1.call-start = ((), (), s32[]{:S(2)}) async-start(), calls=%async_computation.11 | async-start | bytes 11354112 | tf_op jit(solution)/shard_map/reduce_scatter | solution.py:844
  240.2 25.5 %all-to-all-start.5 = ((bf16[4,128,384]{2,1,0:T(8,128)(2,1)}), bf16[4,128,384]{2,1,0:T(8,128)(2,1)S(1)}, u32[]{:S(2)}, u32[]{:S(2)}) async-start(bf16[4,128,384]{2,1,0:T(8,128)(2,1)} %get-tuple-element.141), calls=%async_computation.5 | async-start | bytes 786432 | tf_op jit(solution)/shard_map/all_to_all | solution.py:68
  244.8 19.9 %collective-permute-start.21 = (bf16[384,384]{1,0:T(8,128)(2,1)S(1)}, bf16[384,384]{1,0:T(8,128)(2,1)S(1)}, u32[]{:S(2)}, u32[]{:S(2)}) collective-permute-start(bf16[384,384]{1,0:T(8,128)(2,1)S(1)} %get-tuple-element.217), channel_id=1, source_target_pairs={{0,0},{8,4},{4,8},{12,12},{16,16},{24,20},{20,24},{28,28},{1,1},{9... | collective-permute-start | bytes 884744 | tf_op jit(solution)/shard_map/ppermute | solution.py:53
  246.7 18.0 %collective-permute-start.22 = (bf16[384,384]{1,0:T(8,128)(2,1)S(1)}, bf16[384,384]{1,0:T(8,128)(2,1)S(1)}, u32[]{:S(2)}, u32[]{:S(2)}) collective-permute-start(bf16[384,384]{1,0:T(8,128)(2,1)S(1)} %get-tuple-element.218), channel_id=1, source_target_pairs={{8,0},{0,4},{12,8},{4,12},{24,16},{16,20},{28,24},{20,28},{9,1},{1... | collective-permute-start | bytes 884744 | tf_op jit(solution)/shard_map/ppermute | solution.py:53
  264.2 19.7 %collective-permute-start.23 = (bf16[4,128,384]{2,1,0:T(8,128)(2,1)}, bf16[4,128,384]{2,1,0:T(8,128)(2,1)S(1)}, u32[]{:S(2)}, u32[]{:S(2)}) collective-permute-start(bf16[4,128,384]{2,1,0:T(8,128)(2,1)} %get-tuple-element.139), channel_id=1, source_target_pairs={{0,8},{8,0},{16,24},{24,16},{1,9},{9,1},{17,25},{25,17},{2,10},{10... | collective-permute-start | bytes 1179656 | tf_op jit(solution)/shard_map/ppermute | solution.py:35
  283.9 24.9 %collective-permute-start.24 = (bf16[4,128,384]{2,1,0:T(8,128)(2,1)}, bf16[4,128,384]{2,1,0:T(8,128)(2,1)S(1)}, u32[]{:S(2)}, u32[]{:S(2)}) collective-permute-start(bf16[4,128,384]{2,1,0:T(8,128)(2,1)} %get-tuple-element.143), channel_id=1, source_target_pairs={{0,8},{8,0},{16,24},{24,16},{1,9},{9,1},{17,25},{25,17},{2,10},{10... | collective-permute-start | bytes 1179656 | tf_op jit(solution)/shard_map/ppermute | solution.py:35
  286.9 31.9 %all-to-all-start.7 = ((bf16[4,192,384]{2,1,0:T(8,128)(2,1)}), bf16[4,192,384]{2,1,0:T(8,128)(2,1)S(1)}, u32[]{:S(2)}, u32[]{:S(2)}) async-start(bf16[4,192,384]{2,1,0:T(8,128)(2,1)} %merge.3), calls=%async_computation.7 | async-start | bytes 1179648 | tf_op jit(solution)/shard_map/all_to_all | solution.py:68
  309.6 14.7 %copy-start.46 = (bf16[4,128,384]{2,1,0:T(8,128)(2,1)S(1)}, bf16[4,128,384]{2,1,0:T(8,128)(2,1)}, u32[]{:S(2)}) copy-start(bf16[4,128,384]{2,1,0:T(8,128)(2,1)} %get-tuple-element.149) | copy-start | bytes 1179652
  318.8 12.7 %copy-start.14 = (bf16[4,192,384]{2,1,0:T(8,128)(2,1)}, bf16[4,192,384]{2,1,0:T(8,128)(2,1)S(1)}, u32[]{:S(2)}) copy-start(bf16[4,192,384]{2,1,0:T(8,128)(2,1)S(1)} %all-to-all-done.7.refs_1_) | copy-start | bytes 1769476
  318.8 27.8 %all-to-all-start.6 = ((bf16[4,192,384]{2,1,0:T(8,128)(2,1)}), bf16[4,192,384]{2,1,0:T(8,128)(2,1)S(1)}, u32[]{:S(2)}, u32[]{:S(2)}) async-start(bf16[4,192,384]{2,1,0:T(8,128)(2,1)} %merge.4), calls=%async_computation.6 | async-start | bytes 1179648 | tf_op jit(solution)/shard_map/all_to_all | solution.py:68
  324.3 4.1 collective-permute-start.25
  353.4 8.0 %collective-permute-start.26 = (bf16[2,4,192,384]{3,2,1,0:T(8,128)(2,1)}, bf16[2,4,192,384]{3,2,1,0:T(8,128)(2,1)S(1)}, u32[]{:S(2)}, u32[]{:S(2)}) collective-permute-start(bf16[2,4,192,384]{3,2,1,0:T(8,128)(2,1)} %get-tuple-element.159), channel_id=1, source_target_pairs={{0,8},{8,0},{16,24},{24,16},{1,9},{9,1},{17,25},{25,17},{2,10},{10... | collective-permute-start | bytes 3538952 | tf_op jit(solution)/shard_map/ppermute | solution.py:35
  354.3 27.6 %all-to-all-start.8 = ((bf16[4,192,384]{2,1,0:T(8,128)(2,1)}), bf16[4,192,384]{2,1,0:T(8,128)(2,1)}, u32[]{:S(2)}, u32[]{:S(2)}) async-start(bf16[4,192,384]{2,1,0:T(8,128)(2,1)} %merge.5), calls=%async_computation.8 | async-start | bytes 1179648 | tf_op jit(solution)/shard_map/all_to_all | solution.py:68
  361.6 19.6 %collective-permute-start.27 = (bf16[4,192,384]{2,1,0:T(8,128)(2,1)S(1)}, bf16[4,192,384]{2,1,0:T(8,128)(2,1)S(1)}, u32[]{:S(2)}, u32[]{:S(2)}) collective-permute-start(bf16[4,192,384]{2,1,0:T(8,128)(2,1)S(1)} %get-tuple-element.202), channel_id=1, source_target_pairs={{0,4},{4,0},{1,5},{5,1},{2,6},{6,2},{3,7},{7,3},{8,12},{12,8},{9,1... | collective-permute-start | bytes 1769480 | tf_op jit(solution)/shard_map/ppermute | solution.py:31
  388.1 10.3 %collective-permute-start.30 = (bf16[2,4,96,384]{3,2,1,0:T(8,128)(2,1)S(1)}, bf16[2,4,96,384]{3,2,1,0:T(8,128)(2,1)S(1)}, u32[]{:S(2)}, u32[]{:S(2)}) collective-permute-start(bf16[2,4,96,384]{3,2,1,0:T(8,128)(2,1)S(1)} %copy-done.42), channel_id=1, source_target_pairs={{0,8},{8,0},{16,24},{24,16},{1,9},{9,1},{17,25},{25,17},{2,10},{10... | collective-permute-start | bytes 1769480 | tf_op jit(solution)/shard_map/ppermute | solution.py:35
  391.1 13.4 %collective-permute-start.33 = (bf16[192,384]{1,0:T(8,128)(2,1)S(1)}, bf16[192,384]{1,0:T(8,128)(2,1)S(1)}, u32[]{:S(2)}, u32[]{:S(2)}) collective-permute-start(bf16[192,384]{1,0:T(8,128)(2,1)S(1)} %get-tuple-element.214), channel_id=1, source_target_pairs={{0,1},{1,2},{2,3},{3,0},{4,5},{5,6},{6,7},{7,4},{8,9},{9,10},{10,1... | collective-permute-start | bytes 442376 | tf_op jit(solution)/shard_map/ppermute | solution.py:64
  392.9 17.2 %collective-permute-start.34 = (bf16[192,384]{1,0:T(8,128)(2,1)S(1)}, bf16[192,384]{1,0:T(8,128)(2,1)S(1)}, u32[]{:S(2)}, u32[]{:S(2)}) collective-permute-start(bf16[192,384]{1,0:T(8,128)(2,1)S(1)} %get-tuple-element.213), channel_id=1, source_target_pairs={{0,2},{1,3},{2,0},{3,1},{4,6},{5,7},{6,4},{7,5},{8,10},{9,11},{10,... | collective-permute-start | bytes 442376 | tf_op jit(solution)/shard_map/ppermute | solution.py:64
  397.8 19.3 %collective-permute-start.35 = (bf16[192,384]{1,0:T(8,128)(2,1)S(1)}, bf16[192,384]{1,0:T(8,128)(2,1)S(1)}, u32[]{:S(2)}, u32[]{:S(2)}) collective-permute-start(bf16[192,384]{1,0:T(8,128)(2,1)S(1)} %get-tuple-element.212), channel_id=1, source_target_pairs={{0,3},{1,0},{2,1},{3,2},{4,7},{5,4},{6,5},{7,6},{8,11},{9,8},{10,9... | collective-permute-start | bytes 442376 | tf_op jit(solution)/shard_map/ppermute | solution.py:64
  399.1 18.2 %collective-permute-start.36 = (bf16[4,96,384]{2,1,0:T(8,128)(2,1)S(1)}, bf16[4,96,384]{2,1,0:T(8,128)(2,1)S(1)}, u32[]{:S(2)}, u32[]{:S(2)}) collective-permute-start(bf16[4,96,384]{2,1,0:T(8,128)(2,1)S(1)} %get-tuple-element.203), channel_id=1, source_target_pairs={{0,4},{4,0},{1,5},{5,1},{2,6},{6,2},{3,7},{7,3},{8,12},{12,8},{9,1... | collective-permute-start | bytes 884744 | tf_op jit(solution)/shard_map/ppermute | solution.py:31
  399.9 1.7 collective-permute-start.31
  401.6 20.6 %collective-permute-start.28 = (f32[384,384]{1,0:T(8,128)S(1)}, f32[384,384]{1,0:T(8,128)S(1)}, u32[]{:S(2)}, u32[]{:S(2)}) collective-permute-start(f32[384,384]{1,0:T(8,128)S(1)} %get-tuple-element.207), channel_id=1, source_target_pairs={{0,0},{8,4},{4,8},{12,12},{16,16},{24,20},{20,24},{28,28},{1,1},{9... | collective-permute-start | bytes 1769480 | tf_op jit(solution)/shard_map/ppermute | solution.py:53
  404.5 17.7 %collective-permute-start.29 = (f32[384,384]{1,0:T(8,128)S(1)}, f32[384,384]{1,0:T(8,128)S(1)}, u32[]{:S(2)}, u32[]{:S(2)}) collective-permute-start(f32[384,384]{1,0:T(8,128)S(1)} %get-tuple-element.208), channel_id=1, source_target_pairs={{8,0},{0,4},{12,8},{4,12},{24,16},{16,20},{28,24},{20,28},{9,1},{1... | collective-permute-start | bytes 1769480 | tf_op jit(solution)/shard_map/ppermute | solution.py:53
  410.1 7.1 %collective-permute-start.32 = (f32[7,768]{1,0:T(8,128)S(1)}, f32[7,768]{1,0:T(8,128)S(1)}, u32[]{:S(2)}, u32[]{:S(2)}) collective-permute-start(f32[7,768]{1,0:T(8,128)S(1)} %add.265), channel_id=1, source_target_pairs={{0,1},{1,0},{2,3},{3,2},{4,5},{5,4},{6,7},{7,6},{8,9},{9,8},{10,11... | collective-permute-start | bytes 64520 | tf_op jit(solution)/shard_map/ppermute | solution.py:59
  418.1 3.6 collective-permute-start.37
  421.9 2.7 collective-permute-start.38
  424.7 6.2 %collective-permute-start.39 = (f32[2,10,384]{2,1,0:T(8,128)S(1)}, f32[2,10,384]{2,1,0:T(8,128)S(1)}, u32[]{:S(2)}, u32[]{:S(2)}) collective-permute-start(f32[2,10,384]{2,1,0:T(8,128)S(1)} %pad_maximum_fusion.14), channel_id=1, source_target_pairs={{0,16},{8,24},{16,0},{24,8},{1,17},{9,25},{17,1},{25,9},{2,18},{10... | collective-permute-start | bytes 92168 | tf_op jit(solution)/shard_map/ppermute | solution.py:35
  427.2 16.6 %all-to-all-start.9 = ((bf16[4,96,384]{2,1,0:T(8,128)(2,1)}), bf16[4,96,384]{2,1,0:T(8,128)(2,1)S(1)}, u32[]{:S(2)}, u32[]{:S(2)}) async-start(bf16[4,96,384]{2,1,0:T(8,128)(2,1)} %add_convert_fusion.3), calls=%async_computation.9 | async-start | bytes 589824 | tf_op jit(solution)/shard_map/all_to_all | solution.py:68
  430.7 28.1 %all-gather.4.cloned.1.call-start = ((), (), s32[]{:S(2)}) async-start(), calls=%async_computation.12 | async-start | bytes 1720320 | tf_op jit(solution)/shard_map/all_gather | solution.py:933
  430.7 5.6 %collective-permute-start.42 = (f32[192,384]{1,0:T(8,128)S(1)}, f32[192,384]{1,0:T(8,128)S(1)}, u32[]{:S(2)}, u32[]{:S(2)}) collective-permute-start(f32[192,384]{1,0:T(8,128)S(1)} %convert_reduce_fusion.1), channel_id=1, source_target_pairs={{0,16},{8,24},{16,0},{24,8},{1,17},{9,25},{17,1},{25,9},{2,18},{10... | collective-permute-start | bytes 884744 | tf_op jit(solution)/shard_map/ppermute | solution.py:35
  436.4 15.5 %collective-permute-start.43 = (f32[192,384]{1,0:T(8,128)S(1)}, f32[192,384]{1,0:T(8,128)S(1)}, u32[]{:S(2)}, u32[]{:S(2)}) collective-permute-start(f32[192,384]{1,0:T(8,128)S(1)} %add.281), channel_id=1, source_target_pairs={{0,8},{8,0},{16,24},{24,16},{1,9},{9,1},{17,25},{25,17},{2,10},{10... | collective-permute-start | bytes 884744 | tf_op jit(solution)/shard_map/ppermute | solution.py:35
  443.9 6.2 %collective-permute-start.40 = (f32[96,384]{1,0:T(8,128)S(1)}, f32[96,384]{1,0:T(8,128)S(1)}, u32[]{:S(2)}, u32[]{:S(2)}) collective-permute-start(f32[96,384]{1,0:T(8,128)S(1)} %convert_reduce_fusion.2), channel_id=1, source_target_pairs={{0,16},{8,24},{16,0},{24,8},{1,17},{9,25},{17,1},{25,9},{2,18},{10... | collective-permute-start | bytes 442376 | tf_op jit(solution)/shard_map/ppermute | solution.py:35
  450.1 2.8 collective-permute-start.41
  (42 other events, 191.1 us)
Sparse Core Ops, SparseCore 0:
  18.3 120.1 all-gather.5
  238.7 179.6 reduce-scatter.1
  433.1 25.6 all-gather.3
